TPU v7x, 32 devices: a whole 2x2x4 slice. The times are simulated.
32 devices in a mesh: node: 8 (over z, core), edge: 4 (over y, x).
Axes of the slice: x: 2, y: 2, z: 4, core: 2. Of those that a mesh axis runs over, the one named last changes fastest.
Arguments:
- node_feats: bfloat16 [4096, 512], P(('node', 'edge')), may hold values from -40 to 40
- members: int32 [8, 4, 3072], P('node', None, 'edge'), may hold values from 0 to 511, as said below
- incidence_mask: int32 [8, 4, 3072], P('node', None, 'edge'), may hold values from 0 to 1
- degrees: int32 [3072], P(('edge', 'node')), may hold values from 0 to 32, as said below
- w_query: bfloat16 [512, 512], replicated, may hold values from -1 to 1
- w_key: bfloat16 [512, 512], replicated, may hold values from -1 to 1
- w_value: bfloat16 [512, 512], replicated, may hold values from -0.25 to 0.25
- w_out: bfloat16 [512, 512], replicated, may hold values from -0.5 to 0.5
Outputs:
- mixed: bfloat16 [3072, 512], P(('edge', 'node'))
Inputs may be any that keep to these rules, and one draw needn't show every extreme that they name: `members`: node index within the partition; only slots whose incidence_mask is 1 count. degrees[h] is the number of slots of hyperedge h over all partitions whose incidence_mask is 1; some hyperedge has every slot of every partition filled, and some hyperedge has none.
All inputs are finite; a program needn't handle non-finite values.
Results may differ from a plain program's by a relative error of at most 0.012.
Values may be sent and summed in bfloat16 or wider, within the bound.
No kernel may reach another device: no remote copies, remote signals or barrier semaphores. Data moves between devices by JAX's collectives and lax.ppermute only.
A program may use at most 64 MiB of HBM per device.

v0:
```python
import functools

import jax
import jax.numpy as jnp
from jax import lax
from jax.experimental import pallas as pl
from jax.experimental.pallas import tpu as pltpu
from jax.sharding import PartitionSpec as P


VMEM_LIMIT = 16 * 2**20
CORES = 2


def to_peer(index, step, count):
    if count & (count - 1) == 0:
        return index ^ step
    return (index + step) % count


def from_peer(index, step, count):
    if count & (count - 1) == 0:
        return index ^ step
    return (index + count - step) % count


def swap_cores(value):
    count = lax.axis_size("node")
    return lax.ppermute(value, "node", [(i, i ^ 1) for i in range(count)])


def send_edge(value, step):
    count = lax.axis_size("edge")
    return lax.ppermute(value, "edge", [(i, to_peer(i, step, count)) for i in range(count)])


def send_chip(value, step):
    chips = lax.axis_size("node") // CORES
    return lax.ppermute(
        value,
        "node",
        [(i, to_peer(i // CORES, step, chips) * CORES + i % CORES) for i in range(chips * CORES)],
    )


def vmem_call(kernel, outs, scratch=()):
    def call(*args):
        spec = pl.BlockSpec(memory_space=pltpu.VMEM)
        return pl.pallas_call(
            kernel,
            out_shape=[pltpu.VMEM(shape, dtype) for shape, dtype in outs],
            in_specs=[spec] * len(args),
            out_specs=[spec] * len(outs),
            scratch_shapes=list(scratch),
            compiler_params=pltpu.CompilerParams(vmem_limit_bytes=VMEM_LIMIT),
        )(*[pltpu.with_memory_space_constraint(a, pltpu.VMEM) for a in args])

    return call


def preload_kernel(feats, members, valid, degrees, *refs):
    weights = (len(refs) - 6) // 2
    sources, feats_here, code = refs[:weights], refs[weights], refs[weights + 1]
    copies, (members_here, valid_here, degrees_here, sems) = refs[weights + 2 : -4], refs[-4:]
    moves = [
        pltpu.make_async_copy(source, target, sems.at[i])
        for i, (source, target) in enumerate(
            zip(
                (members, valid, degrees, feats) + tuple(sources),
                (members_here, valid_here, degrees_here, feats_here) + tuple(copies),
            )
        )
    ]
    for move in moves:
        move.start()
    for move in moves[:3]:
        move.wait()
    slots, owned = members.shape[0], degrees.shape[1]
    code[:slots, :] = jnp.where(valid_here[...] == 1, members_here[...], -1)
    code[slots : slots + 1, :owned] = degrees_here[...]
    for move in moves[3:]:
        move.wait()


def preload(feats, members, valid, degrees, *weights):
    args = (feats, members, valid, degrees) + weights
    outside = pl.BlockSpec(memory_space=pltpu.HBM)
    spec = pl.BlockSpec(memory_space=pltpu.VMEM)
    kept = [feats.shape, (2 * members.shape[0], members.shape[1])] + [w.shape for w in weights]
    kinds = [feats.dtype, members.dtype] + [w.dtype for w in weights]
    return pl.pallas_call(
        preload_kernel,
        out_shape=[pltpu.VMEM(shape, kind) for shape, kind in zip(kept, kinds)],
        in_specs=[outside] * len(args),
        out_specs=[spec] * len(kept),
        scratch_shapes=[
            pltpu.VMEM(members.shape, members.dtype),
            pltpu.VMEM(valid.shape, valid.dtype),
            pltpu.VMEM(degrees.shape, degrees.dtype),
            pltpu.SemaphoreType.DMA((len(args),)),
        ],
        compiler_params=pltpu.CompilerParams(vmem_limit_bytes=VMEM_LIMIT),
        name="preload",
    )(*[pltpu.with_memory_space_constraint(a, pltpu.HBM) for a in args])


def feature_map(values):
    return jnp.where(values > 0, values + 1.0, jnp.exp(jnp.minimum(values, 0.0)))


def half_place(half):
    core = lax.axis_index("node") % CORES
    mine = pl.ds(pl.multiple_of(core * half, half), half)
    other = pl.ds(pl.multiple_of((1 - core) * half, half), half)
    return mine, other


def pack_kernel(own, other, out):
    part, width = own.shape
    columns, _ = half_place(width // CORES)
    mine, theirs = half_place(part)
    out[mine, :] = own[:, columns]
    out[theirs, :] = other[:, columns]


def counts_kernel(chips, edges, owned, part, slots, code, code_other, counts, scale, columns):
    core = lax.axis_index("node") % CORES
    chip = lax.axis_index("node") // CORES
    edge = lax.axis_index("edge")
    first = jnp.where(core == 0, code[...], code_other[...])
    second = jnp.where(core == 0, code_other[...], code[...])
    columns[...] = jnp.concatenate([first, second], axis=0).T
    for side in range(CORES):
        place = side * 2 * slots + slots
        degree = jnp.maximum(columns[:owned, place : place + 1], 1).astype(jnp.float32)
        scale[side * owned : (side + 1) * owned, :] = jnp.broadcast_to(degree, (owned, scale.shape[1]))
    lanes = lax.broadcasted_iota(jnp.int32, (owned, part), 1)

    def chunk(step, turn):
        source = (to_peer(chip, step, chips) * CORES + turn) * owned
        rows = columns[pl.ds(pl.multiple_of(source, 8), owned), :]
        target = (step * CORES + turn) * owned
        if not isinstance(target, int):
            target = pl.multiple_of(target, 8)
        for side in range(CORES):
            base = side * 2 * slots
            wanted = [rows[:, base + s : base + s + 1] for s in range(slots)]
            for block in range(edges):
                nodes = lanes + from_peer(edge, block, edges) * part
                total = jnp.zeros((owned, part), jnp.float32)
                for column in wanted:
                    total = total + jnp.where(column == nodes, 1.0, 0.0)
                place = (block * CORES + side) * part
                counts[pl.ds(target, owned), place : place + part] = total.astype(jnp.bfloat16)

    if chips <= 4:
        for step in range(chips):
            for turn in range(CORES):
                chunk(step, turn)
    else:
        lax.fori_loop(0, chips * CORES, lambda i, _: chunk(i // CORES, i % CORES), None)


def aggregate_kernel(chips, edges, counts, *refs):
    blocks, outs = refs[:edges], refs[edges:]
    nodes = blocks[0].shape[0]
    rows = outs[0].shape[0]
    group = min(chips, 4)
    for start in range(0, chips, group):
        total = None
        for block in range(edges):
            term = jnp.dot(
                counts[start * rows : (start + group) * rows, block * nodes : (block + 1) * nodes],
                blocks[block][...],
                preferred_element_type=jnp.float32,
            )
            total = term if total is None else total + term
        for step in range(group):
            out = outs[start + step]
            out[...] = total[step * rows : (step + 1) * rows].astype(out.dtype)


def hedge_kernel(scale, own, *refs):
    received, out = refs[:-1], refs[-1]
    total = own[...]
    for ref in received:
        total = total + ref[...].astype(jnp.float32)
    out[...] = (total / scale[:, :1]).astype(out.dtype)


def gram_kernel(edges, hedge, hedge_other, w_key, w_value, *refs):
    outs, full, gram = refs[:edges], refs[edges], refs[edges + 1]
    edge = lax.axis_index("edge")
    width = w_key.shape[0]
    half = width // CORES
    rows = width // edges
    mine, other = half_place(half)
    full[:, mine] = hedge[...]
    full[:, other] = hedge_other[...]
    both = full[...]
    keys = feature_map(jnp.dot(both, w_key[...], preferred_element_type=jnp.float32)).astype(jnp.bfloat16)
    values = jnp.dot(both, w_value[:, mine], preferred_element_type=jnp.float32).astype(jnp.bfloat16)
    gram[...] = lax.dot_general(
        keys, values, (((0,), (0,)), ((), ())), preferred_element_type=jnp.float32
    )
    key_sum = jnp.sum(keys.astype(jnp.float32), axis=0, keepdims=True)
    tail = [key_sum[:, i * half : (i + 1) * half] for i in range(CORES)]
    tail = jnp.concatenate(tail + [jnp.zeros((8 - CORES, half), jnp.float32)], axis=0)
    for step in range(edges):
        first = pl.multiple_of(to_peer(edge, step, edges) * rows, rows)
        outs[step][:rows, :] = gram[pl.ds(first, rows), :].astype(outs[step].dtype)
        outs[step][rows:, :] = tail.astype(outs[step].dtype)


def query_kernel(full, w_query, out):
    out[...] = feature_map(
        jnp.dot(full[...], w_query[...], preferred_element_type=jnp.float32)
    ).astype(out.dtype)


def add_kernel(own, *refs, count):
    received, outs = refs[:count], refs[count:]
    total = own[...]
    for ref in received:
        total = total + ref[...].astype(jnp.float32)
    for out in outs:
        out[...] = total[: out.shape[0]].astype(out.dtype)


def denom_kernel(query, whole, out):
    half = whole.shape[1]
    tail = whole[whole.shape[0] - 8 :, :].astype(jnp.float32)
    denom = None
    for side in range(CORES):
        part = query[:, side * half : (side + 1) * half].astype(jnp.float32) * tail[side : side + 1, :]
        part = jnp.sum(part, axis=1, keepdims=True)
        denom = part if denom is None else denom + part
    out[...] = jnp.broadcast_to(denom, out.shape)


def attend_kernel(edges, query, denom, *refs):
    pieces, (mine, other, gram, attended) = refs[:edges], refs[edges:]
    edge = lax.axis_index("edge")
    rows = query.shape[1] // edges
    for step in range(edges):
        first = pl.multiple_of(from_peer(edge, step, edges) * rows, rows)
        gram[pl.ds(first, rows), :] = pieces[step][:rows, :]
    numer = jnp.dot(query[...], gram[...], preferred_element_type=jnp.float32)
    attended[...] = (numer / denom[:, :1]).astype(attended.dtype)
    here, there = half_place(mine.shape[0])
    mine[...] = attended[here, :]
    other[...] = attended[there, :]


def base_kernel(full, mine, w_out, out):
    here, _ = half_place(mine.shape[0])
    rows, _ = half_place(mine.shape[1])
    out[...] = full[here, :].astype(jnp.float32) + jnp.dot(
        mine[...], w_out[rows, :], preferred_element_type=jnp.float32
    )


def output_kernel(base, other, w_out, out, result, sems):
    _, rows = half_place(other.shape[1])
    half = other.shape[1]
    moves = []
    for side in range(CORES):
        place = pl.ds(side * half, half)
        mixed = base[:, place] + jnp.dot(
            other[...], w_out[rows, place], preferred_element_type=jnp.float32
        )
        result[:, place] = mixed.astype(result.dtype)
        moves.append(pltpu.make_async_copy(result.at[:, place], out.at[:, place], sems.at[side]))
        moves[-1].start()
    for move in moves:
        move.wait()


def write_output(base, other, w_out):
    args = (base, other, w_out)
    spec = pl.BlockSpec(memory_space=pltpu.VMEM)
    return pl.pallas_call(
        output_kernel,
        out_shape=pltpu.HBM(base.shape, other.dtype),
        in_specs=[spec] * len(args),
        out_specs=pl.BlockSpec(memory_space=pltpu.HBM),
        scratch_shapes=[
            pltpu.VMEM(base.shape, other.dtype),
            pltpu.SemaphoreType.DMA((CORES,)),
        ],
        compiler_params=pltpu.CompilerParams(vmem_limit_bytes=VMEM_LIMIT),
        name="output",
    )(*[pltpu.with_memory_space_constraint(a, pltpu.VMEM) for a in args])


def body(node_feats, members, incidence_mask, degrees, w_query, w_key, w_value, w_out):
    bf16, f32 = jnp.bfloat16, jnp.float32
    chips = lax.axis_size("node") // CORES
    edges = lax.axis_size("edge")
    part, width = node_feats.shape
    half = width // CORES
    owned = degrees.shape[0]
    pair = owned * CORES
    slots, shard = members.shape[1:]
    rows = width // edges
    piece = rows + 8

    feats_other = swap_cores(node_feats)
    feats, code, w_query, w_key, w_value, w_out = preload(
        node_feats, members[0], incidence_mask[0], degrees[None], w_query, w_key, w_value, w_out
    )
    (packed,) = vmem_call(pack_kernel, [((part * CORES, half), bf16)])(feats, feats_other)
    blocks = [packed] + [send_edge(packed, step) for step in range(1, edges)]
    code_other = swap_cores(code)
    counts, scale = vmem_call(
        functools.partial(counts_kernel, chips, edges, owned, part, slots),
        [((shard, CORES * edges * part), bf16), ((pair, 128), f32)],
        [pltpu.VMEM((shard, CORES * 2 * slots), jnp.int32)],
    )(code, code_other)
    partial = vmem_call(
        functools.partial(aggregate_kernel, chips, edges),
        [((pair, half), f32)] + [((pair, half), bf16)] * (chips - 1),
    )(counts, *blocks)
    arrived = [send_chip(partial[step], step) for step in range(1, chips)]
    (hedge,) = vmem_call(hedge_kernel, [((pair, half), bf16)])(scale, partial[0], *arrived)

    hedge_other = swap_cores(hedge)
    *grams, full = vmem_call(
        functools.partial(gram_kernel, edges),
        [((piece, half), f32)] + [((piece, half), bf16)] * (edges - 1) + [((pair, width), bf16)],
        [pltpu.VMEM((width, half), f32)],
    )(hedge, hedge_other, w_key, w_value)
    arrived = [send_edge(grams[step], step) for step in range(1, edges)]
    (query,) = vmem_call(query_kernel, [((pair, width), bf16)])(full, w_query)
    plane, plane16 = vmem_call(
        functools.partial(add_kernel, count=edges - 1),
        [((piece, half), f32), ((piece, half), bf16)],
    )(grams[0], *arrived)
    arrived = [send_chip(plane16, step) for step in range(1, chips)]
    whole, strip = vmem_call(
        functools.partial(add_kernel, count=chips - 1),
        [((piece, half), bf16), ((rows, half), bf16)],
    )(plane, *arrived)
    pieces = [whole] + [send_edge(strip, step) for step in range(1, edges)]
    (denom,) = vmem_call(denom_kernel, [((pair, 128), f32)])(query, whole)
    mine, other = vmem_call(
        functools.partial(attend_kernel, edges),
        [((owned, half), bf16)] * CORES,
        [pltpu.VMEM((width, half), bf16), pltpu.VMEM((pair, half), bf16)],
    )(query, denom, *pieces)
    arrived = swap_cores(other)
    (base,) = vmem_call(base_kernel, [((owned, width), f32)])(full, mine, w_out)
    return write_output(base, arrived, w_out)


def solution(mesh):
    placed = (
        P(("node", "edge"), None),
        P("node", None, "edge"),
        P("node", None, "edge"),
        P(("edge", "node")),
        P(),
        P(),
        P(),
        P(),
    )
    return jax.shard_map(
        body, mesh=mesh, in_specs=placed, out_specs=P(("edge", "node"), None), check_vma=False
    )
```

profile of v0, /device:TPU:0, one launch (start us, length us, event | category | flops | bytes accessed | tf_op | source)
XLA Modules:
  0.0 53.7 jit_solution(982332061796026862)
XLA Ops:
  0.0 0.5 collective-permute-start.1
  0.5 1.7 %preload.1 = (bf16[128,512]{1,0:T(8,128)(2,1)S(1)}, s32[8,768]{1,0:T(8,128)S(1)}, bf16[512,512]{1,0:T(8,128)(2,1)S(1)}, bf16[512,512]{1,0:T(8,128)(2,1)S(1)}, bf...) custom-call(bf16[128,512]{1,0:T(8,128)(2,1)} %feats.1, s32[4,768]{1,0:T(4,128)} %bitcast.3, s32[4,768]{1,0:T(4,128)} %bitcast.4, ...), custom_call_target="tpu_custom_call" | custom-call | tf_op jit(solution)/shard_map/preload/pallas_call | solution.py:91
  2.2 0.0 collective-permute-done.1.other
  2.2 3.5 %collective-permute-start.4 = (bf16[256,256]{1,0:T(8,128)(2,1)S(1)}, bf16[256,256]{1,0:T(8,128)(2,1)S(1)}, u32[]{:S(2)}, u32[]{:S(2)}) collective-permute-start(bf16[256,256]{1,0:T(8,128)(2,1)S(1)} %shard_map.83.refs_0_), channel_id=1, source_target_pairs={{0,3},{1,2},{2,1},{3,0},{4,7},{5,6},{6,5},{7,4},{8,11},{9,10},{10,... | collective-permute-start | bytes 393224 | tf_op jit(solution)/shard_map/ppermute | solution.py:34
  5.7 0.5 collective-permute-start.3
  6.2 0.1 collective-permute-start.2
  6.4 0.0 collective-permute-start
  6.4 1.2 %collective-permute-done.code_other = s32[8,768]{1,0:T(8,128)S(1)} collective-permute-done((s32[8,768]{1,0:T(8,128)S(1)}, s32[8,768]{1,0:T(8,128)S(1)}, u32[]{:S(2)}, u32[]{:S(2)}) %collective-permute-start) | collective-permute-done | bytes 24608 | tf_op jit(solution)/shard_map/ppermute | solution.py:29
  7.6 1.5 %shard_map.82 = (bf16[768,1024]{1,0:T(8,128)(2,1)S(1)}, f32[192,128]{1,0:T(8,128)S(1)}) custom-call(s32[8,768]{1,0:T(8,128)S(1)} %get-tuple-element.28.code, s32[8,768]{1,0:T(8,128)S(1)} %collective-permute-done.code_other), custom_call_target="tpu_custom_call" | custom-call | tf_op jit(solution)/shard_map/pallas_call | solution.py:49
  9.1 0.9 %collective-permute-done.4.refs_3_ = bf16[256,256]{1,0:T(8,128)(2,1)S(1)} collective-permute-done((bf16[256,256]{1,0:T(8,128)(2,1)S(1)}, bf16[256,256]{1,0:T(8,128)(2,1)S(1)}, u32[]{:S(2)}, u32[]{:S(2)}) %collective-permute-start.4) | collective-permute-done | bytes 131104 | tf_op jit(solution)/shard_map/ppermute | solution.py:34
  10.1 2.6 %collective-permute-done.3.refs_2_ = bf16[256,256]{1,0:T(8,128)(2,1)S(1)} collective-permute-done((bf16[256,256]{1,0:T(8,128)(2,1)S(1)}, bf16[256,256]{1,0:T(8,128)(2,1)S(1)}, u32[]{:S(2)}, u32[]{:S(2)}) %collective-permute-start.3) | collective-permute-done | bytes 131104 | tf_op jit(solution)/shard_map/ppermute | solution.py:34
  12.7 0.3 collective-permute-done.2.refs_1_
  13.0 0.6 %shard_map.84 = (f32[192,256]{1,0:T(8,128)S(1)}, bf16[192,256]{1,0:T(8,128)(2,1)S(1)}, bf16[192,256]{1,0:T(8,128)(2,1)S(1)}, bf16[192,256]{1,0:T(8,128)(2,1)S(1)}) custom-call(bf16[768,1024]{1,0:T(8,128)(2,1)S(1)} %get-tuple-element.30.counts, bf16[256,256]{1,0:T(8,128)(2,1)S(1)} %shard_map.83.refs_0_, bf16[256,256]{1,0:T(8,128)(2,1)S(1)} %collective-permute-done.2.refs_1_, ...), custom_call_target="tpu_custom_call" | custom-call | tf_op jit(solution)/shard_map/pallas_call | solution.py:49
  13.6 1.6 %collective-permute-start.5 = (bf16[192,256]{1,0:T(8,128)(2,1)S(1)}, bf16[192,256]{1,0:T(8,128)(2,1)S(1)}, u32[]{:S(2)}, u32[]{:S(2)}) collective-permute-start(bf16[192,256]{1,0:T(8,128)(2,1)S(1)} %get-tuple-element.33), channel_id=1, source_target_pairs={{0,8},{4,12},{8,0},{12,4},{16,24},{20,28},{24,16},{28,20},{1,9},{5... | collective-permute-start | bytes 294920 | tf_op jit(solution)/shard_map/ppermute | solution.py:39
  15.2 2.6 %collective-permute-start.6 = (bf16[192,256]{1,0:T(8,128)(2,1)S(1)}, bf16[192,256]{1,0:T(8,128)(2,1)S(1)}, u32[]{:S(2)}, u32[]{:S(2)}) collective-permute-start(bf16[192,256]{1,0:T(8,128)(2,1)S(1)} %get-tuple-element.34), channel_id=1, source_target_pairs={{0,16},{4,20},{8,24},{12,28},{16,0},{20,4},{24,8},{28,12},{1,17},{... | collective-permute-start | bytes 294920 | tf_op jit(solution)/shard_map/ppermute | solution.py:39
  17.8 0.2 collective-permute-start.7
  18.0 0.2 collective-permute-done.5.refs_0_
  18.3 7.5 %collective-permute-done.6.refs_1_ = bf16[192,256]{1,0:T(8,128)(2,1)S(1)} collective-permute-done((bf16[192,256]{1,0:T(8,128)(2,1)S(1)}, bf16[192,256]{1,0:T(8,128)(2,1)S(1)}, u32[]{:S(2)}, u32[]{:S(2)}) %collective-permute-start.6) | collective-permute-done | bytes 98336 | tf_op jit(solution)/shard_map/ppermute | solution.py:39
  25.8 0.0 collective-permute-done.7.refs_2_
  25.8 0.1 shard_map.85.hedge
  25.9 0.1 collective-permute-start.8
  26.0 1.3 %collective-permute-done.8.hedge_other = bf16[192,256]{1,0:T(8,128)(2,1)S(1)} collective-permute-done((bf16[192,256]{1,0:T(8,128)(2,1)S(1)}, bf16[192,256]{1,0:T(8,128)(2,1)S(1)}, u32[]{:S(2)}, u32[]{:S(2)}) %collective-permute-start.8) | collective-permute-done | bytes 98336 | tf_op jit(solution)/shard_map/ppermute | solution.py:29
  27.3 0.7 %shard_map.86 = (f32[136,256]{1,0:T(8,128)S(1)}, bf16[136,256]{1,0:T(8,128)(2,1)S(1)}, bf16[136,256]{1,0:T(8,128)(2,1)S(1)}, bf16[136,256]{1,0:T(8,128)(2,1)S(1)}, bf16[192,512]{1,0:T(8,128)(2,1)S(1)}) custom-call(bf16[192,256]{1,0:T(8,128)(2,1)S(1)} %shard_map.85.hedge, bf16[192,256]{1,0:T(8,128)(2,1)S(1)} %collective-permute-done.8.hedge_other, ...), custom_call_target="tpu_custom_call" | custom-call | tf_op jit(solution)/shard_map/pallas_call | solution.py:49
  28.0 1.6 %collective-permute-start.9 = (bf16[136,256]{1,0:T(8,128)(2,1)S(1)}, bf16[136,256]{1,0:T(8,128)(2,1)S(1)}, u32[]{:S(2)}, u32[]{:S(2)}) collective-permute-start(bf16[136,256]{1,0:T(8,128)(2,1)S(1)} %get-tuple-element.41), channel_id=1, source_target_pairs={{0,1},{1,0},{2,3},{3,2},{4,5},{5,4},{6,7},{7,6},{8,9},{9,8},{10,11... | collective-permute-start | bytes 208904 | tf_op jit(solution)/shard_map/ppermute | solution.py:34
  29.5 0.2 collective-permute-start.10
  29.7 1.8 %collective-permute-start.11 = (bf16[136,256]{1,0:T(8,128)(2,1)S(1)}, bf16[136,256]{1,0:T(8,128)(2,1)S(1)}, u32[]{:S(2)}, u32[]{:S(2)}) collective-permute-start(bf16[136,256]{1,0:T(8,128)(2,1)S(1)} %get-tuple-element.43), channel_id=1, source_target_pairs={{0,3},{1,2},{2,1},{3,0},{4,7},{5,6},{6,5},{7,4},{8,11},{9,10},{10,... | collective-permute-start | bytes 208904 | tf_op jit(solution)/shard_map/ppermute | solution.py:34
  31.5 0.8 %collective-permute-done.9.refs_0_ = bf16[136,256]{1,0:T(8,128)(2,1)S(1)} collective-permute-done((bf16[136,256]{1,0:T(8,128)(2,1)S(1)}, bf16[136,256]{1,0:T(8,128)(2,1)S(1)}, u32[]{:S(2)}, u32[]{:S(2)}) %collective-permute-start.9) | collective-permute-done | bytes 69664 | tf_op jit(solution)/shard_map/ppermute | solution.py:34
  32.3 2.9 %collective-permute-done.10.refs_1_ = bf16[136,256]{1,0:T(8,128)(2,1)S(1)} collective-permute-done((bf16[136,256]{1,0:T(8,128)(2,1)S(1)}, bf16[136,256]{1,0:T(8,128)(2,1)S(1)}, u32[]{:S(2)}, u32[]{:S(2)}) %collective-permute-start.10) | collective-permute-done | bytes 69664 | tf_op jit(solution)/shard_map/ppermute | solution.py:34
  35.3 0.0 collective-permute-done.11.refs_2_
  35.3 2.6 %collective-permute-start.14 = (bf16[136,256]{1,0:T(8,128)(2,1)S(1)}, bf16[136,256]{1,0:T(8,128)(2,1)S(1)}, u32[]{:S(2)}, u32[]{:S(2)}) collective-permute-start(bf16[136,256]{1,0:T(8,128)(2,1)S(1)} %get-tuple-element.45), channel_id=1, source_target_pairs={{0,24},{4,28},{8,16},{12,20},{16,8},{20,12},{24,0},{28,4},{1,25},{... | collective-permute-start | bytes 208904 | tf_op jit(solution)/shard_map/ppermute | solution.py:39
  37.9 0.6 %collective-permute-start.13 = (bf16[136,256]{1,0:T(8,128)(2,1)S(1)}, bf16[136,256]{1,0:T(8,128)(2,1)S(1)}, u32[]{:S(2)}, u32[]{:S(2)}) collective-permute-start(bf16[136,256]{1,0:T(8,128)(2,1)S(1)} %get-tuple-element.45), channel_id=1, source_target_pairs={{0,16},{4,20},{8,24},{12,28},{16,0},{20,4},{24,8},{28,12},{1,17},{... | collective-permute-start | bytes 208904 | tf_op jit(solution)/shard_map/ppermute | solution.py:39
  38.5 1.3 %collective-permute-start.12 = (bf16[136,256]{1,0:T(8,128)(2,1)S(1)}, bf16[136,256]{1,0:T(8,128)(2,1)S(1)}, u32[]{:S(2)}, u32[]{:S(2)}) collective-permute-start(bf16[136,256]{1,0:T(8,128)(2,1)S(1)} %get-tuple-element.45), channel_id=1, source_target_pairs={{0,8},{4,12},{8,0},{12,4},{16,24},{20,28},{24,16},{28,20},{1,9},{5... | collective-permute-start | bytes 208904 | tf_op jit(solution)/shard_map/ppermute | solution.py:39
  39.8 2.3 %collective-permute-done.14.refs_2_ = bf16[136,256]{1,0:T(8,128)(2,1)S(1)} collective-permute-done((bf16[136,256]{1,0:T(8,128)(2,1)S(1)}, bf16[136,256]{1,0:T(8,128)(2,1)S(1)}, u32[]{:S(2)}, u32[]{:S(2)}) %collective-permute-start.14) | collective-permute-done | bytes 69664 | tf_op jit(solution)/shard_map/ppermute | solution.py:39
  42.0 2.2 %collective-permute-done.13.refs_1_ = bf16[136,256]{1,0:T(8,128)(2,1)S(1)} collective-permute-done((bf16[136,256]{1,0:T(8,128)(2,1)S(1)}, bf16[136,256]{1,0:T(8,128)(2,1)S(1)}, u32[]{:S(2)}, u32[]{:S(2)}) %collective-permute-start.13) | collective-permute-done | bytes 69664 | tf_op jit(solution)/shard_map/ppermute | solution.py:39
  44.2 0.0 collective-permute-done.12.refs_0_
  44.3 1.5 %collective-permute-start.17 = (bf16[128,256]{1,0:T(8,128)(2,1)S(1)}, bf16[128,256]{1,0:T(8,128)(2,1)S(1)}, u32[]{:S(2)}, u32[]{:S(2)}) collective-permute-start(bf16[128,256]{1,0:T(8,128)(2,1)S(1)} %get-tuple-element.47), channel_id=1, source_target_pairs={{0,3},{1,2},{2,1},{3,0},{4,7},{5,6},{6,5},{7,4},{8,11},{9,10},{10,... | collective-permute-start | bytes 196616 | tf_op jit(solution)/shard_map/ppermute | solution.py:34
  45.8 1.3 %collective-permute-start.16 = (bf16[128,256]{1,0:T(8,128)(2,1)S(1)}, bf16[128,256]{1,0:T(8,128)(2,1)S(1)}, u32[]{:S(2)}, u32[]{:S(2)}) collective-permute-start(bf16[128,256]{1,0:T(8,128)(2,1)S(1)} %get-tuple-element.47), channel_id=1, source_target_pairs={{0,2},{1,3},{2,0},{3,1},{4,6},{5,7},{6,4},{7,5},{8,10},{9,11},{10,... | collective-permute-start | bytes 196616 | tf_op jit(solution)/shard_map/ppermute | solution.py:34
  47.1 0.8 %collective-permute-start.15 = (bf16[128,256]{1,0:T(8,128)(2,1)S(1)}, bf16[128,256]{1,0:T(8,128)(2,1)S(1)}, u32[]{:S(2)}, u32[]{:S(2)}) collective-permute-start(bf16[128,256]{1,0:T(8,128)(2,1)S(1)} %get-tuple-element.47), channel_id=1, source_target_pairs={{0,1},{1,0},{2,3},{3,2},{4,5},{5,4},{6,7},{7,6},{8,9},{9,8},{10,11... | collective-permute-start | bytes 196616 | tf_op jit(solution)/shard_map/ppermute | solution.py:34
  47.8 0.3 shard_map.87.query
  48.1 0.1 shard_map.90.denom
  48.3 1.2 %collective-permute-done.17.refs_3_ = bf16[128,256]{1,0:T(8,128)(2,1)S(1)} collective-permute-done((bf16[128,256]{1,0:T(8,128)(2,1)S(1)}, bf16[128,256]{1,0:T(8,128)(2,1)S(1)}, u32[]{:S(2)}, u32[]{:S(2)}) %collective-permute-start.17) | collective-permute-done | bytes 65568 | tf_op jit(solution)/shard_map/ppermute | solution.py:34
  49.5 0.7 %collective-permute-done.16.refs_2_ = bf16[128,256]{1,0:T(8,128)(2,1)S(1)} collective-permute-done((bf16[128,256]{1,0:T(8,128)(2,1)S(1)}, bf16[128,256]{1,0:T(8,128)(2,1)S(1)}, u32[]{:S(2)}, u32[]{:S(2)}) %collective-permute-start.16) | collective-permute-done | bytes 65568 | tf_op jit(solution)/shard_map/ppermute | solution.py:34
  50.2 1.1 %collective-permute-done.15.refs_1_ = bf16[128,256]{1,0:T(8,128)(2,1)S(1)} collective-permute-done((bf16[128,256]{1,0:T(8,128)(2,1)S(1)}, bf16[128,256]{1,0:T(8,128)(2,1)S(1)}, u32[]{:S(2)}, u32[]{:S(2)}) %collective-permute-start.15) | collective-permute-done | bytes 65568 | tf_op jit(solution)/shard_map/ppermute | solution.py:34
  51.3 0.3 shard_map.91
  51.6 0.1 collective-permute-start.18
  51.7 0.2 shard_map.92.base
  51.9 1.0 %collective-permute-done.18.other = bf16[96,256]{1,0:T(8,128)(2,1)S(1)} collective-permute-done((bf16[96,256]{1,0:T(8,128)(2,1)S(1)}, bf16[96,256]{1,0:T(8,128)(2,1)S(1)}, u32[]{:S(2)}, u32[]{:S(2)}) %collective-permute-start.18) | collective-permute-done | bytes 49184 | tf_op jit(solution)/shard_map/ppermute | solution.py:29
  52.9 0.8 %output.1 = bf16[96,512]{1,0:T(8,128)(2,1)} custom-call(f32[96,512]{1,0:T(8,128)S(1)} %shard_map.92.base, bf16[96,256]{1,0:T(8,128)(2,1)S(1)} %collective-permute-done.18.other, bf16[512,512]{1,0:T(8,128)(2,1)S(1)} %get-tuple-element.49.w_out), custom_call_target="tpu_custom_call" | custom-call | tf_op jit(solution)/shard_map/output/pallas_call | solution.py:282
  (3 shorter events, 0.1 us)
Async XLA Ops:
  0.0 2.2 %collective-permute-start.1 = (bf16[128,512]{1,0:T(8,128)(2,1)}, bf16[128,512]{1,0:T(8,128)(2,1)S(1)}, u32[]{:S(2)}, u32[]{:S(2)}) collective-permute-start(bf16[128,512]{1,0:T(8,128)(2,1)} %feats.1), channel_id=1, source_target_pairs={{0,4},{4,0},{8,12},{12,8},{16,20},{20,16},{24,28},{28,24},{1,5},{5... | collective-permute-start | bytes 393224 | tf_op jit(solution)/shard_map/ppermute | solution.py:29
  2.2 7.8 %collective-permute-start.4 = (bf16[256,256]{1,0:T(8,128)(2,1)S(1)}, bf16[256,256]{1,0:T(8,128)(2,1)S(1)}, u32[]{:S(2)}, u32[]{:S(2)}) collective-permute-start(bf16[256,256]{1,0:T(8,128)(2,1)S(1)} %shard_map.83.refs_0_), channel_id=1, source_target_pairs={{0,3},{1,2},{2,1},{3,0},{4,7},{5,6},{6,5},{7,4},{8,11},{9,10},{10,... | collective-permute-start | bytes 393224 | tf_op jit(solution)/shard_map/ppermute | solution.py:34
  5.7 7.0 %collective-permute-start.3 = (bf16[256,256]{1,0:T(8,128)(2,1)S(1)}, bf16[256,256]{1,0:T(8,128)(2,1)S(1)}, u32[]{:S(2)}, u32[]{:S(2)}) collective-permute-start(bf16[256,256]{1,0:T(8,128)(2,1)S(1)} %shard_map.83.refs_0_), channel_id=1, source_target_pairs={{0,2},{1,3},{2,0},{3,1},{4,6},{5,7},{6,4},{7,5},{8,10},{9,11},{10,... | collective-permute-start | bytes 393224 | tf_op jit(solution)/shard_map/ppermute | solution.py:34
  6.2 6.8 %collective-permute-start.2 = (bf16[256,256]{1,0:T(8,128)(2,1)S(1)}, bf16[256,256]{1,0:T(8,128)(2,1)S(1)}, u32[]{:S(2)}, u32[]{:S(2)}) collective-permute-start(bf16[256,256]{1,0:T(8,128)(2,1)S(1)} %shard_map.83.refs_0_), channel_id=1, source_target_pairs={{0,1},{1,0},{2,3},{3,2},{4,5},{5,4},{6,7},{7,6},{8,9},{9,8},{10,11... | collective-permute-start | bytes 393224 | tf_op jit(solution)/shard_map/ppermute | solution.py:34
  6.4 1.2 %collective-permute-start = (s32[8,768]{1,0:T(8,128)S(1)}, s32[8,768]{1,0:T(8,128)S(1)}, u32[]{:S(2)}, u32[]{:S(2)}) collective-permute-start(s32[8,768]{1,0:T(8,128)S(1)} %get-tuple-element.28.code), channel_id=1, source_target_pairs={{0,4},{4,0},{8,12},{12,8},{16,20},{20,16},{24,28},{28,24},{1,5},{5... | collective-permute-start | bytes 73736 | tf_op jit(solution)/shard_map/ppermute | solution.py:29
  13.6 4.7 %collective-permute-start.5 = (bf16[192,256]{1,0:T(8,128)(2,1)S(1)}, bf16[192,256]{1,0:T(8,128)(2,1)S(1)}, u32[]{:S(2)}, u32[]{:S(2)}) collective-permute-start(bf16[192,256]{1,0:T(8,128)(2,1)S(1)} %get-tuple-element.33), channel_id=1, source_target_pairs={{0,8},{4,12},{8,0},{12,4},{16,24},{20,28},{24,16},{28,20},{1,9},{5... | collective-permute-start | bytes 294920 | tf_op jit(solution)/shard_map/ppermute | solution.py:39
  15.2 10.6 %collective-permute-start.6 = (bf16[192,256]{1,0:T(8,128)(2,1)S(1)}, bf16[192,256]{1,0:T(8,128)(2,1)S(1)}, u32[]{:S(2)}, u32[]{:S(2)}) collective-permute-start(bf16[192,256]{1,0:T(8,128)(2,1)S(1)} %get-tuple-element.34), channel_id=1, source_target_pairs={{0,16},{4,20},{8,24},{12,28},{16,0},{20,4},{24,8},{28,12},{1,17},{... | collective-permute-start | bytes 294920 | tf_op jit(solution)/shard_map/ppermute | solution.py:39
  17.8 8.0 %collective-permute-start.7 = (bf16[192,256]{1,0:T(8,128)(2,1)S(1)}, bf16[192,256]{1,0:T(8,128)(2,1)S(1)}, u32[]{:S(2)}, u32[]{:S(2)}) collective-permute-start(bf16[192,256]{1,0:T(8,128)(2,1)S(1)} %get-tuple-element.35), channel_id=1, source_target_pairs={{0,24},{4,28},{8,16},{12,20},{16,8},{20,12},{24,0},{28,4},{1,25},{... | collective-permute-start | bytes 294920 | tf_op jit(solution)/shard_map/ppermute | solution.py:39
  25.9 1.4 %collective-permute-start.8 = (bf16[192,256]{1,0:T(8,128)(2,1)S(1)}, bf16[192,256]{1,0:T(8,128)(2,1)S(1)}, u32[]{:S(2)}, u32[]{:S(2)}) collective-permute-start(bf16[192,256]{1,0:T(8,128)(2,1)S(1)} %shard_map.85.hedge), channel_id=1, source_target_pairs={{0,4},{4,0},{8,12},{12,8},{16,20},{20,16},{24,28},{28,24},{1,5},{5... | collective-permute-start | bytes 294920 | tf_op jit(solution)/shard_map/ppermute | solution.py:29
  28.0 4.4 %collective-permute-start.9 = (bf16[136,256]{1,0:T(8,128)(2,1)S(1)}, bf16[136,256]{1,0:T(8,128)(2,1)S(1)}, u32[]{:S(2)}, u32[]{:S(2)}) collective-permute-start(bf16[136,256]{1,0:T(8,128)(2,1)S(1)} %get-tuple-element.41), channel_id=1, source_target_pairs={{0,1},{1,0},{2,3},{3,2},{4,5},{5,4},{6,7},{7,6},{8,9},{9,8},{10,11... | collective-permute-start | bytes 208904 | tf_op jit(solution)/shard_map/ppermute | solution.py:34
  29.5 5.7 %collective-permute-start.10 = (bf16[136,256]{1,0:T(8,128)(2,1)S(1)}, bf16[136,256]{1,0:T(8,128)(2,1)S(1)}, u32[]{:S(2)}, u32[]{:S(2)}) collective-permute-start(bf16[136,256]{1,0:T(8,128)(2,1)S(1)} %get-tuple-element.42), channel_id=1, source_target_pairs={{0,2},{1,3},{2,0},{3,1},{4,6},{5,7},{6,4},{7,5},{8,10},{9,11},{10,... | collective-permute-start | bytes 208904 | tf_op jit(solution)/shard_map/ppermute | solution.py:34
  29.7 5.6 %collective-permute-start.11 = (bf16[136,256]{1,0:T(8,128)(2,1)S(1)}, bf16[136,256]{1,0:T(8,128)(2,1)S(1)}, u32[]{:S(2)}, u32[]{:S(2)}) collective-permute-start(bf16[136,256]{1,0:T(8,128)(2,1)S(1)} %get-tuple-element.43), channel_id=1, source_target_pairs={{0,3},{1,2},{2,1},{3,0},{4,7},{5,6},{6,5},{7,4},{8,11},{9,10},{10,... | collective-permute-start | bytes 208904 | tf_op jit(solution)/shard_map/ppermute | solution.py:34
  35.3 6.7 %collective-permute-start.14 = (bf16[136,256]{1,0:T(8,128)(2,1)S(1)}, bf16[136,256]{1,0:T(8,128)(2,1)S(1)}, u32[]{:S(2)}, u32[]{:S(2)}) collective-permute-start(bf16[136,256]{1,0:T(8,128)(2,1)S(1)} %get-tuple-element.45), channel_id=1, source_target_pairs={{0,24},{4,28},{8,16},{12,20},{16,8},{20,12},{24,0},{28,4},{1,25},{... | collective-permute-start | bytes 208904 | tf_op jit(solution)/shard_map/ppermute | solution.py:39
  37.9 6.4 %collective-permute-start.13 = (bf16[136,256]{1,0:T(8,128)(2,1)S(1)}, bf16[136,256]{1,0:T(8,128)(2,1)S(1)}, u32[]{:S(2)}, u32[]{:S(2)}) collective-permute-start(bf16[136,256]{1,0:T(8,128)(2,1)S(1)} %get-tuple-element.45), channel_id=1, source_target_pairs={{0,16},{4,20},{8,24},{12,28},{16,0},{20,4},{24,8},{28,12},{1,17},{... | collective-permute-start | bytes 208904 | tf_op jit(solution)/shard_map/ppermute | solution.py:39
  38.5 5.8 %collective-permute-start.12 = (bf16[136,256]{1,0:T(8,128)(2,1)S(1)}, bf16[136,256]{1,0:T(8,128)(2,1)S(1)}, u32[]{:S(2)}, u32[]{:S(2)}) collective-permute-start(bf16[136,256]{1,0:T(8,128)(2,1)S(1)} %get-tuple-element.45), channel_id=1, source_target_pairs={{0,8},{4,12},{8,0},{12,4},{16,24},{20,28},{24,16},{28,20},{1,9},{5... | collective-permute-start | bytes 208904 | tf_op jit(solution)/shard_map/ppermute | solution.py:39
  44.3 5.2 %collective-permute-start.17 = (bf16[128,256]{1,0:T(8,128)(2,1)S(1)}, bf16[128,256]{1,0:T(8,128)(2,1)S(1)}, u32[]{:S(2)}, u32[]{:S(2)}) collective-permute-start(bf16[128,256]{1,0:T(8,128)(2,1)S(1)} %get-tuple-element.47), channel_id=1, source_target_pairs={{0,3},{1,2},{2,1},{3,0},{4,7},{5,6},{6,5},{7,4},{8,11},{9,10},{10,... | collective-permute-start | bytes 196616 | tf_op jit(solution)/shard_map/ppermute | solution.py:34
  45.8 4.4 %collective-permute-start.16 = (bf16[128,256]{1,0:T(8,128)(2,1)S(1)}, bf16[128,256]{1,0:T(8,128)(2,1)S(1)}, u32[]{:S(2)}, u32[]{:S(2)}) collective-permute-start(bf16[128,256]{1,0:T(8,128)(2,1)S(1)} %get-tuple-element.47), channel_id=1, source_target_pairs={{0,2},{1,3},{2,0},{3,1},{4,6},{5,7},{6,4},{7,5},{8,10},{9,11},{10,... | collective-permute-start | bytes 196616 | tf_op jit(solution)/shard_map/ppermute | solution.py:34
  47.1 4.3 %collective-permute-start.15 = (bf16[128,256]{1,0:T(8,128)(2,1)S(1)}, bf16[128,256]{1,0:T(8,128)(2,1)S(1)}, u32[]{:S(2)}, u32[]{:S(2)}) collective-permute-start(bf16[128,256]{1,0:T(8,128)(2,1)S(1)} %get-tuple-element.47), channel_id=1, source_target_pairs={{0,1},{1,0},{2,3},{3,2},{4,5},{5,4},{6,7},{7,6},{8,9},{9,8},{10,11... | collective-permute-start | bytes 196616 | tf_op jit(solution)/shard_map/ppermute | solution.py:34
  51.6 1.3 %collective-permute-start.18 = (bf16[96,256]{1,0:T(8,128)(2,1)S(1)}, bf16[96,256]{1,0:T(8,128)(2,1)S(1)}, u32[]{:S(2)}, u32[]{:S(2)}) collective-permute-start(bf16[96,256]{1,0:T(8,128)(2,1)S(1)} %get-tuple-element.50), channel_id=1, source_target_pairs={{0,4},{4,0},{8,12},{12,8},{16,20},{20,16},{24,28},{28,24},{1,5},{5... | collective-permute-start | bytes 147464 | tf_op jit(solution)/shard_map/ppermute | solution.py:29
where the time goes:
time: 53.9 us; the launch traced here: 53.7 us
  waiting for transfers between devices  26.4 us (49%)
  starting transfers between devices  20.8 us (39%)
  Pallas kernels  6.4 us (12%)
    ppermute x6, waiting for transfers between devices, send_chip(): lax.ppermute(value, 'node', [(i, to_peer(i // CORES, step, chips) * CORES...  12.2 us
    ppermute x9, starting transfers between devices, send_edge(): lax.ppermute(value, 'edge', [(i, to_peer(i, step, count)) for i in range(...  11.2 us
    ppermute x9, waiting for transfers between devices, send_edge(): lax.ppermute(value, 'edge', [(i, to_peer(i, step, count)) for i in range(...  10.7 us
    ppermute x6, starting transfers between devices, send_chip(): lax.ppermute(value, 'node', [(i, to_peer(i // CORES, step, chips) * CORES...  8.9 us
    pallas_call x11, Pallas kernels, call(): pl.pallas_call(kernel, out_shape=[pltpu.VMEM(shape, dtype) for shape, dty...  3.87 us
    ppermute x4, waiting for transfers between devices, swap_cores(): return lax.ppermute(value, 'node', [(i, i ^ 1) for i in range(count)])  3.5 us
    pallas_call x1, Pallas kernels, preload(): pl.pallas_call(preload_kernel, out_shape=[pltpu.VMEM(shape, kind) for sha...  1.7 us
  transfers between devices with their start and end apart: 19, of which 15 were waited for; matrix products, arithmetic and copies ran while one was open for 0% of the time, Pallas kernels for 7%

commit v1 on v0

--- a/solution.py
+++ b/solution.py
@@ -58,16 +58,34 @@
     return call
 
 
-def preload_kernel(feats, members, valid, degrees, *refs):
-    weights = (len(refs) - 6) // 2
-    sources, feats_here, code = refs[:weights], refs[weights], refs[weights + 1]
-    copies, (members_here, valid_here, degrees_here, sems) = refs[weights + 2 : -4], refs[-4:]
+def fetch_kernel(source, out, sem):
+    move = pltpu.make_async_copy(source, out, sem)
+    move.start()
+    move.wait()
+
+
+def fetch(value):
+    return pl.pallas_call(
+        fetch_kernel,
+        out_shape=pltpu.VMEM(value.shape, value.dtype),
+        in_specs=[pl.BlockSpec(memory_space=pltpu.HBM)],
+        out_specs=pl.BlockSpec(memory_space=pltpu.VMEM),
+        scratch_shapes=[pltpu.SemaphoreType.DMA],
+        compiler_params=pltpu.CompilerParams(vmem_limit_bytes=VMEM_LIMIT),
+        name="fetch",
+    )(pltpu.with_memory_space_constraint(value, pltpu.HBM))
+
+
+def preload_kernel(members, valid, degrees, *refs):
+    weights = (len(refs) - 5) // 2
+    sources, code = refs[:weights], refs[weights]
+    copies, (members_here, valid_here, degrees_here, sems) = refs[weights + 1 : -4], refs[-4:]
     moves = [
         pltpu.make_async_copy(source, target, sems.at[i])
         for i, (source, target) in enumerate(
             zip(
-                (members, valid, degrees, feats) + tuple(sources),
-                (members_here, valid_here, degrees_here, feats_here) + tuple(copies),
+                (members, valid, degrees) + tuple(sources),
+                (members_here, valid_here, degrees_here) + tuple(copies),
             )
         )
     ]
@@ -82,12 +100,12 @@
         move.wait()
 
 
-def preload(feats, members, valid, degrees, *weights):
-    args = (feats, members, valid, degrees) + weights
+def preload(members, valid, degrees, *weights):
+    args = (members, valid, degrees) + weights
     outside = pl.BlockSpec(memory_space=pltpu.HBM)
     spec = pl.BlockSpec(memory_space=pltpu.VMEM)
-    kept = [feats.shape, (2 * members.shape[0], members.shape[1])] + [w.shape for w in weights]
-    kinds = [feats.dtype, members.dtype] + [w.dtype for w in weights]
+    kept = [(2 * members.shape[0], members.shape[1])] + [w.shape for w in weights]
+    kinds = [members.dtype] + [w.dtype for w in weights]
     return pl.pallas_call(
         preload_kernel,
         out_shape=[pltpu.VMEM(shape, kind) for shape, kind in zip(kept, kinds)],
@@ -161,20 +179,31 @@
         lax.fori_loop(0, chips * CORES, lambda i, _: chunk(i // CORES, i % CORES), None)
 
 
-def aggregate_kernel(chips, edges, counts, *refs):
-    blocks, outs = refs[:edges], refs[edges:]
+def blocks_sum(counts, place, blocks, used):
     nodes = blocks[0].shape[0]
+    total = None
+    for ref, block in zip(blocks, used):
+        term = jnp.dot(
+            counts[place, block * nodes : (block + 1) * nodes], ref[...], preferred_element_type=jnp.float32
+        )
+        total = term if total is None else total + term
+    return total
+
+
+def first_kernel(group, used, counts, *refs):
+    blocks, out = refs[:-1], refs[-1]
+    for start in range(0, out.shape[0], group):
+        place = pl.ds(start, group)
+        out[place, :] = blocks_sum(counts, place, blocks, used)
+
+
+def aggregate_kernel(chips, used, counts, first, *refs):
+    blocks, outs = refs[: len(used)], refs[len(used) :]
     rows = outs[0].shape[0]
     group = min(chips, 4)
     for start in range(0, chips, group):
-        total = None
-        for block in range(edges):
-            term = jnp.dot(
-                counts[start * rows : (start + group) * rows, block * nodes : (block + 1) * nodes],
-                blocks[block][...],
-                preferred_element_type=jnp.float32,
-            )
-            total = term if total is None else total + term
+        place = pl.ds(start * rows, group * rows)
+        total = first[place, :] + blocks_sum(counts, place, blocks, used)
         for step in range(group):
             out = outs[start + step]
             out[...] = total[step * rows : (step + 1) * rows].astype(out.dtype)
@@ -188,20 +217,25 @@
     out[...] = (total / scale[:, :1]).astype(out.dtype)
 
 
-def gram_kernel(edges, hedge, hedge_other, w_key, w_value, *refs):
-    outs, full, gram = refs[:edges], refs[edges], refs[edges + 1]
+def project_kernel(hedge, w_key, w_value, key_part, value_part):
+    mine, _ = half_place(hedge.shape[1])
+    key_part[...] = jnp.dot(hedge[...], w_key[mine, :], preferred_element_type=jnp.float32)
+    value_part[...] = jnp.dot(hedge[...], w_value[mine, mine], preferred_element_type=jnp.float32)
+
+
+def gram_kernel(edges, hedge_other, key_part, value_part, w_key, w_value, *refs):
+    outs, gram = refs[:edges], refs[edges]
     edge = lax.axis_index("edge")
     width = w_key.shape[0]
     half = width // CORES
     rows = width // edges
     mine, other = half_place(half)
-    full[:, mine] = hedge[...]
-    full[:, other] = hedge_other[...]
-    both = full[...]
-    keys = feature_map(jnp.dot(both, w_key[...], preferred_element_type=jnp.float32)).astype(jnp.bfloat16)
-    values = jnp.dot(both, w_value[:, mine], preferred_element_type=jnp.float32).astype(jnp.bfloat16)
+    both = hedge_other[...]
+    keys = key_part[...] + jnp.dot(both, w_key[other, :], preferred_element_type=jnp.float32)
+    keys = feature_map(keys).astype(jnp.bfloat16)
+    values = value_part[...] + jnp.dot(both, w_value[other, mine], preferred_element_type=jnp.float32)
     gram[...] = lax.dot_general(
-        keys, values, (((0,), (0,)), ((), ())), preferred_element_type=jnp.float32
+        keys, values.astype(jnp.bfloat16), (((0,), (0,)), ((), ())), preferred_element_type=jnp.float32
     )
     key_sum = jnp.sum(keys.astype(jnp.float32), axis=0, keepdims=True)
     tail = [key_sum[:, i * half : (i + 1) * half] for i in range(CORES)]
@@ -212,7 +246,10 @@
         outs[step][rows:, :] = tail.astype(outs[step].dtype)
 
 
-def query_kernel(full, w_query, out):
+def query_kernel(hedge, hedge_other, w_query, out, full):
+    mine, other = half_place(hedge.shape[1])
+    full[:, mine] = hedge[...]
+    full[:, other] = hedge_other[...]
     out[...] = feature_map(
         jnp.dot(full[...], w_query[...], preferred_element_type=jnp.float32)
     ).astype(out.dtype)
@@ -225,6 +262,17 @@
         total = total + ref[...].astype(jnp.float32)
     for out in outs:
         out[...] = total[: out.shape[0]].astype(out.dtype)
+
+
+def numer_sum(edges, query, pieces, used):
+    edge = lax.axis_index("edge")
+    rows = query.shape[1] // edges
+    total = None
+    for ref, step in zip(pieces, used):
+        place = pl.ds(pl.multiple_of(from_peer(edge, step, edges) * rows, 128), rows)
+        term = jnp.dot(query[:, place], ref[:rows, :], preferred_element_type=jnp.float32)
+        total = term if total is None else total + term
+    return total
 
 
 def denom_kernel(query, whole, out):
@@ -238,8 +286,19 @@
     out[...] = jnp.broadcast_to(denom, out.shape)
 
 
-def attend_kernel(edges, query, denom, *refs):
-    pieces, (mine, other, gram, attended) = refs[:edges], refs[edges:]
+def numer_kernel(edges, used, query, *refs):
+    refs[-1][...] = numer_sum(edges, query, refs[:-1], used)
+
+
+def attend_kernel(edges, used, query, denom, numer, *refs):
+    pieces, (mine, other, attended) = refs[: len(used)], refs[len(used) :]
+    total = numer[...] + numer_sum(edges, query, pieces, used)
+    attended[...] = (total / denom[:, :1]).astype(attended.dtype)
+    split_rows(attended, mine, other)
+
+
+def gather_kernel(edges, query, denom, *refs):
+    pieces, (mine, other, attended, gram) = refs[:edges], refs[edges:]
     edge = lax.axis_index("edge")
     rows = query.shape[1] // edges
     for step in range(edges):
@@ -247,6 +306,10 @@
         gram[pl.ds(first, rows), :] = pieces[step][:rows, :]
     numer = jnp.dot(query[...], gram[...], preferred_element_type=jnp.float32)
     attended[...] = (numer / denom[:, :1]).astype(attended.dtype)
+    split_rows(attended, mine, other)
+
+
+def split_rows(attended, mine, other):
     here, there = half_place(mine.shape[0])
     mine[...] = attended[here, :]
     other[...] = attended[there, :]
@@ -306,48 +369,63 @@
     piece = rows + 8
 
     feats_other = swap_cores(node_feats)
-    feats, code, w_query, w_key, w_value, w_out = preload(
-        node_feats, members[0], incidence_mask[0], degrees[None], w_query, w_key, w_value, w_out
-    )
-    (packed,) = vmem_call(pack_kernel, [((part * CORES, half), bf16)])(feats, feats_other)
+    (packed,) = vmem_call(pack_kernel, [((part * CORES, half), bf16)])(
+        fetch(node_feats), feats_other
+    )
     blocks = [packed] + [send_edge(packed, step) for step in range(1, edges)]
+    code, w_query, w_key, w_value, w_out = preload(
+        members[0], incidence_mask[0], degrees[None], w_query, w_key, w_value, w_out
+    )
     code_other = swap_cores(code)
     counts, scale = vmem_call(
         functools.partial(counts_kernel, chips, edges, owned, part, slots),
         [((shard, CORES * edges * part), bf16), ((pair, 128), f32)],
         [pltpu.VMEM((shard, CORES * 2 * slots), jnp.int32)],
     )(code, code_other)
+    early, late = [0, edges - 1], list(range(1, edges - 1))
+    (first,) = vmem_call(
+        functools.partial(first_kernel, min(chips, 4) * pair, early), [((shard, half), f32)]
+    )(counts, *[blocks[i] for i in early])
     partial = vmem_call(
-        functools.partial(aggregate_kernel, chips, edges),
-        [((pair, half), f32)] + [((pair, half), bf16)] * (chips - 1),
-    )(counts, *blocks)
+        functools.partial(aggregate_kernel, chips, late), [((pair, half), f32)] + [((pair, half), bf16)] * (chips - 1)
+    )(counts, first, *[blocks[i] for i in late])
     arrived = [send_chip(partial[step], step) for step in range(1, chips)]
-    (hedge,) = vmem_call(hedge_kernel, [((pair, half), bf16)])(scale, partial[0], *arrived)
+    (hedge,) = vmem_call(hedge_kernel, [((pair, half), bf16)])(
+        scale, partial[0], *arrived
+    )
 
     hedge_other = swap_cores(hedge)
-    *grams, full = vmem_call(
+    parts = vmem_call(project_kernel, [((pair, width), f32), ((pair, half), f32)])(hedge, w_key, w_value)
+    grams = vmem_call(
         functools.partial(gram_kernel, edges),
-        [((piece, half), f32)] + [((piece, half), bf16)] * (edges - 1) + [((pair, width), bf16)],
+        [((piece, half), f32)] + [((piece, half), bf16)] * (edges - 1),
         [pltpu.VMEM((width, half), f32)],
-    )(hedge, hedge_other, w_key, w_value)
+    )(hedge_other, *parts, w_key, w_value)
     arrived = [send_edge(grams[step], step) for step in range(1, edges)]
-    (query,) = vmem_call(query_kernel, [((pair, width), bf16)])(full, w_query)
+    query, full = vmem_call(query_kernel, [((pair, width), bf16)] * 2)(
+        hedge, hedge_other, w_query
+    )
     plane, plane16 = vmem_call(
-        functools.partial(add_kernel, count=edges - 1),
-        [((piece, half), f32), ((piece, half), bf16)],
+        functools.partial(add_kernel, count=edges - 1), [((piece, half), f32), ((piece, half), bf16)]
     )(grams[0], *arrived)
     arrived = [send_chip(plane16, step) for step in range(1, chips)]
     whole, strip = vmem_call(
-        functools.partial(add_kernel, count=chips - 1),
-        [((piece, half), bf16), ((rows, half), bf16)],
+        functools.partial(add_kernel, count=chips - 1), [((piece, half), bf16), ((rows, half), bf16)]
     )(plane, *arrived)
     pieces = [whole] + [send_edge(strip, step) for step in range(1, edges)]
     (denom,) = vmem_call(denom_kernel, [((pair, 128), f32)])(query, whole)
-    mine, other = vmem_call(
-        functools.partial(attend_kernel, edges),
-        [((owned, half), bf16)] * CORES,
-        [pltpu.VMEM((width, half), bf16), pltpu.VMEM((pair, half), bf16)],
-    )(query, denom, *pieces)
+    halves, held = [((owned, half), bf16)] * CORES, pltpu.VMEM((pair, half), bf16)
+    if rows % 128 == 0:
+        (numer,) = vmem_call(
+            functools.partial(numer_kernel, edges, early), [((pair, half), f32)]
+        )(query, *[pieces[i] for i in early])
+        mine, other = vmem_call(
+            functools.partial(attend_kernel, edges, late), halves, [held]
+        )(query, denom, numer, *[pieces[i] for i in late])
+    else:
+        mine, other = vmem_call(
+            functools.partial(gather_kernel, edges), halves, [held, pltpu.VMEM((width, half), bf16)]
+        )(query, denom, *pieces)
     arrived = swap_cores(other)
     (base,) = vmem_call(base_kernel, [((owned, width), f32)])(full, mine, w_out)
     return write_output(base, arrived, w_out)
@@ -364,6 +442,4 @@
         P(),
         P(),
     )
-    return jax.shard_map(
-        body, mesh=mesh, in_specs=placed, out_specs=P(("edge", "node"), None), check_vma=False
-    )
+    return jax.shard_map(body, mesh=mesh, in_specs=placed, out_specs=P(("edge", "node"), None), check_vma=False)

time: 53.9 us -> 53 us (0.983)
  waiting for transfers between devices: 26.4 us -> 23.8 us
  Pallas kernels: 6.4 us -> 7.7 us
    ppermute x9, waiting for transfers between devices: 10.7 us -> 8.18 us  [send_edge(): lax.ppermute(value, 'edge', [(i, to_peer(i, step, count)) for i in range(...]
    pallas_call x0 -> x1, Pallas kernels: none -> 0.91 us  [fetch(): pl.pallas_call(fetch_kernel, out_shape=pltpu.VMEM(value.shape, value.dtyp...]
    pallas_call x11 -> x14, Pallas kernels: 3.87 us -> 4.33 us  [call(): pl.pallas_call(kernel, out_shape=[pltpu.VMEM(shape, dtype) for shape, dty...]
  transfers between devices with their start and end apart: 19 -> 19, of which waited for: 15 -> 16; matrix products, arithmetic and copies ran while one was open for 0% -> 0% of each run, Pallas kernels for 7% -> 10%
where the time goes in v1:
time: 53 us; the launch traced here: 52.8 us
  waiting for transfers between devices  23.8 us (45%)
  starting transfers between devices  21.2 us (40%)
  Pallas kernels  7.7 us (15%)
    ppermute x6, waiting for transfers between devices, send_chip(): lax.ppermute(value, 'node', [(i, to_peer(i // CORES, step, chips) * CORES...  12.1 us
    ppermute x9, starting transfers between devices, send_edge(): lax.ppermute(value, 'edge', [(i, to_peer(i, step, count)) for i in range(...  11.6 us
    ppermute x6, starting transfers between devices, send_chip(): lax.ppermute(value, 'node', [(i, to_peer(i // CORES, step, chips) * CORES...  8.9 us
    ppermute x9, waiting for transfers between devices, send_edge(): lax.ppermute(value, 'edge', [(i, to_peer(i, step, count)) for i in range(...  8.18 us
    pallas_call x14, Pallas kernels, call(): pl.pallas_call(kernel, out_shape=[pltpu.VMEM(shape, dtype) for shape, dty...  4.33 us
    ppermute x4, waiting for transfers between devices, swap_cores(): return lax.ppermute(value, 'node', [(i, i ^ 1) for i in range(count)])  3.51 us
    pallas_call x1, Pallas kernels, preload(): pl.pallas_call(preload_kernel, out_shape=[pltpu.VMEM(shape, kind) for sha...  1.62 us
  transfers between devices with their start and end apart: 19, of which 16 were waited for; matrix products, arithmetic and copies ran while one was open for 0% of the time, Pallas kernels for 10%

profile of v1, /device:TPU:0, one launch (start us, length us, event | category | flops | bytes accessed | tf_op | source)
XLA Modules:
  0.0 52.8 jit_solution(13159753108307185826)
XLA Ops:
  0.0 0.5 collective-permute-start.1
  0.5 0.9 %fetch.1.own = bf16[128,512]{1,0:T(8,128)(2,1)S(1)} custom-call(bf16[128,512]{1,0:T(8,128)(2,1)} %source.1), custom_call_target="tpu_custom_call" | custom-call | tf_op jit(solution)/shard_map/fetch/pallas_call | solution.py:68
  1.4 0.3 collective-permute-done.1.other
  1.7 3.9 %collective-permute-start.2 = (bf16[256,256]{1,0:T(8,128)(2,1)S(1)}, bf16[256,256]{1,0:T(8,128)(2,1)S(1)}, u32[]{:S(2)}, u32[]{:S(2)}) collective-permute-start(bf16[256,256]{1,0:T(8,128)(2,1)S(1)} %shard_map.83.refs_0_), channel_id=1, source_target_pairs={{0,3},{1,2},{2,1},{3,0},{4,7},{5,6},{6,5},{7,4},{8,11},{9,10},{10,... | collective-permute-start | bytes 393224 | tf_op jit(solution)/shard_map/ppermute | solution.py:34
  5.6 0.5 collective-permute-start.4
  6.1 0.1 collective-permute-start.3
  6.2 1.6 %preload.1 = (s32[8,768]{1,0:T(8,128)S(1)}, bf16[512,512]{1,0:T(8,128)(2,1)S(1)}, bf16[512,512]{1,0:T(8,128)(2,1)S(1)}, bf16[512,512]{1,0:T(8,128)(2,1)S(1)}, bf16[512,512]{1,0:T(8,128)(2,1)S(1)}) custom-call(s32[4,768]{1,0:T(4,128)} %bitcast.3, s32[4,768]{1,0:T(4,128)} %bitcast.4, s32[1,96]{1,0:T(1,128)} %bitcast.5, bf16[512,512]{1,0:T(8,128)(2,1)} %refs_0_.1, ...), custom_call_target="tpu_custom_call" | custom-call | tf_op jit(solution)/shard_map/preload/pallas_call | solution.py:109
  7.8 0.1 collective-permute-start
  7.9 1.2 %collective-permute-done.code_other = s32[8,768]{1,0:T(8,128)S(1)} collective-permute-done((s32[8,768]{1,0:T(8,128)S(1)}, s32[8,768]{1,0:T(8,128)S(1)}, u32[]{:S(2)}, u32[]{:S(2)}) %collective-permute-start) | collective-permute-done | bytes 24608 | tf_op jit(solution)/shard_map/ppermute | solution.py:29
  9.1 1.5 %shard_map.82 = (bf16[768,1024]{1,0:T(8,128)(2,1)S(1)}, f32[192,128]{1,0:T(8,128)S(1)}) custom-call(s32[8,768]{1,0:T(8,128)S(1)} %get-tuple-element.30.code, s32[8,768]{1,0:T(8,128)S(1)} %collective-permute-done.code_other), custom_call_target="tpu_custom_call" | custom-call | tf_op jit(solution)/shard_map/pallas_call | solution.py:49
  10.7 0.0 collective-permute-done.2.refs_1_
  10.7 0.4 shard_map.84.first
  11.0 1.2 %collective-permute-done.4.refs_1_ = bf16[256,256]{1,0:T(8,128)(2,1)S(1)} collective-permute-done((bf16[256,256]{1,0:T(8,128)(2,1)S(1)}, bf16[256,256]{1,0:T(8,128)(2,1)S(1)}, u32[]{:S(2)}, u32[]{:S(2)}) %collective-permute-start.4) | collective-permute-done | bytes 131104 | tf_op jit(solution)/shard_map/ppermute | solution.py:34
  12.2 0.3 collective-permute-done.3.refs_0_
  12.5 0.4 shard_map.85
  12.8 1.6 %collective-permute-start.5 = (bf16[192,256]{1,0:T(8,128)(2,1)S(1)}, bf16[192,256]{1,0:T(8,128)(2,1)S(1)}, u32[]{:S(2)}, u32[]{:S(2)}) collective-permute-start(bf16[192,256]{1,0:T(8,128)(2,1)S(1)} %get-tuple-element.34), channel_id=1, source_target_pairs={{0,8},{4,12},{8,0},{12,4},{16,24},{20,28},{24,16},{28,20},{1,9},{5... | collective-permute-start | bytes 294920 | tf_op jit(solution)/shard_map/ppermute | solution.py:39
  14.5 2.6 %collective-permute-start.6 = (bf16[192,256]{1,0:T(8,128)(2,1)S(1)}, bf16[192,256]{1,0:T(8,128)(2,1)S(1)}, u32[]{:S(2)}, u32[]{:S(2)}) collective-permute-start(bf16[192,256]{1,0:T(8,128)(2,1)S(1)} %get-tuple-element.35), channel_id=1, source_target_pairs={{0,16},{4,20},{8,24},{12,28},{16,0},{20,4},{24,8},{28,12},{1,17},{... | collective-permute-start | bytes 294920 | tf_op jit(solution)/shard_map/ppermute | solution.py:39
  17.1 0.2 collective-permute-start.7
  17.3 0.2 collective-permute-done.5.refs_0_
  17.5 7.5 %collective-permute-done.6.refs_1_ = bf16[192,256]{1,0:T(8,128)(2,1)S(1)} collective-permute-done((bf16[192,256]{1,0:T(8,128)(2,1)S(1)}, bf16[192,256]{1,0:T(8,128)(2,1)S(1)}, u32[]{:S(2)}, u32[]{:S(2)}) %collective-permute-start.6) | collective-permute-done | bytes 98336 | tf_op jit(solution)/shard_map/ppermute | solution.py:39
  25.0 0.0 collective-permute-done.7.refs_2_
  25.0 0.1 shard_map.86.hedge
  25.1 0.1 collective-permute-start.8
  25.2 0.3 shard_map.88
  25.5 1.0 %collective-permute-done.8.hedge_other = bf16[192,256]{1,0:T(8,128)(2,1)S(1)} collective-permute-done((bf16[192,256]{1,0:T(8,128)(2,1)S(1)}, bf16[192,256]{1,0:T(8,128)(2,1)S(1)}, u32[]{:S(2)}, u32[]{:S(2)}) %collective-permute-start.8) | collective-permute-done | bytes 98336 | tf_op jit(solution)/shard_map/ppermute | solution.py:29
  26.5 0.6 %shard_map.89 = (f32[136,256]{1,0:T(8,128)S(1)}, bf16[136,256]{1,0:T(8,128)(2,1)S(1)}, bf16[136,256]{1,0:T(8,128)(2,1)S(1)}, bf16[136,256]{1,0:T(8,128)(2,1)S(1)}) custom-call(bf16[192,256]{1,0:T(8,128)(2,1)S(1)} %collective-permute-done.8.hedge_other, f32[192,512]{1,0:T(8,128)S(1)} %get-tuple-element.42.key_part, ...), custom_call_target="tpu_custom_call" | custom-call | tf_op jit(solution)/shard_map/pallas_call | solution.py:49
  27.1 1.5 %collective-permute-start.9 = (bf16[136,256]{1,0:T(8,128)(2,1)S(1)}, bf16[136,256]{1,0:T(8,128)(2,1)S(1)}, u32[]{:S(2)}, u32[]{:S(2)}) collective-permute-start(bf16[136,256]{1,0:T(8,128)(2,1)S(1)} %get-tuple-element.45), channel_id=1, source_target_pairs={{0,1},{1,0},{2,3},{3,2},{4,5},{5,4},{6,7},{7,6},{8,9},{9,8},{10,11... | collective-permute-start | bytes 208904 | tf_op jit(solution)/shard_map/ppermute | solution.py:34
  28.6 0.8 %collective-permute-start.10 = (bf16[136,256]{1,0:T(8,128)(2,1)S(1)}, bf16[136,256]{1,0:T(8,128)(2,1)S(1)}, u32[]{:S(2)}, u32[]{:S(2)}) collective-permute-start(bf16[136,256]{1,0:T(8,128)(2,1)S(1)} %get-tuple-element.46), channel_id=1, source_target_pairs={{0,2},{1,3},{2,0},{3,1},{4,6},{5,7},{6,4},{7,5},{8,10},{9,11},{10,... | collective-permute-start | bytes 208904 | tf_op jit(solution)/shard_map/ppermute | solution.py:34
  29.4 1.2 %collective-permute-start.11 = (bf16[136,256]{1,0:T(8,128)(2,1)S(1)}, bf16[136,256]{1,0:T(8,128)(2,1)S(1)}, u32[]{:S(2)}, u32[]{:S(2)}) collective-permute-start(bf16[136,256]{1,0:T(8,128)(2,1)S(1)} %get-tuple-element.47), channel_id=1, source_target_pairs={{0,3},{1,2},{2,1},{3,0},{4,7},{5,6},{6,5},{7,4},{8,11},{9,10},{10,... | collective-permute-start | bytes 208904 | tf_op jit(solution)/shard_map/ppermute | solution.py:34
  30.7 0.8 %collective-permute-done.9.refs_0_ = bf16[136,256]{1,0:T(8,128)(2,1)S(1)} collective-permute-done((bf16[136,256]{1,0:T(8,128)(2,1)S(1)}, bf16[136,256]{1,0:T(8,128)(2,1)S(1)}, u32[]{:S(2)}, u32[]{:S(2)}) %collective-permute-start.9) | collective-permute-done | bytes 69664 | tf_op jit(solution)/shard_map/ppermute | solution.py:34
  31.5 2.2 %collective-permute-done.10.refs_1_ = bf16[136,256]{1,0:T(8,128)(2,1)S(1)} collective-permute-done((bf16[136,256]{1,0:T(8,128)(2,1)S(1)}, bf16[136,256]{1,0:T(8,128)(2,1)S(1)}, u32[]{:S(2)}, u32[]{:S(2)}) %collective-permute-start.10) | collective-permute-done | bytes 69664 | tf_op jit(solution)/shard_map/ppermute | solution.py:34
  33.7 0.9 %collective-permute-done.11.refs_2_ = bf16[136,256]{1,0:T(8,128)(2,1)S(1)} collective-permute-done((bf16[136,256]{1,0:T(8,128)(2,1)S(1)}, bf16[136,256]{1,0:T(8,128)(2,1)S(1)}, u32[]{:S(2)}, u32[]{:S(2)}) %collective-permute-start.11) | collective-permute-done | bytes 69664 | tf_op jit(solution)/shard_map/ppermute | solution.py:34
  34.7 2.5 %collective-permute-start.14 = (bf16[136,256]{1,0:T(8,128)(2,1)S(1)}, bf16[136,256]{1,0:T(8,128)(2,1)S(1)}, u32[]{:S(2)}, u32[]{:S(2)}) collective-permute-start(bf16[136,256]{1,0:T(8,128)(2,1)S(1)} %get-tuple-element.49), channel_id=1, source_target_pairs={{0,24},{4,28},{8,16},{12,20},{16,8},{20,12},{24,0},{28,4},{1,25},{... | collective-permute-start | bytes 208904 | tf_op jit(solution)/shard_map/ppermute | solution.py:39
  37.2 0.6 %collective-permute-start.13 = (bf16[136,256]{1,0:T(8,128)(2,1)S(1)}, bf16[136,256]{1,0:T(8,128)(2,1)S(1)}, u32[]{:S(2)}, u32[]{:S(2)}) collective-permute-start(bf16[136,256]{1,0:T(8,128)(2,1)S(1)} %get-tuple-element.49), channel_id=1, source_target_pairs={{0,16},{4,20},{8,24},{12,28},{16,0},{20,4},{24,8},{28,12},{1,17},{... | collective-permute-start | bytes 208904 | tf_op jit(solution)/shard_map/ppermute | solution.py:39
  37.8 1.3 %collective-permute-start.12 = (bf16[136,256]{1,0:T(8,128)(2,1)S(1)}, bf16[136,256]{1,0:T(8,128)(2,1)S(1)}, u32[]{:S(2)}, u32[]{:S(2)}) collective-permute-start(bf16[136,256]{1,0:T(8,128)(2,1)S(1)} %get-tuple-element.49), channel_id=1, source_target_pairs={{0,8},{4,12},{8,0},{12,4},{16,24},{20,28},{24,16},{28,20},{1,9},{5... | collective-permute-start | bytes 208904 | tf_op jit(solution)/shard_map/ppermute | solution.py:39
  39.1 2.5 %collective-permute-done.14.refs_2_ = bf16[136,256]{1,0:T(8,128)(2,1)S(1)} collective-permute-done((bf16[136,256]{1,0:T(8,128)(2,1)S(1)}, bf16[136,256]{1,0:T(8,128)(2,1)S(1)}, u32[]{:S(2)}, u32[]{:S(2)}) %collective-permute-start.14) | collective-permute-done | bytes 69664 | tf_op jit(solution)/shard_map/ppermute | solution.py:39
  41.6 1.8 %collective-permute-done.13.refs_1_ = bf16[136,256]{1,0:T(8,128)(2,1)S(1)} collective-permute-done((bf16[136,256]{1,0:T(8,128)(2,1)S(1)}, bf16[136,256]{1,0:T(8,128)(2,1)S(1)}, u32[]{:S(2)}, u32[]{:S(2)}) %collective-permute-start.13) | collective-permute-done | bytes 69664 | tf_op jit(solution)/shard_map/ppermute | solution.py:39
  43.4 0.0 collective-permute-done.12.refs_0_
  43.5 1.4 %collective-permute-start.15 = (bf16[128,256]{1,0:T(8,128)(2,1)S(1)}, bf16[128,256]{1,0:T(8,128)(2,1)S(1)}, u32[]{:S(2)}, u32[]{:S(2)}) collective-permute-start(bf16[128,256]{1,0:T(8,128)(2,1)S(1)} %get-tuple-element.51), channel_id=1, source_target_pairs={{0,3},{1,2},{2,1},{3,0},{4,7},{5,6},{6,5},{7,4},{8,11},{9,10},{10,... | collective-permute-start | bytes 196616 | tf_op jit(solution)/shard_map/ppermute | solution.py:34
  44.9 1.3 %collective-permute-start.17 = (bf16[128,256]{1,0:T(8,128)(2,1)S(1)}, bf16[128,256]{1,0:T(8,128)(2,1)S(1)}, u32[]{:S(2)}, u32[]{:S(2)}) collective-permute-start(bf16[128,256]{1,0:T(8,128)(2,1)S(1)} %get-tuple-element.51), channel_id=1, source_target_pairs={{0,2},{1,3},{2,0},{3,1},{4,6},{5,7},{6,4},{7,5},{8,10},{9,11},{10,... | collective-permute-start | bytes 196616 | tf_op jit(solution)/shard_map/ppermute | solution.py:34
  46.2 0.8 %collective-permute-start.16 = (bf16[128,256]{1,0:T(8,128)(2,1)S(1)}, bf16[128,256]{1,0:T(8,128)(2,1)S(1)}, u32[]{:S(2)}, u32[]{:S(2)}) collective-permute-start(bf16[128,256]{1,0:T(8,128)(2,1)S(1)} %get-tuple-element.51), channel_id=1, source_target_pairs={{0,1},{1,0},{2,3},{3,2},{4,5},{5,4},{6,7},{7,6},{8,9},{9,8},{10,11... | collective-permute-start | bytes 196616 | tf_op jit(solution)/shard_map/ppermute | solution.py:34
  47.1 0.3 shard_map.87
  47.4 0.1 shard_map.92.denom
  47.5 1.2 %collective-permute-done.15.refs_1_ = bf16[128,256]{1,0:T(8,128)(2,1)S(1)} collective-permute-done((bf16[128,256]{1,0:T(8,128)(2,1)S(1)}, bf16[128,256]{1,0:T(8,128)(2,1)S(1)}, u32[]{:S(2)}, u32[]{:S(2)}) %collective-permute-start.15) | collective-permute-done | bytes 65568 | tf_op jit(solution)/shard_map/ppermute | solution.py:34
  48.7 0.2 shard_map.93.numer
  48.9 0.5 collective-permute-done.17.refs_1_
  49.4 1.0 %collective-permute-done.16.refs_0_ = bf16[128,256]{1,0:T(8,128)(2,1)S(1)} collective-permute-done((bf16[128,256]{1,0:T(8,128)(2,1)S(1)}, bf16[128,256]{1,0:T(8,128)(2,1)S(1)}, u32[]{:S(2)}, u32[]{:S(2)}) %collective-permute-start.16) | collective-permute-done | bytes 65568 | tf_op jit(solution)/shard_map/ppermute | solution.py:34
  50.5 0.2 shard_map.94
  50.7 0.1 collective-permute-start.18
  50.8 0.2 shard_map.95.base
  51.0 1.0 %collective-permute-done.18.other = bf16[96,256]{1,0:T(8,128)(2,1)S(1)} collective-permute-done((bf16[96,256]{1,0:T(8,128)(2,1)S(1)}, bf16[96,256]{1,0:T(8,128)(2,1)S(1)}, u32[]{:S(2)}, u32[]{:S(2)}) %collective-permute-start.18) | collective-permute-done | bytes 49184 | tf_op jit(solution)/shard_map/ppermute | solution.py:29
  52.0 0.8 %output.1 = bf16[96,512]{1,0:T(8,128)(2,1)} custom-call(f32[96,512]{1,0:T(8,128)S(1)} %shard_map.95.base, bf16[96,256]{1,0:T(8,128)(2,1)S(1)} %collective-permute-done.18.other, bf16[512,512]{1,0:T(8,128)(2,1)S(1)} %get-tuple-element.53.w_out), custom_call_target="tpu_custom_call" | custom-call | tf_op jit(solution)/shard_map/output/pallas_call | solution.py:345
  (3 shorter events, 0.1 us)
Async XLA Ops:
  0.0 1.7 %collective-permute-start.1 = (bf16[128,512]{1,0:T(8,128)(2,1)}, bf16[128,512]{1,0:T(8,128)(2,1)S(1)}, u32[]{:S(2)}, u32[]{:S(2)}) collective-permute-start(bf16[128,512]{1,0:T(8,128)(2,1)} %source.1), channel_id=1, source_target_pairs={{0,4},{4,0},{8,12},{12,8},{16,20},{20,16},{24,28},{28,24},{1,5},{5... | collective-permute-start | bytes 393224 | tf_op jit(solution)/shard_map/ppermute | solution.py:29
  1.7 8.9 %collective-permute-start.2 = (bf16[256,256]{1,0:T(8,128)(2,1)S(1)}, bf16[256,256]{1,0:T(8,128)(2,1)S(1)}, u32[]{:S(2)}, u32[]{:S(2)}) collective-permute-start(bf16[256,256]{1,0:T(8,128)(2,1)S(1)} %shard_map.83.refs_0_), channel_id=1, source_target_pairs={{0,3},{1,2},{2,1},{3,0},{4,7},{5,6},{6,5},{7,4},{8,11},{9,10},{10,... | collective-permute-start | bytes 393224 | tf_op jit(solution)/shard_map/ppermute | solution.py:34
  5.6 6.6 %collective-permute-start.4 = (bf16[256,256]{1,0:T(8,128)(2,1)S(1)}, bf16[256,256]{1,0:T(8,128)(2,1)S(1)}, u32[]{:S(2)}, u32[]{:S(2)}) collective-permute-start(bf16[256,256]{1,0:T(8,128)(2,1)S(1)} %shard_map.83.refs_0_), channel_id=1, source_target_pairs={{0,2},{1,3},{2,0},{3,1},{4,6},{5,7},{6,4},{7,5},{8,10},{9,11},{10,... | collective-permute-start | bytes 393224 | tf_op jit(solution)/shard_map/ppermute | solution.py:34
  6.1 6.4 %collective-permute-start.3 = (bf16[256,256]{1,0:T(8,128)(2,1)S(1)}, bf16[256,256]{1,0:T(8,128)(2,1)S(1)}, u32[]{:S(2)}, u32[]{:S(2)}) collective-permute-start(bf16[256,256]{1,0:T(8,128)(2,1)S(1)} %shard_map.83.refs_0_), channel_id=1, source_target_pairs={{0,1},{1,0},{2,3},{3,2},{4,5},{5,4},{6,7},{7,6},{8,9},{9,8},{10,11... | collective-permute-start | bytes 393224 | tf_op jit(solution)/shard_map/ppermute | solution.py:34
  7.8 1.3 %collective-permute-start = (s32[8,768]{1,0:T(8,128)S(1)}, s32[8,768]{1,0:T(8,128)S(1)}, u32[]{:S(2)}, u32[]{:S(2)}) collective-permute-start(s32[8,768]{1,0:T(8,128)S(1)} %get-tuple-element.30.code), channel_id=1, source_target_pairs={{0,4},{4,0},{8,12},{12,8},{16,20},{20,16},{24,28},{28,24},{1,5},{5... | collective-permute-start | bytes 73736 | tf_op jit(solution)/shard_map/ppermute | solution.py:29
  12.8 4.7 %collective-permute-start.5 = (bf16[192,256]{1,0:T(8,128)(2,1)S(1)}, bf16[192,256]{1,0:T(8,128)(2,1)S(1)}, u32[]{:S(2)}, u32[]{:S(2)}) collective-permute-start(bf16[192,256]{1,0:T(8,128)(2,1)S(1)} %get-tuple-element.34), channel_id=1, source_target_pairs={{0,8},{4,12},{8,0},{12,4},{16,24},{20,28},{24,16},{28,20},{1,9},{5... | collective-permute-start | bytes 294920 | tf_op jit(solution)/shard_map/ppermute | solution.py:39
  14.5 10.6 %collective-permute-start.6 = (bf16[192,256]{1,0:T(8,128)(2,1)S(1)}, bf16[192,256]{1,0:T(8,128)(2,1)S(1)}, u32[]{:S(2)}, u32[]{:S(2)}) collective-permute-start(bf16[192,256]{1,0:T(8,128)(2,1)S(1)} %get-tuple-element.35), channel_id=1, source_target_pairs={{0,16},{4,20},{8,24},{12,28},{16,0},{20,4},{24,8},{28,12},{1,17},{... | collective-permute-start | bytes 294920 | tf_op jit(solution)/shard_map/ppermute | solution.py:39
  17.1 8.0 %collective-permute-start.7 = (bf16[192,256]{1,0:T(8,128)(2,1)S(1)}, bf16[192,256]{1,0:T(8,128)(2,1)S(1)}, u32[]{:S(2)}, u32[]{:S(2)}) collective-permute-start(bf16[192,256]{1,0:T(8,128)(2,1)S(1)} %get-tuple-element.36), channel_id=1, source_target_pairs={{0,24},{4,28},{8,16},{12,20},{16,8},{20,12},{24,0},{28,4},{1,25},{... | collective-permute-start | bytes 294920 | tf_op jit(solution)/shard_map/ppermute | solution.py:39
  25.1 1.4 %collective-permute-start.8 = (bf16[192,256]{1,0:T(8,128)(2,1)S(1)}, bf16[192,256]{1,0:T(8,128)(2,1)S(1)}, u32[]{:S(2)}, u32[]{:S(2)}) collective-permute-start(bf16[192,256]{1,0:T(8,128)(2,1)S(1)} %shard_map.86.hedge), channel_id=1, source_target_pairs={{0,4},{4,0},{8,12},{12,8},{16,20},{20,16},{24,28},{28,24},{1,5},{5... | collective-permute-start | bytes 294920 | tf_op jit(solution)/shard_map/ppermute | solution.py:29
  27.1 4.4 %collective-permute-start.9 = (bf16[136,256]{1,0:T(8,128)(2,1)S(1)}, bf16[136,256]{1,0:T(8,128)(2,1)S(1)}, u32[]{:S(2)}, u32[]{:S(2)}) collective-permute-start(bf16[136,256]{1,0:T(8,128)(2,1)S(1)} %get-tuple-element.45), channel_id=1, source_target_pairs={{0,1},{1,0},{2,3},{3,2},{4,5},{5,4},{6,7},{7,6},{8,9},{9,8},{10,11... | collective-permute-start | bytes 208904 | tf_op jit(solution)/shard_map/ppermute | solution.py:34
  28.6 5.1 %collective-permute-start.10 = (bf16[136,256]{1,0:T(8,128)(2,1)S(1)}, bf16[136,256]{1,0:T(8,128)(2,1)S(1)}, u32[]{:S(2)}, u32[]{:S(2)}) collective-permute-start(bf16[136,256]{1,0:T(8,128)(2,1)S(1)} %get-tuple-element.46), channel_id=1, source_target_pairs={{0,2},{1,3},{2,0},{3,1},{4,6},{5,7},{6,4},{7,5},{8,10},{9,11},{10,... | collective-permute-start | bytes 208904 | tf_op jit(solution)/shard_map/ppermute | solution.py:34
  29.4 5.2 %collective-permute-start.11 = (bf16[136,256]{1,0:T(8,128)(2,1)S(1)}, bf16[136,256]{1,0:T(8,128)(2,1)S(1)}, u32[]{:S(2)}, u32[]{:S(2)}) collective-permute-start(bf16[136,256]{1,0:T(8,128)(2,1)S(1)} %get-tuple-element.47), channel_id=1, source_target_pairs={{0,3},{1,2},{2,1},{3,0},{4,7},{5,6},{6,5},{7,4},{8,11},{9,10},{10,... | collective-permute-start | bytes 208904 | tf_op jit(solution)/shard_map/ppermute | solution.py:34
  34.7 6.9 %collective-permute-start.14 = (bf16[136,256]{1,0:T(8,128)(2,1)S(1)}, bf16[136,256]{1,0:T(8,128)(2,1)S(1)}, u32[]{:S(2)}, u32[]{:S(2)}) collective-permute-start(bf16[136,256]{1,0:T(8,128)(2,1)S(1)} %get-tuple-element.49), channel_id=1, source_target_pairs={{0,24},{4,28},{8,16},{12,20},{16,8},{20,12},{24,0},{28,4},{1,25},{... | collective-permute-start | bytes 208904 | tf_op jit(solution)/shard_map/ppermute | solution.py:39
  37.2 6.2 %collective-permute-start.13 = (bf16[136,256]{1,0:T(8,128)(2,1)S(1)}, bf16[136,256]{1,0:T(8,128)(2,1)S(1)}, u32[]{:S(2)}, u32[]{:S(2)}) collective-permute-start(bf16[136,256]{1,0:T(8,128)(2,1)S(1)} %get-tuple-element.49), channel_id=1, source_target_pairs={{0,16},{4,20},{8,24},{12,28},{16,0},{20,4},{24,8},{28,12},{1,17},{... | collective-permute-start | bytes 208904 | tf_op jit(solution)/shard_map/ppermute | solution.py:39
  37.8 5.6 %collective-permute-start.12 = (bf16[136,256]{1,0:T(8,128)(2,1)S(1)}, bf16[136,256]{1,0:T(8,128)(2,1)S(1)}, u32[]{:S(2)}, u32[]{:S(2)}) collective-permute-start(bf16[136,256]{1,0:T(8,128)(2,1)S(1)} %get-tuple-element.49), channel_id=1, source_target_pairs={{0,8},{4,12},{8,0},{12,4},{16,24},{20,28},{24,16},{28,20},{1,9},{5... | collective-permute-start | bytes 208904 | tf_op jit(solution)/shard_map/ppermute | solution.py:39
  43.5 5.3 %collective-permute-start.15 = (bf16[128,256]{1,0:T(8,128)(2,1)S(1)}, bf16[128,256]{1,0:T(8,128)(2,1)S(1)}, u32[]{:S(2)}, u32[]{:S(2)}) collective-permute-start(bf16[128,256]{1,0:T(8,128)(2,1)S(1)} %get-tuple-element.51), channel_id=1, source_target_pairs={{0,3},{1,2},{2,1},{3,0},{4,7},{5,6},{6,5},{7,4},{8,11},{9,10},{10,... | collective-permute-start | bytes 196616 | tf_op jit(solution)/shard_map/ppermute | solution.py:34
  44.9 4.5 %collective-permute-start.17 = (bf16[128,256]{1,0:T(8,128)(2,1)S(1)}, bf16[128,256]{1,0:T(8,128)(2,1)S(1)}, u32[]{:S(2)}, u32[]{:S(2)}) collective-permute-start(bf16[128,256]{1,0:T(8,128)(2,1)S(1)} %get-tuple-element.51), channel_id=1, source_target_pairs={{0,2},{1,3},{2,0},{3,1},{4,6},{5,7},{6,4},{7,5},{8,10},{9,11},{10,... | collective-permute-start | bytes 196616 | tf_op jit(solution)/shard_map/ppermute | solution.py:34
  46.2 4.3 %collective-permute-start.16 = (bf16[128,256]{1,0:T(8,128)(2,1)S(1)}, bf16[128,256]{1,0:T(8,128)(2,1)S(1)}, u32[]{:S(2)}, u32[]{:S(2)}) collective-permute-start(bf16[128,256]{1,0:T(8,128)(2,1)S(1)} %get-tuple-element.51), channel_id=1, source_target_pairs={{0,1},{1,0},{2,3},{3,2},{4,5},{5,4},{6,7},{7,6},{8,9},{9,8},{10,11... | collective-permute-start | bytes 196616 | tf_op jit(solution)/shard_map/ppermute | solution.py:34
  50.7 1.3 %collective-permute-start.18 = (bf16[96,256]{1,0:T(8,128)(2,1)S(1)}, bf16[96,256]{1,0:T(8,128)(2,1)S(1)}, u32[]{:S(2)}, u32[]{:S(2)}) collective-permute-start(bf16[96,256]{1,0:T(8,128)(2,1)S(1)} %get-tuple-element.54), channel_id=1, source_target_pairs={{0,4},{4,0},{8,12},{12,8},{16,20},{20,16},{24,28},{28,24},{1,5},{5... | collective-permute-start | bytes 147464 | tf_op jit(solution)/shard_map/ppermute | solution.py:29

commit v2 on v1

--- a/solution.py
+++ b/solution.py
@@ -9,6 +9,8 @@
 
 
 VMEM_LIMIT = 16 * 2**20
+
+SENDS_FIRST = 1
 CORES = 2
 
 
@@ -76,52 +78,6 @@
     )(pltpu.with_memory_space_constraint(value, pltpu.HBM))
 
 
-def preload_kernel(members, valid, degrees, *refs):
-    weights = (len(refs) - 5) // 2
-    sources, code = refs[:weights], refs[weights]
-    copies, (members_here, valid_here, degrees_here, sems) = refs[weights + 1 : -4], refs[-4:]
-    moves = [
-        pltpu.make_async_copy(source, target, sems.at[i])
-        for i, (source, target) in enumerate(
-            zip(
-                (members, valid, degrees) + tuple(sources),
-                (members_here, valid_here, degrees_here) + tuple(copies),
-            )
-        )
-    ]
-    for move in moves:
-        move.start()
-    for move in moves[:3]:
-        move.wait()
-    slots, owned = members.shape[0], degrees.shape[1]
-    code[:slots, :] = jnp.where(valid_here[...] == 1, members_here[...], -1)
-    code[slots : slots + 1, :owned] = degrees_here[...]
-    for move in moves[3:]:
-        move.wait()
-
-
-def preload(members, valid, degrees, *weights):
-    args = (members, valid, degrees) + weights
-    outside = pl.BlockSpec(memory_space=pltpu.HBM)
-    spec = pl.BlockSpec(memory_space=pltpu.VMEM)
-    kept = [(2 * members.shape[0], members.shape[1])] + [w.shape for w in weights]
-    kinds = [members.dtype] + [w.dtype for w in weights]
-    return pl.pallas_call(
-        preload_kernel,
-        out_shape=[pltpu.VMEM(shape, kind) for shape, kind in zip(kept, kinds)],
-        in_specs=[outside] * len(args),
-        out_specs=[spec] * len(kept),
-        scratch_shapes=[
-            pltpu.VMEM(members.shape, members.dtype),
-            pltpu.VMEM(valid.shape, valid.dtype),
-            pltpu.VMEM(degrees.shape, degrees.dtype),
-            pltpu.SemaphoreType.DMA((len(args),)),
-        ],
-        compiler_params=pltpu.CompilerParams(vmem_limit_bytes=VMEM_LIMIT),
-        name="preload",
-    )(*[pltpu.with_memory_space_constraint(a, pltpu.HBM) for a in args])
-
-
 def feature_map(values):
     return jnp.where(values > 0, values + 1.0, jnp.exp(jnp.minimum(values, 0.0)))
 
@@ -141,17 +97,46 @@
     out[theirs, :] = other[:, columns]
 
 
-def counts_kernel(chips, edges, owned, part, slots, code, code_other, counts, scale, columns):
+def prepare_kernel(turn, chips, edges, owned, part, weights, *refs):
+    members, valid, degrees, members_other, valid_other = refs[:5]
+    sources, refs = refs[5 : 5 + weights], refs[5 + weights :]
+    if len(refs) > 7 + weights:
+        refs = refs[2 + weights :]
+    counts, degree = refs[:2]
+    copies, (members_here, valid_here, degrees_here, columns, sems) = refs[2 : 2 + weights], refs[2 + weights :]
     core = lax.axis_index("node") % CORES
+    slots = members.shape[0]
+
+    @pl.when(core == turn)
+    def work():
+        moves = [
+            pltpu.make_async_copy(source, target, sems.at[i])
+            for i, (source, target) in enumerate(
+                zip(
+                    (members, valid, degrees) + tuple(sources),
+                    (members_here, valid_here, degrees_here) + tuple(copies),
+                )
+            )
+        ]
+        for move in moves:
+            move.start()
+        for move in moves[:3]:
+            move.wait()
+        degree[...] = jnp.ones(degree.shape, degree.dtype)
+        degree[:1, :owned] = degrees_here[...]
+        own = jnp.where(valid_here[...] == 1, members_here[...], -1)
+        other = jnp.where(valid_other[...] == 1, members_other[...], -1)
+        first = jnp.where(core == 0, own, other)
+        second = jnp.where(core == 0, other, own)
+        columns[...] = jnp.concatenate([first, second], axis=0).T
+        build_counts(chips, edges, owned, part, slots, columns, counts)
+        for move in moves[3:]:
+            move.wait()
+
+
+def build_counts(chips, edges, owned, part, slots, columns, counts):
     chip = lax.axis_index("node") // CORES
     edge = lax.axis_index("edge")
-    first = jnp.where(core == 0, code[...], code_other[...])
-    second = jnp.where(core == 0, code_other[...], code[...])
-    columns[...] = jnp.concatenate([first, second], axis=0).T
-    for side in range(CORES):
-        place = side * 2 * slots + slots
-        degree = jnp.maximum(columns[:owned, place : place + 1], 1).astype(jnp.float32)
-        scale[side * owned : (side + 1) * owned, :] = jnp.broadcast_to(degree, (owned, scale.shape[1]))
     lanes = lax.broadcasted_iota(jnp.int32, (owned, part), 1)
 
     def chunk(step, turn):
@@ -161,8 +146,7 @@
         if not isinstance(target, int):
             target = pl.multiple_of(target, 8)
         for side in range(CORES):
-            base = side * 2 * slots
-            wanted = [rows[:, base + s : base + s + 1] for s in range(slots)]
+            wanted = [rows[:, side * slots + s : side * slots + s + 1] for s in range(slots)]
             for block in range(edges):
                 nodes = lanes + from_peer(edge, block, edges) * part
                 total = jnp.zeros((owned, part), jnp.float32)
@@ -177,6 +161,45 @@
                 chunk(step, turn)
     else:
         lax.fori_loop(0, chips * CORES, lambda i, _: chunk(i // CORES, i % CORES), None)
+
+
+def prepare(turn, sizes, held, members, valid, degrees, members_other, valid_other, *weights):
+    chips, edges, owned, part = sizes
+    slots, shard = members.shape
+    shapes = [((shard, CORES * edges * part), jnp.bfloat16), ((8, 128), jnp.int32)]
+    shapes += [(w.shape, w.dtype) for w in weights]
+    outside, spec = pl.BlockSpec(memory_space=pltpu.HBM), pl.BlockSpec(memory_space=pltpu.VMEM)
+    given = [pltpu.with_memory_space_constraint(a, pltpu.HBM) for a in (members, valid, degrees)]
+    given += [pltpu.with_memory_space_constraint(a, pltpu.VMEM) for a in (members_other, valid_other)]
+    given += [pltpu.with_memory_space_constraint(a, pltpu.HBM) for a in weights]
+    specs = [outside] * 3 + [spec] * 2 + [outside] * len(weights)
+    aliases = {len(given) + i: i for i in range(len(held))}
+    given += [pltpu.with_memory_space_constraint(a, pltpu.VMEM) for a in held]
+    specs += [spec] * len(held)
+    return pl.pallas_call(
+        functools.partial(prepare_kernel, turn, chips, edges, owned, part, len(weights)),
+        out_shape=[pltpu.VMEM(shape, kind) for shape, kind in shapes],
+        in_specs=specs,
+        out_specs=[spec] * len(shapes),
+        scratch_shapes=[
+            pltpu.VMEM(members.shape, members.dtype),
+            pltpu.VMEM(valid.shape, valid.dtype),
+            pltpu.VMEM(degrees.shape, degrees.dtype),
+            pltpu.VMEM((shard, CORES * slots), jnp.int32),
+            pltpu.SemaphoreType.DMA((3 + len(weights),)),
+        ],
+        input_output_aliases=aliases,
+        compiler_params=pltpu.CompilerParams(vmem_limit_bytes=VMEM_LIMIT),
+    )(*given)
+
+
+def scale_kernel(degree, degree_other, scale):
+    core = lax.axis_index("node") % CORES
+    owned = scale.shape[0] // CORES
+    for here, ref in ((core, degree), (1 - core, degree_other)):
+        line = jnp.maximum(ref[:1, :], 1).astype(jnp.float32)
+        column = jnp.broadcast_to(line, (128, 128)).T
+        scale[pl.ds(pl.multiple_of(here * owned, 8), owned), :] = column[:owned, :]
 
 
 def blocks_sum(counts, place, blocks, used):
@@ -364,7 +387,7 @@
     half = width // CORES
     owned = degrees.shape[0]
     pair = owned * CORES
-    slots, shard = members.shape[1:]
+    _, shard = members.shape[1:]
     rows = width // edges
     piece = rows + 8
 
@@ -373,15 +396,12 @@
         fetch(node_feats), feats_other
     )
     blocks = [packed] + [send_edge(packed, step) for step in range(1, edges)]
-    code, w_query, w_key, w_value, w_out = preload(
-        members[0], incidence_mask[0], degrees[None], w_query, w_key, w_value, w_out
-    )
-    code_other = swap_cores(code)
-    counts, scale = vmem_call(
-        functools.partial(counts_kernel, chips, edges, owned, part, slots),
-        [((shard, CORES * edges * part), bf16), ((pair, 128), f32)],
-        [pltpu.VMEM((shard, CORES * 2 * slots), jnp.int32)],
-    )(code, code_other)
+    weights = (w_query, w_key, w_value, w_out)
+    sizes = (chips, edges, owned, part)
+    given = (members[0], incidence_mask[0], degrees[None])
+    given += (swap_cores(given[0]), swap_cores(given[1])) + weights
+    held = prepare(1 - SENDS_FIRST, sizes, (), *given)
+    counts, degree, w_query, w_key, w_value, w_out = prepare(SENDS_FIRST, sizes, held, *given)
     early, late = [0, edges - 1], list(range(1, edges - 1))
     (first,) = vmem_call(
         functools.partial(first_kernel, min(chips, 4) * pair, early), [((shard, half), f32)]
@@ -390,6 +410,7 @@
         functools.partial(aggregate_kernel, chips, late), [((pair, half), f32)] + [((pair, half), bf16)] * (chips - 1)
     )(counts, first, *[blocks[i] for i in late])
     arrived = [send_chip(partial[step], step) for step in range(1, chips)]
+    (scale,) = vmem_call(scale_kernel, [((pair, 128), f32)])(degree, swap_cores(degree))
     (hedge,) = vmem_call(hedge_kernel, [((pair, half), bf16)])(
         scale, partial[0], *arrived
     )

time: 53 us -> 53.5 us (level)
  Pallas kernels: 7.7 us -> 7.1 us
  waiting for transfers between devices: 23.8 us -> 24.4 us
    pallas_call x14, Pallas kernels: 4.33 us -> 2.89 us  [call(): pl.pallas_call(kernel, out_shape=[pltpu.VMEM(shape, dtype) for shape, dty...]
    ppermute x6, waiting for transfers between devices: 12.1 us -> 11 us  [send_chip(): lax.ppermute(value, 'node', [(i, to_peer(i // CORES, step, chips) * CORES...]
    ppermute x4 -> x6, waiting for transfers between devices: 3.51 us -> 4.54 us  [swap_cores(): return lax.ppermute(value, 'node', [(i, i ^ 1) for i in range(count)])]
    pallas_call x1 -> x2, Pallas kernels: 1.62 us -> 2.47 us  [prepare(): pl.pallas_call(functools.partial(prepare_kernel, turn, chips, edges, owne...]
    ppermute x9, waiting for transfers between devices: 8.18 us -> 8.89 us  [send_edge(): lax.ppermute(value, 'edge', [(i, to_peer(i, step, count)) for i in range(...]
    ppermute x4 -> x6, starting transfers between devices: 0.7 us -> 1.15 us  [swap_cores(): return lax.ppermute(value, 'node', [(i, i ^ 1) for i in range(count)])]
  transfers between devices with their start and end apart: 19 -> 21, of which waited for: 16 -> 16; matrix products, arithmetic and copies ran while one was open for 0% -> 0% of each run, Pallas kernels for 10% -> 9%
where the time goes in v2:
time: 53.5 us; the launch traced here: 53.3 us
  waiting for transfers between devices  24.4 us (46%)
  starting transfers between devices  21.7 us (41%)
  Pallas kernels  7.1 us (13%)
    ppermute x9, starting transfers between devices, send_edge(): lax.ppermute(value, 'edge', [(i, to_peer(i, step, count)) for i in range(...  11.6 us
    ppermute x6, waiting for transfers between devices, send_chip(): lax.ppermute(value, 'node', [(i, to_peer(i // CORES, step, chips) * CORES...  11 us
    ppermute x6, starting transfers between devices, send_chip(): lax.ppermute(value, 'node', [(i, to_peer(i // CORES, step, chips) * CORES...  8.9 us
    ppermute x9, waiting for transfers between devices, send_edge(): lax.ppermute(value, 'edge', [(i, to_peer(i, step, count)) for i in range(...  8.89 us
    ppermute x6, waiting for transfers between devices, swap_cores(): return lax.ppermute(value, 'node', [(i, i ^ 1) for i in range(count)])  4.54 us
    pallas_call x14, Pallas kernels, call(): pl.pallas_call(kernel, out_shape=[pltpu.VMEM(shape, dtype) for shape, dty...  2.89 us
    pallas_call x2, Pallas kernels, prepare(): pl.pallas_call(functools.partial(prepare_kernel, turn, chips, edges, owne...  2.47 us
    ppermute x6, starting transfers between devices, swap_cores(): return lax.ppermute(value, 'node', [(i, i ^ 1) for i in range(count)])  1.15 us
  transfers between devices with their start and end apart: 21, of which 16 were waited for; matrix products, arithmetic and copies ran while one was open for 0% of the time, Pallas kernels for 9%

profile of v2, /device:TPU:0, one launch (start us, length us, event | category | flops | bytes accessed | tf_op | source)
XLA Modules:
  0.0 53.3 jit_solution(3903144739089537144)
XLA Ops:
  0.0 0.5 collective-permute-start.3
  0.5 0.9 %fetch.1.own = bf16[128,512]{1,0:T(8,128)(2,1)S(1)} custom-call(bf16[128,512]{1,0:T(8,128)(2,1)} %source.1), custom_call_target="tpu_custom_call" | custom-call | tf_op jit(solution)/shard_map/fetch/pallas_call | solution.py:70
  1.4 0.3 collective-permute-done.3.other
  1.7 3.9 %collective-permute-start.4 = (bf16[256,256]{1,0:T(8,128)(2,1)S(1)}, bf16[256,256]{1,0:T(8,128)(2,1)S(1)}, u32[]{:S(2)}, u32[]{:S(2)}) collective-permute-start(bf16[256,256]{1,0:T(8,128)(2,1)S(1)} %shard_map.85.refs_0_), channel_id=1, source_target_pairs={{0,3},{1,2},{2,1},{3,0},{4,7},{5,6},{6,5},{7,4},{8,11},{9,10},{10,... | collective-permute-start | bytes 393224 | tf_op jit(solution)/shard_map/ppermute | solution.py:36
  5.6 0.5 %collective-permute-start.5 = (bf16[256,256]{1,0:T(8,128)(2,1)S(1)}, bf16[256,256]{1,0:T(8,128)(2,1)S(1)}, u32[]{:S(2)}, u32[]{:S(2)}) collective-permute-start(bf16[256,256]{1,0:T(8,128)(2,1)S(1)} %shard_map.85.refs_0_), channel_id=1, source_target_pairs={{0,1},{1,0},{2,3},{3,2},{4,5},{5,4},{6,7},{7,6},{8,9},{9,8},{10,11... | collective-permute-start | bytes 393224 | tf_op jit(solution)/shard_map/ppermute | solution.py:36
  6.1 0.1 collective-permute-start.6
  6.2 0.0 collective-permute-start
  6.2 0.5 collective-permute-start.1
  6.7 0.9 %collective-permute-done.refs_3_ = s32[4,768]{1,0:T(4,128)S(1)} collective-permute-done((s32[4,768]{1,0:T(4,128)}, s32[4,768]{1,0:T(4,128)S(1)}, u32[]{:S(2)}, u32[]{:S(2)}) %collective-permute-start) | collective-permute-done | bytes 12320 | tf_op jit(solution)/shard_map/ppermute | solution.py:31
  7.6 0.2 collective-permute-done.1.refs_4_
  7.8 2.4 %shard_map.82 = (bf16[768,1024]{1,0:T(8,128)(2,1)S(1)}, s32[8,128]{1,0:T(8,128)S(1)}, bf16[512,512]{1,0:T(8,128)(2,1)S(1)}, bf16[512,512]{1,0:T(8,128)(2,1)S(1)}...) custom-call(s32[4,768]{1,0:T(4,128)} %bitcast.4, s32[4,768]{1,0:T(4,128)} %bitcast.7, s32[1,96]{1,0:T(1,128)} %bitcast.9, ...), custom_call_target="tpu_custom_call" | custom-call | tf_op jit(solution)/shard_map/pallas_call | solution.py:179
  10.1 0.1 shard_map.83
  10.2 0.0 collective-permute-done.4.refs_1_
  10.3 0.4 shard_map.86.first
  10.6 1.8 %collective-permute-done.5.refs_0_ = bf16[256,256]{1,0:T(8,128)(2,1)S(1)} collective-permute-done((bf16[256,256]{1,0:T(8,128)(2,1)S(1)}, bf16[256,256]{1,0:T(8,128)(2,1)S(1)}, u32[]{:S(2)}, u32[]{:S(2)}) %collective-permute-start.5) | collective-permute-done | bytes 131104 | tf_op jit(solution)/shard_map/ppermute | solution.py:36
  12.4 0.0 collective-permute-done.6.refs_1_
  12.4 0.4 shard_map.87
  12.8 1.6 %collective-permute-start.7 = (bf16[192,256]{1,0:T(8,128)(2,1)S(1)}, bf16[192,256]{1,0:T(8,128)(2,1)S(1)}, u32[]{:S(2)}, u32[]{:S(2)}) collective-permute-start(bf16[192,256]{1,0:T(8,128)(2,1)S(1)} %get-tuple-element.44), channel_id=1, source_target_pairs={{0,8},{4,12},{8,0},{12,4},{16,24},{20,28},{24,16},{28,20},{1,9},{5... | collective-permute-start | bytes 294920 | tf_op jit(solution)/shard_map/ppermute | solution.py:41
  14.5 2.6 %collective-permute-start.8 = (bf16[192,256]{1,0:T(8,128)(2,1)S(1)}, bf16[192,256]{1,0:T(8,128)(2,1)S(1)}, u32[]{:S(2)}, u32[]{:S(2)}) collective-permute-start(bf16[192,256]{1,0:T(8,128)(2,1)S(1)} %get-tuple-element.45), channel_id=1, source_target_pairs={{0,16},{4,20},{8,24},{12,28},{16,0},{20,4},{24,8},{28,12},{1,17},{... | collective-permute-start | bytes 294920 | tf_op jit(solution)/shard_map/ppermute | solution.py:41
  17.0 0.2 collective-permute-start.9
  17.3 0.0 collective-permute-start.2
  17.3 1.2 %collective-permute-done.2.degree_other = s32[8,128]{1,0:T(8,128)S(1)} collective-permute-done((s32[8,128]{1,0:T(8,128)S(1)}, s32[8,128]{1,0:T(8,128)S(1)}, u32[]{:S(2)}, u32[]{:S(2)}) %collective-permute-start.2) | collective-permute-done | bytes 4128 | tf_op jit(solution)/shard_map/ppermute | solution.py:31
  18.4 0.1 shard_map.84.scale
  18.5 0.0 collective-permute-done.7.refs_0_
  18.6 6.1 %collective-permute-done.8.refs_1_ = bf16[192,256]{1,0:T(8,128)(2,1)S(1)} collective-permute-done((bf16[192,256]{1,0:T(8,128)(2,1)S(1)}, bf16[192,256]{1,0:T(8,128)(2,1)S(1)}, u32[]{:S(2)}, u32[]{:S(2)}) %collective-permute-start.8) | collective-permute-done | bytes 98336 | tf_op jit(solution)/shard_map/ppermute | solution.py:41
  24.6 0.0 collective-permute-done.9.refs_2_
  24.6 0.1 shard_map.88.hedge
  24.8 0.1 collective-permute-start.10
  24.8 0.3 shard_map.90
  25.1 1.0 %collective-permute-done.10.hedge_other = bf16[192,256]{1,0:T(8,128)(2,1)S(1)} collective-permute-done((bf16[192,256]{1,0:T(8,128)(2,1)S(1)}, bf16[192,256]{1,0:T(8,128)(2,1)S(1)}, u32[]{:S(2)}, u32[]{:S(2)}) %collective-permute-start.10) | collective-permute-done | bytes 98336 | tf_op jit(solution)/shard_map/ppermute | solution.py:31
  26.1 0.6 %shard_map.91 = (f32[136,256]{1,0:T(8,128)S(1)}, bf16[136,256]{1,0:T(8,128)(2,1)S(1)}, bf16[136,256]{1,0:T(8,128)(2,1)S(1)}, bf16[136,256]{1,0:T(8,128)(2,1)S(1)}) custom-call(bf16[192,256]{1,0:T(8,128)(2,1)S(1)} %collective-permute-done.10.hedge_other, f32[192,512]{1,0:T(8,128)S(1)} %get-tuple-element.52.key_part, ...), custom_call_target="tpu_custom_call" | custom-call | tf_op jit(solution)/shard_map/pallas_call | solution.py:51
  26.7 1.6 %collective-permute-start.11 = (bf16[136,256]{1,0:T(8,128)(2,1)S(1)}, bf16[136,256]{1,0:T(8,128)(2,1)S(1)}, u32[]{:S(2)}, u32[]{:S(2)}) collective-permute-start(bf16[136,256]{1,0:T(8,128)(2,1)S(1)} %get-tuple-element.55), channel_id=1, source_target_pairs={{0,1},{1,0},{2,3},{3,2},{4,5},{5,4},{6,7},{7,6},{8,9},{9,8},{10,11... | collective-permute-start | bytes 208904 | tf_op jit(solution)/shard_map/ppermute | solution.py:36
  28.3 1.9 %collective-permute-start.12 = (bf16[136,256]{1,0:T(8,128)(2,1)S(1)}, bf16[136,256]{1,0:T(8,128)(2,1)S(1)}, u32[]{:S(2)}, u32[]{:S(2)}) collective-permute-start(bf16[136,256]{1,0:T(8,128)(2,1)S(1)} %get-tuple-element.56), channel_id=1, source_target_pairs={{0,2},{1,3},{2,0},{3,1},{4,6},{5,7},{6,4},{7,5},{8,10},{9,11},{10,... | collective-permute-start | bytes 208904 | tf_op jit(solution)/shard_map/ppermute | solution.py:36
  30.2 0.1 collective-permute-start.13
  30.3 0.8 %collective-permute-done.11.refs_0_ = bf16[136,256]{1,0:T(8,128)(2,1)S(1)} collective-permute-done((bf16[136,256]{1,0:T(8,128)(2,1)S(1)}, bf16[136,256]{1,0:T(8,128)(2,1)S(1)}, u32[]{:S(2)}, u32[]{:S(2)}) %collective-permute-start.11) | collective-permute-done | bytes 69664 | tf_op jit(solution)/shard_map/ppermute | solution.py:36
  31.1 2.3 %collective-permute-done.12.refs_1_ = bf16[136,256]{1,0:T(8,128)(2,1)S(1)} collective-permute-done((bf16[136,256]{1,0:T(8,128)(2,1)S(1)}, bf16[136,256]{1,0:T(8,128)(2,1)S(1)}, u32[]{:S(2)}, u32[]{:S(2)}) %collective-permute-start.12) | collective-permute-done | bytes 69664 | tf_op jit(solution)/shard_map/ppermute | solution.py:36
  33.3 2.1 %collective-permute-done.13.refs_2_ = bf16[136,256]{1,0:T(8,128)(2,1)S(1)} collective-permute-done((bf16[136,256]{1,0:T(8,128)(2,1)S(1)}, bf16[136,256]{1,0:T(8,128)(2,1)S(1)}, u32[]{:S(2)}, u32[]{:S(2)}) %collective-permute-start.13) | collective-permute-done | bytes 69664 | tf_op jit(solution)/shard_map/ppermute | solution.py:36
  35.4 1.7 %collective-permute-start.14 = (bf16[136,256]{1,0:T(8,128)(2,1)S(1)}, bf16[136,256]{1,0:T(8,128)(2,1)S(1)}, u32[]{:S(2)}, u32[]{:S(2)}) collective-permute-start(bf16[136,256]{1,0:T(8,128)(2,1)S(1)} %get-tuple-element.59), channel_id=1, source_target_pairs={{0,8},{4,12},{8,0},{12,4},{16,24},{20,28},{24,16},{28,20},{1,9},{5... | collective-permute-start | bytes 208904 | tf_op jit(solution)/shard_map/ppermute | solution.py:41
  37.1 1.4 %collective-permute-start.15 = (bf16[136,256]{1,0:T(8,128)(2,1)S(1)}, bf16[136,256]{1,0:T(8,128)(2,1)S(1)}, u32[]{:S(2)}, u32[]{:S(2)}) collective-permute-start(bf16[136,256]{1,0:T(8,128)(2,1)S(1)} %get-tuple-element.59), channel_id=1, source_target_pairs={{0,16},{4,20},{8,24},{12,28},{16,0},{20,4},{24,8},{28,12},{1,17},{... | collective-permute-start | bytes 208904 | tf_op jit(solution)/shard_map/ppermute | solution.py:41
  38.6 1.3 %collective-permute-start.16 = (bf16[136,256]{1,0:T(8,128)(2,1)S(1)}, bf16[136,256]{1,0:T(8,128)(2,1)S(1)}, u32[]{:S(2)}, u32[]{:S(2)}) collective-permute-start(bf16[136,256]{1,0:T(8,128)(2,1)S(1)} %get-tuple-element.59), channel_id=1, source_target_pairs={{0,24},{4,28},{8,16},{12,20},{16,8},{20,12},{24,0},{28,4},{1,25},{... | collective-permute-start | bytes 208904 | tf_op jit(solution)/shard_map/ppermute | solution.py:41
  39.9 0.3 collective-permute-done.14.refs_0_
  40.2 3.1 %collective-permute-done.15.refs_1_ = bf16[136,256]{1,0:T(8,128)(2,1)S(1)} collective-permute-done((bf16[136,256]{1,0:T(8,128)(2,1)S(1)}, bf16[136,256]{1,0:T(8,128)(2,1)S(1)}, u32[]{:S(2)}, u32[]{:S(2)}) %collective-permute-start.15) | collective-permute-done | bytes 69664 | tf_op jit(solution)/shard_map/ppermute | solution.py:41
  43.3 1.5 %collective-permute-done.16.refs_2_ = bf16[136,256]{1,0:T(8,128)(2,1)S(1)} collective-permute-done((bf16[136,256]{1,0:T(8,128)(2,1)S(1)}, bf16[136,256]{1,0:T(8,128)(2,1)S(1)}, u32[]{:S(2)}, u32[]{:S(2)}) %collective-permute-start.16) | collective-permute-done | bytes 69664 | tf_op jit(solution)/shard_map/ppermute | solution.py:41
  44.8 0.4 collective-permute-start.17
  45.2 1.5 %collective-permute-start.18 = (bf16[128,256]{1,0:T(8,128)(2,1)S(1)}, bf16[128,256]{1,0:T(8,128)(2,1)S(1)}, u32[]{:S(2)}, u32[]{:S(2)}) collective-permute-start(bf16[128,256]{1,0:T(8,128)(2,1)S(1)} %get-tuple-element.61), channel_id=1, source_target_pairs={{0,1},{1,0},{2,3},{3,2},{4,5},{5,4},{6,7},{7,6},{8,9},{9,8},{10,11... | collective-permute-start | bytes 196616 | tf_op jit(solution)/shard_map/ppermute | solution.py:36
  46.7 1.7 %collective-permute-start.19 = (bf16[128,256]{1,0:T(8,128)(2,1)S(1)}, bf16[128,256]{1,0:T(8,128)(2,1)S(1)}, u32[]{:S(2)}, u32[]{:S(2)}) collective-permute-start(bf16[128,256]{1,0:T(8,128)(2,1)S(1)} %get-tuple-element.61), channel_id=1, source_target_pairs={{0,2},{1,3},{2,0},{3,1},{4,6},{5,7},{6,4},{7,5},{8,10},{9,11},{10,... | collective-permute-start | bytes 196616 | tf_op jit(solution)/shard_map/ppermute | solution.py:36
  48.4 0.3 shard_map.89
  48.7 0.1 shard_map.94.denom
  48.8 1.2 %collective-permute-done.17.refs_1_ = bf16[128,256]{1,0:T(8,128)(2,1)S(1)} collective-permute-done((bf16[128,256]{1,0:T(8,128)(2,1)S(1)}, bf16[128,256]{1,0:T(8,128)(2,1)S(1)}, u32[]{:S(2)}, u32[]{:S(2)}) %collective-permute-start.17) | collective-permute-done | bytes 65568 | tf_op jit(solution)/shard_map/ppermute | solution.py:36
  50.0 0.2 shard_map.95.numer
  50.2 0.0 collective-permute-done.18.refs_0_
  50.2 0.7 %collective-permute-done.19.refs_1_ = bf16[128,256]{1,0:T(8,128)(2,1)S(1)} collective-permute-done((bf16[128,256]{1,0:T(8,128)(2,1)S(1)}, bf16[128,256]{1,0:T(8,128)(2,1)S(1)}, u32[]{:S(2)}, u32[]{:S(2)}) %collective-permute-start.19) | collective-permute-done | bytes 65568 | tf_op jit(solution)/shard_map/ppermute | solution.py:36
  51.0 0.2 shard_map.96
  51.2 0.1 collective-permute-start.20
  51.3 0.2 shard_map.97.base
  51.5 1.0 %collective-permute-done.20.other = bf16[96,256]{1,0:T(8,128)(2,1)S(1)} collective-permute-done((bf16[96,256]{1,0:T(8,128)(2,1)S(1)}, bf16[96,256]{1,0:T(8,128)(2,1)S(1)}, u32[]{:S(2)}, u32[]{:S(2)}) %collective-permute-start.20) | collective-permute-done | bytes 49184 | tf_op jit(solution)/shard_map/ppermute | solution.py:31
  52.5 0.8 %output.1 = bf16[96,512]{1,0:T(8,128)(2,1)} custom-call(f32[96,512]{1,0:T(8,128)S(1)} %shard_map.97.base, bf16[96,256]{1,0:T(8,128)(2,1)S(1)} %collective-permute-done.20.other, bf16[512,512]{1,0:T(8,128)(2,1)S(1)} %get-tuple-element.63.w_out), custom_call_target="tpu_custom_call" | custom-call | tf_op jit(solution)/shard_map/output/pallas_call | solution.py:368
  (3 shorter events, 0.1 us)
Async XLA Ops:
  0.0 1.7 %collective-permute-start.3 = (bf16[128,512]{1,0:T(8,128)(2,1)}, bf16[128,512]{1,0:T(8,128)(2,1)S(1)}, u32[]{:S(2)}, u32[]{:S(2)}) collective-permute-start(bf16[128,512]{1,0:T(8,128)(2,1)} %source.1), channel_id=1, source_target_pairs={{0,4},{4,0},{8,12},{12,8},{16,20},{20,16},{24,28},{28,24},{1,5},{5... | collective-permute-start | bytes 393224 | tf_op jit(solution)/shard_map/ppermute | solution.py:31
  1.7 8.5 %collective-permute-start.4 = (bf16[256,256]{1,0:T(8,128)(2,1)S(1)}, bf16[256,256]{1,0:T(8,128)(2,1)S(1)}, u32[]{:S(2)}, u32[]{:S(2)}) collective-permute-start(bf16[256,256]{1,0:T(8,128)(2,1)S(1)} %shard_map.85.refs_0_), channel_id=1, source_target_pairs={{0,3},{1,2},{2,1},{3,0},{4,7},{5,6},{6,5},{7,4},{8,11},{9,10},{10,... | collective-permute-start | bytes 393224 | tf_op jit(solution)/shard_map/ppermute | solution.py:36
  5.6 6.9 %collective-permute-start.5 = (bf16[256,256]{1,0:T(8,128)(2,1)S(1)}, bf16[256,256]{1,0:T(8,128)(2,1)S(1)}, u32[]{:S(2)}, u32[]{:S(2)}) collective-permute-start(bf16[256,256]{1,0:T(8,128)(2,1)S(1)} %shard_map.85.refs_0_), channel_id=1, source_target_pairs={{0,1},{1,0},{2,3},{3,2},{4,5},{5,4},{6,7},{7,6},{8,9},{9,8},{10,11... | collective-permute-start | bytes 393224 | tf_op jit(solution)/shard_map/ppermute | solution.py:36
  6.1 6.3 %collective-permute-start.6 = (bf16[256,256]{1,0:T(8,128)(2,1)S(1)}, bf16[256,256]{1,0:T(8,128)(2,1)S(1)}, u32[]{:S(2)}, u32[]{:S(2)}) collective-permute-start(bf16[256,256]{1,0:T(8,128)(2,1)S(1)} %shard_map.85.refs_0_), channel_id=1, source_target_pairs={{0,2},{1,3},{2,0},{3,1},{4,6},{5,7},{6,4},{7,5},{8,10},{9,11},{10,... | collective-permute-start | bytes 393224 | tf_op jit(solution)/shard_map/ppermute | solution.py:36
  6.2 1.4 %collective-permute-start = (s32[4,768]{1,0:T(4,128)}, s32[4,768]{1,0:T(4,128)S(1)}, u32[]{:S(2)}, u32[]{:S(2)}) collective-permute-start(s32[4,768]{1,0:T(4,128)} %bitcast.3), channel_id=1, source_target_pairs={{0,4},{4,0},{8,12},{12,8},{16,20},{20,16},{24,28},{28,24},{1,5},{5... | collective-permute-start | bytes 36872 | tf_op jit(solution)/shard_map/ppermute | solution.py:31
  6.2 1.6 %collective-permute-start.1 = (s32[4,768]{1,0:T(4,128)}, s32[4,768]{1,0:T(4,128)S(1)}, u32[]{:S(2)}, u32[]{:S(2)}) collective-permute-start(s32[4,768]{1,0:T(4,128)} %bitcast.6), channel_id=1, source_target_pairs={{0,4},{4,0},{8,12},{12,8},{16,20},{20,16},{24,28},{28,24},{1,5},{5... | collective-permute-start | bytes 36872 | tf_op jit(solution)/shard_map/ppermute | solution.py:31
  12.8 5.7 %collective-permute-start.7 = (bf16[192,256]{1,0:T(8,128)(2,1)S(1)}, bf16[192,256]{1,0:T(8,128)(2,1)S(1)}, u32[]{:S(2)}, u32[]{:S(2)}) collective-permute-start(bf16[192,256]{1,0:T(8,128)(2,1)S(1)} %get-tuple-element.44), channel_id=1, source_target_pairs={{0,8},{4,12},{8,0},{12,4},{16,24},{20,28},{24,16},{28,20},{1,9},{5... | collective-permute-start | bytes 294920 | tf_op jit(solution)/shard_map/ppermute | solution.py:41
  14.5 10.2 %collective-permute-start.8 = (bf16[192,256]{1,0:T(8,128)(2,1)S(1)}, bf16[192,256]{1,0:T(8,128)(2,1)S(1)}, u32[]{:S(2)}, u32[]{:S(2)}) collective-permute-start(bf16[192,256]{1,0:T(8,128)(2,1)S(1)} %get-tuple-element.45), channel_id=1, source_target_pairs={{0,16},{4,20},{8,24},{12,28},{16,0},{20,4},{24,8},{28,12},{1,17},{... | collective-permute-start | bytes 294920 | tf_op jit(solution)/shard_map/ppermute | solution.py:41
  17.0 7.6 %collective-permute-start.9 = (bf16[192,256]{1,0:T(8,128)(2,1)S(1)}, bf16[192,256]{1,0:T(8,128)(2,1)S(1)}, u32[]{:S(2)}, u32[]{:S(2)}) collective-permute-start(bf16[192,256]{1,0:T(8,128)(2,1)S(1)} %get-tuple-element.46), channel_id=1, source_target_pairs={{0,24},{4,28},{8,16},{12,20},{16,8},{20,12},{24,0},{28,4},{1,25},{... | collective-permute-start | bytes 294920 | tf_op jit(solution)/shard_map/ppermute | solution.py:41
  17.3 1.2 %collective-permute-start.2 = (s32[8,128]{1,0:T(8,128)S(1)}, s32[8,128]{1,0:T(8,128)S(1)}, u32[]{:S(2)}, u32[]{:S(2)}) collective-permute-start(s32[8,128]{1,0:T(8,128)S(1)} %get-tuple-element.41.degree), channel_id=1, source_target_pairs={{0,4},{4,0},{8,12},{12,8},{16,20},{20,16},{24,28},{28,24},{1,5},{5... | collective-permute-start | bytes 12296 | tf_op jit(solution)/shard_map/ppermute | solution.py:31
  24.8 1.4 %collective-permute-start.10 = (bf16[192,256]{1,0:T(8,128)(2,1)S(1)}, bf16[192,256]{1,0:T(8,128)(2,1)S(1)}, u32[]{:S(2)}, u32[]{:S(2)}) collective-permute-start(bf16[192,256]{1,0:T(8,128)(2,1)S(1)} %shard_map.88.hedge), channel_id=1, source_target_pairs={{0,4},{4,0},{8,12},{12,8},{16,20},{20,16},{24,28},{28,24},{1,5},{5... | collective-permute-start | bytes 294920 | tf_op jit(solution)/shard_map/ppermute | solution.py:31
  26.7 4.4 %collective-permute-start.11 = (bf16[136,256]{1,0:T(8,128)(2,1)S(1)}, bf16[136,256]{1,0:T(8,128)(2,1)S(1)}, u32[]{:S(2)}, u32[]{:S(2)}) collective-permute-start(bf16[136,256]{1,0:T(8,128)(2,1)S(1)} %get-tuple-element.55), channel_id=1, source_target_pairs={{0,1},{1,0},{2,3},{3,2},{4,5},{5,4},{6,7},{7,6},{8,9},{9,8},{10,11... | collective-permute-start | bytes 208904 | tf_op jit(solution)/shard_map/ppermute | solution.py:36
  28.3 5.1 %collective-permute-start.12 = (bf16[136,256]{1,0:T(8,128)(2,1)S(1)}, bf16[136,256]{1,0:T(8,128)(2,1)S(1)}, u32[]{:S(2)}, u32[]{:S(2)}) collective-permute-start(bf16[136,256]{1,0:T(8,128)(2,1)S(1)} %get-tuple-element.56), channel_id=1, source_target_pairs={{0,2},{1,3},{2,0},{3,1},{4,6},{5,7},{6,4},{7,5},{8,10},{9,11},{10,... | collective-permute-start | bytes 208904 | tf_op jit(solution)/shard_map/ppermute | solution.py:36
  30.2 5.2 %collective-permute-start.13 = (bf16[136,256]{1,0:T(8,128)(2,1)S(1)}, bf16[136,256]{1,0:T(8,128)(2,1)S(1)}, u32[]{:S(2)}, u32[]{:S(2)}) collective-permute-start(bf16[136,256]{1,0:T(8,128)(2,1)S(1)} %get-tuple-element.57), channel_id=1, source_target_pairs={{0,3},{1,2},{2,1},{3,0},{4,7},{5,6},{6,5},{7,4},{8,11},{9,10},{10,... | collective-permute-start | bytes 208904 | tf_op jit(solution)/shard_map/ppermute | solution.py:36
  35.4 4.8 %collective-permute-start.14 = (bf16[136,256]{1,0:T(8,128)(2,1)S(1)}, bf16[136,256]{1,0:T(8,128)(2,1)S(1)}, u32[]{:S(2)}, u32[]{:S(2)}) collective-permute-start(bf16[136,256]{1,0:T(8,128)(2,1)S(1)} %get-tuple-element.59), channel_id=1, source_target_pairs={{0,8},{4,12},{8,0},{12,4},{16,24},{20,28},{24,16},{28,20},{1,9},{5... | collective-permute-start | bytes 208904 | tf_op jit(solution)/shard_map/ppermute | solution.py:41
  37.1 6.2 %collective-permute-start.15 = (bf16[136,256]{1,0:T(8,128)(2,1)S(1)}, bf16[136,256]{1,0:T(8,128)(2,1)S(1)}, u32[]{:S(2)}, u32[]{:S(2)}) collective-permute-start(bf16[136,256]{1,0:T(8,128)(2,1)S(1)} %get-tuple-element.59), channel_id=1, source_target_pairs={{0,16},{4,20},{8,24},{12,28},{16,0},{20,4},{24,8},{28,12},{1,17},{... | collective-permute-start | bytes 208904 | tf_op jit(solution)/shard_map/ppermute | solution.py:41
  38.6 6.2 %collective-permute-start.16 = (bf16[136,256]{1,0:T(8,128)(2,1)S(1)}, bf16[136,256]{1,0:T(8,128)(2,1)S(1)}, u32[]{:S(2)}, u32[]{:S(2)}) collective-permute-start(bf16[136,256]{1,0:T(8,128)(2,1)S(1)} %get-tuple-element.59), channel_id=1, source_target_pairs={{0,24},{4,28},{8,16},{12,20},{16,8},{20,12},{24,0},{28,4},{1,25},{... | collective-permute-start | bytes 208904 | tf_op jit(solution)/shard_map/ppermute | solution.py:41
  44.8 5.2 %collective-permute-start.17 = (bf16[128,256]{1,0:T(8,128)(2,1)S(1)}, bf16[128,256]{1,0:T(8,128)(2,1)S(1)}, u32[]{:S(2)}, u32[]{:S(2)}) collective-permute-start(bf16[128,256]{1,0:T(8,128)(2,1)S(1)} %get-tuple-element.61), channel_id=1, source_target_pairs={{0,3},{1,2},{2,1},{3,0},{4,7},{5,6},{6,5},{7,4},{8,11},{9,10},{10,... | collective-permute-start | bytes 196616 | tf_op jit(solution)/shard_map/ppermute | solution.py:36
  45.2 5.0 %collective-permute-start.18 = (bf16[128,256]{1,0:T(8,128)(2,1)S(1)}, bf16[128,256]{1,0:T(8,128)(2,1)S(1)}, u32[]{:S(2)}, u32[]{:S(2)}) collective-permute-start(bf16[128,256]{1,0:T(8,128)(2,1)S(1)} %get-tuple-element.61), channel_id=1, source_target_pairs={{0,1},{1,0},{2,3},{3,2},{4,5},{5,4},{6,7},{7,6},{8,9},{9,8},{10,11... | collective-permute-start | bytes 196616 | tf_op jit(solution)/shard_map/ppermute | solution.py:36
  46.7 4.3 %collective-permute-start.19 = (bf16[128,256]{1,0:T(8,128)(2,1)S(1)}, bf16[128,256]{1,0:T(8,128)(2,1)S(1)}, u32[]{:S(2)}, u32[]{:S(2)}) collective-permute-start(bf16[128,256]{1,0:T(8,128)(2,1)S(1)} %get-tuple-element.61), channel_id=1, source_target_pairs={{0,2},{1,3},{2,0},{3,1},{4,6},{5,7},{6,4},{7,5},{8,10},{9,11},{10,... | collective-permute-start | bytes 196616 | tf_op jit(solution)/shard_map/ppermute | solution.py:36
  51.2 1.3 %collective-permute-start.20 = (bf16[96,256]{1,0:T(8,128)(2,1)S(1)}, bf16[96,256]{1,0:T(8,128)(2,1)S(1)}, u32[]{:S(2)}, u32[]{:S(2)}) collective-permute-start(bf16[96,256]{1,0:T(8,128)(2,1)S(1)} %get-tuple-element.64), channel_id=1, source_target_pairs={{0,4},{4,0},{8,12},{12,8},{16,20},{20,16},{24,28},{28,24},{1,5},{5... | collective-permute-start | bytes 147464 | tf_op jit(solution)/shard_map/ppermute | solution.py:31

commit v3 on v2

--- a/solution.py
+++ b/solution.py
@@ -240,23 +240,30 @@
     out[...] = (total / scale[:, :1]).astype(out.dtype)
 
 
-def project_kernel(hedge, w_key, w_value, key_part, value_part):
+def fold_kernel(w_value, w_out, folded):
+    mine, _ = half_place(folded.shape[1])
+    folded[...] = jnp.dot(w_value[...], w_out[:, mine], preferred_element_type=jnp.float32).astype(
+        folded.dtype
+    )
+
+
+def project_kernel(hedge, w_key, folded, key_part, value_part):
     mine, _ = half_place(hedge.shape[1])
     key_part[...] = jnp.dot(hedge[...], w_key[mine, :], preferred_element_type=jnp.float32)
-    value_part[...] = jnp.dot(hedge[...], w_value[mine, mine], preferred_element_type=jnp.float32)
-
-
-def gram_kernel(edges, hedge_other, key_part, value_part, w_key, w_value, *refs):
+    value_part[...] = jnp.dot(hedge[...], folded[mine, :], preferred_element_type=jnp.float32)
+
+
+def gram_kernel(edges, hedge_other, key_part, value_part, w_key, folded, *refs):
     outs, gram = refs[:edges], refs[edges]
     edge = lax.axis_index("edge")
     width = w_key.shape[0]
     half = width // CORES
     rows = width // edges
-    mine, other = half_place(half)
+    _, other = half_place(half)
     both = hedge_other[...]
     keys = key_part[...] + jnp.dot(both, w_key[other, :], preferred_element_type=jnp.float32)
     keys = feature_map(keys).astype(jnp.bfloat16)
-    values = value_part[...] + jnp.dot(both, w_value[other, mine], preferred_element_type=jnp.float32)
+    values = value_part[...] + jnp.dot(both, folded[other, :], preferred_element_type=jnp.float32)
     gram[...] = lax.dot_general(
         keys, values.astype(jnp.bfloat16), (((0,), (0,)), ((), ())), preferred_element_type=jnp.float32
     )
@@ -269,13 +276,11 @@
         outs[step][rows:, :] = tail.astype(outs[step].dtype)
 
 
-def query_kernel(hedge, hedge_other, w_query, out, full):
+def query_kernel(hedge, hedge_other, w_query, out):
     mine, other = half_place(hedge.shape[1])
-    full[:, mine] = hedge[...]
-    full[:, other] = hedge_other[...]
-    out[...] = feature_map(
-        jnp.dot(full[...], w_query[...], preferred_element_type=jnp.float32)
-    ).astype(out.dtype)
+    total = jnp.dot(hedge[...], w_query[mine, :], preferred_element_type=jnp.float32)
+    total = total + jnp.dot(hedge_other[...], w_query[other, :], preferred_element_type=jnp.float32)
+    out[...] = feature_map(total).astype(out.dtype)
 
 
 def add_kernel(own, *refs, count):
@@ -313,70 +318,51 @@
     refs[-1][...] = numer_sum(edges, query, refs[:-1], used)
 
 
-def attend_kernel(edges, used, query, denom, numer, *refs):
-    pieces, (mine, other, attended) = refs[: len(used)], refs[len(used) :]
+def attend_kernel(edges, used, hedge, query, denom, numer, *refs):
+    pieces, (mine, other, mixed) = refs[: len(used)], refs[len(used) :]
     total = numer[...] + numer_sum(edges, query, pieces, used)
-    attended[...] = (total / denom[:, :1]).astype(attended.dtype)
-    split_rows(attended, mine, other)
-
-
-def gather_kernel(edges, query, denom, *refs):
-    pieces, (mine, other, attended, gram) = refs[:edges], refs[edges:]
+    mix_rows(hedge, total / denom[:, :1], mixed, mine, other)
+
+
+def gather_kernel(edges, hedge, query, denom, *refs):
+    pieces, (mine, other, mixed, gram) = refs[:edges], refs[edges:]
     edge = lax.axis_index("edge")
     rows = query.shape[1] // edges
     for step in range(edges):
         first = pl.multiple_of(from_peer(edge, step, edges) * rows, rows)
         gram[pl.ds(first, rows), :] = pieces[step][:rows, :]
     numer = jnp.dot(query[...], gram[...], preferred_element_type=jnp.float32)
-    attended[...] = (numer / denom[:, :1]).astype(attended.dtype)
-    split_rows(attended, mine, other)
-
-
-def split_rows(attended, mine, other):
+    mix_rows(hedge, numer / denom[:, :1], mixed, mine, other)
+
+
+def mix_rows(hedge, attended, mixed, mine, other):
+    mixed[...] = (hedge[...].astype(jnp.float32) + attended).astype(mixed.dtype)
     here, there = half_place(mine.shape[0])
-    mine[...] = attended[here, :]
-    other[...] = attended[there, :]
-
-
-def base_kernel(full, mine, w_out, out):
-    here, _ = half_place(mine.shape[0])
-    rows, _ = half_place(mine.shape[1])
-    out[...] = full[here, :].astype(jnp.float32) + jnp.dot(
-        mine[...], w_out[rows, :], preferred_element_type=jnp.float32
-    )
-
-
-def output_kernel(base, other, w_out, out, result, sems):
-    _, rows = half_place(other.shape[1])
-    half = other.shape[1]
-    moves = []
-    for side in range(CORES):
-        place = pl.ds(side * half, half)
-        mixed = base[:, place] + jnp.dot(
-            other[...], w_out[rows, place], preferred_element_type=jnp.float32
-        )
-        result[:, place] = mixed.astype(result.dtype)
-        moves.append(pltpu.make_async_copy(result.at[:, place], out.at[:, place], sems.at[side]))
-        moves[-1].start()
-    for move in moves:
-        move.wait()
-
-
-def write_output(base, other, w_out):
-    args = (base, other, w_out)
-    spec = pl.BlockSpec(memory_space=pltpu.VMEM)
+    mine[...] = mixed[here, :]
+    other[...] = mixed[there, :]
+
+
+def store_kernel(side, value, *refs):
+    out, sem = refs[-2:]
+    move = pltpu.make_async_copy(value, out.at[:, half_place(value.shape[1])[side]], sem)
+    move.start()
+    move.wait()
+
+
+def store(side, value, *held):
+    outside = pl.BlockSpec(memory_space=pltpu.HBM)
     return pl.pallas_call(
-        output_kernel,
-        out_shape=pltpu.HBM(base.shape, other.dtype),
-        in_specs=[spec] * len(args),
-        out_specs=pl.BlockSpec(memory_space=pltpu.HBM),
-        scratch_shapes=[
-            pltpu.VMEM(base.shape, other.dtype),
-            pltpu.SemaphoreType.DMA((CORES,)),
-        ],
+        functools.partial(store_kernel, side),
+        out_shape=pltpu.HBM((value.shape[0], CORES * value.shape[1]), value.dtype),
+        in_specs=[pl.BlockSpec(memory_space=pltpu.VMEM)] + [outside] * len(held),
+        out_specs=outside,
+        scratch_shapes=[pltpu.SemaphoreType.DMA],
+        input_output_aliases={1 + i: i for i in range(len(held))},
         compiler_params=pltpu.CompilerParams(vmem_limit_bytes=VMEM_LIMIT),
-        name="output",
-    )(*[pltpu.with_memory_space_constraint(a, pltpu.VMEM) for a in args])
+    )(
+        pltpu.with_memory_space_constraint(value, pltpu.VMEM),
+        *[pltpu.with_memory_space_constraint(a, pltpu.HBM) for a in held],
+    )
 
 
 def body(node_feats, members, incidence_mask, degrees, w_query, w_key, w_value, w_out):
@@ -402,7 +388,7 @@
     given += (swap_cores(given[0]), swap_cores(given[1])) + weights
     held = prepare(1 - SENDS_FIRST, sizes, (), *given)
     counts, degree, w_query, w_key, w_value, w_out = prepare(SENDS_FIRST, sizes, held, *given)
-    early, late = [0, edges - 1], list(range(1, edges - 1))
+    early, late = [0, edges - 1] + list(range(1, edges - 2)), [edges - 2]
     (first,) = vmem_call(
         functools.partial(first_kernel, min(chips, 4) * pair, early), [((shard, half), f32)]
     )(counts, *[blocks[i] for i in early])
@@ -415,15 +401,18 @@
         scale, partial[0], *arrived
     )
 
+    (folded,) = vmem_call(fold_kernel, [((width, half), bf16)])(w_value, w_out)
     hedge_other = swap_cores(hedge)
-    parts = vmem_call(project_kernel, [((pair, width), f32), ((pair, half), f32)])(hedge, w_key, w_value)
+    parts = vmem_call(project_kernel, [((pair, width), f32), ((pair, half), f32)])(
+        hedge, w_key, folded
+    )
     grams = vmem_call(
         functools.partial(gram_kernel, edges),
         [((piece, half), f32)] + [((piece, half), bf16)] * (edges - 1),
         [pltpu.VMEM((width, half), f32)],
-    )(hedge_other, *parts, w_key, w_value)
+    )(hedge_other, *parts, w_key, folded)
     arrived = [send_edge(grams[step], step) for step in range(1, edges)]
-    query, full = vmem_call(query_kernel, [((pair, width), bf16)] * 2)(
+    (query,) = vmem_call(query_kernel, [((pair, width), bf16)])(
         hedge, hedge_other, w_query
     )
     plane, plane16 = vmem_call(
@@ -442,14 +431,13 @@
         )(query, *[pieces[i] for i in early])
         mine, other = vmem_call(
             functools.partial(attend_kernel, edges, late), halves, [held]
-        )(query, denom, numer, *[pieces[i] for i in late])
+        )(hedge, query, denom, numer, *[pieces[i] for i in late])
     else:
         mine, other = vmem_call(
             functools.partial(gather_kernel, edges), halves, [held, pltpu.VMEM((width, half), bf16)]
-        )(query, denom, *pieces)
+        )(hedge, query, denom, *pieces)
     arrived = swap_cores(other)
-    (base,) = vmem_call(base_kernel, [((owned, width), f32)])(full, mine, w_out)
-    return write_output(base, arrived, w_out)
+    return store(1, arrived, store(0, mine))
 
 
 def solution(mesh):

time: 53.5 us -> 53.2 us (level)
  waiting for transfers between devices: 24.4 us -> 23.5 us
  Pallas kernels: 7.1 us -> 7.66 us
    ppermute x6, waiting for transfers between devices: 4.54 us -> 3.76 us  [swap_cores(): return lax.ppermute(value, 'node', [(i, i ^ 1) for i in range(count)])]
    pallas_call x1 -> x2, Pallas kernels: 0.83 us -> 1.27 us  [store(): pl.pallas_call(functools.partial(store_kernel, side), out_shape=pltpu.HBM...]
  transfers between devices with their start and end apart: 21 -> 21, of which waited for: 16 -> 16; matrix products, arithmetic and copies ran while one was open for 0% -> 0% of each run, Pallas kernels for 9% -> 11%
where the time goes in v3:
time: 53.2 us; the launch traced here: 53 us
  waiting for transfers between devices  23.5 us (44%)
  starting transfers between devices  21.7 us (41%)
  Pallas kernels  7.66 us (14%)
    ppermute x9, starting transfers between devices, send_edge(): lax.ppermute(value, 'edge', [(i, to_peer(i, step, count)) for i in range(...  11.6 us
    ppermute x6, waiting for transfers between devices, send_chip(): lax.ppermute(value, 'node', [(i, to_peer(i // CORES, step, chips) * CORES...  10.7 us
    ppermute x9, waiting for transfers between devices, send_edge(): lax.ppermute(value, 'edge', [(i, to_peer(i, step, count)) for i in range(...  9.06 us
    ppermute x6, starting transfers between devices, send_chip(): lax.ppermute(value, 'node', [(i, to_peer(i // CORES, step, chips) * CORES...  8.9 us
    ppermute x6, waiting for transfers between devices, swap_cores(): return lax.ppermute(value, 'node', [(i, i ^ 1) for i in range(count)])  3.76 us
    pallas_call x14, Pallas kernels, call(): pl.pallas_call(kernel, out_shape=[pltpu.VMEM(shape, dtype) for shape, dty...  3 us
    pallas_call x2, Pallas kernels, prepare(): pl.pallas_call(functools.partial(prepare_kernel, turn, chips, edges, owne...  2.47 us
    pallas_call x2, Pallas kernels, store(): pl.pallas_call(functools.partial(store_kernel, side), out_shape=pltpu.HBM...  1.27 us
  transfers between devices with their start and end apart: 21, of which 16 were waited for; matrix products, arithmetic and copies ran while one was open for 0% of the time, Pallas kernels for 11%

profile of v3, /device:TPU:0, one launch (start us, length us, event | category | flops | bytes accessed | tf_op | source)
XLA Modules:
  0.0 53.0 jit_solution(16998459955093535036)
XLA Ops:
  0.0 0.5 collective-permute-start.3
  0.5 0.9 %fetch.1.own = bf16[128,512]{1,0:T(8,128)(2,1)S(1)} custom-call(bf16[128,512]{1,0:T(8,128)(2,1)} %source.1), custom_call_target="tpu_custom_call" | custom-call | tf_op jit(solution)/shard_map/fetch/pallas_call | solution.py:70
  1.4 0.3 collective-permute-done.3.other
  1.7 3.9 %collective-permute-start.4 = (bf16[256,256]{1,0:T(8,128)(2,1)S(1)}, bf16[256,256]{1,0:T(8,128)(2,1)S(1)}, u32[]{:S(2)}, u32[]{:S(2)}) collective-permute-start(bf16[256,256]{1,0:T(8,128)(2,1)S(1)} %shard_map.85.refs_0_), channel_id=1, source_target_pairs={{0,3},{1,2},{2,1},{3,0},{4,7},{5,6},{6,5},{7,4},{8,11},{9,10},{10,... | collective-permute-start | bytes 393224 | tf_op jit(solution)/shard_map/ppermute | solution.py:36
  5.6 0.5 %collective-permute-start.5 = (bf16[256,256]{1,0:T(8,128)(2,1)S(1)}, bf16[256,256]{1,0:T(8,128)(2,1)S(1)}, u32[]{:S(2)}, u32[]{:S(2)}) collective-permute-start(bf16[256,256]{1,0:T(8,128)(2,1)S(1)} %shard_map.85.refs_0_), channel_id=1, source_target_pairs={{0,1},{1,0},{2,3},{3,2},{4,5},{5,4},{6,7},{7,6},{8,9},{9,8},{10,11... | collective-permute-start | bytes 393224 | tf_op jit(solution)/shard_map/ppermute | solution.py:36
  6.1 0.1 collective-permute-start.6
  6.2 0.0 collective-permute-start
  6.2 0.5 collective-permute-start.1
  6.7 0.9 %collective-permute-done.refs_3_ = s32[4,768]{1,0:T(4,128)S(1)} collective-permute-done((s32[4,768]{1,0:T(4,128)}, s32[4,768]{1,0:T(4,128)S(1)}, u32[]{:S(2)}, u32[]{:S(2)}) %collective-permute-start) | collective-permute-done | bytes 12320 | tf_op jit(solution)/shard_map/ppermute | solution.py:31
  7.6 0.2 collective-permute-done.1.refs_4_
  7.8 2.4 %shard_map.82 = (bf16[768,1024]{1,0:T(8,128)(2,1)S(1)}, s32[8,128]{1,0:T(8,128)S(1)}, bf16[512,512]{1,0:T(8,128)(2,1)S(1)}, bf16[512,512]{1,0:T(8,128)(2,1)S(1)}...) custom-call(s32[4,768]{1,0:T(4,128)} %bitcast.4, s32[4,768]{1,0:T(4,128)} %bitcast.7, s32[1,96]{1,0:T(1,128)} %bitcast.9, ...), custom_call_target="tpu_custom_call" | custom-call | tf_op jit(solution)/shard_map/pallas_call | solution.py:179
  10.1 0.1 shard_map.83
  10.2 0.0 collective-permute-done.4.refs_1_
  10.3 2.2 %collective-permute-done.5.refs_2_ = bf16[256,256]{1,0:T(8,128)(2,1)S(1)} collective-permute-done((bf16[256,256]{1,0:T(8,128)(2,1)S(1)}, bf16[256,256]{1,0:T(8,128)(2,1)S(1)}, u32[]{:S(2)}, u32[]{:S(2)}) %collective-permute-start.5) | collective-permute-done | bytes 131104 | tf_op jit(solution)/shard_map/ppermute | solution.py:36
  12.4 0.5 shard_map.86.first
  12.9 0.0 collective-permute-done.6.refs_0_
  12.9 0.3 shard_map.87
  13.2 1.6 %collective-permute-start.7 = (bf16[192,256]{1,0:T(8,128)(2,1)S(1)}, bf16[192,256]{1,0:T(8,128)(2,1)S(1)}, u32[]{:S(2)}, u32[]{:S(2)}) collective-permute-start(bf16[192,256]{1,0:T(8,128)(2,1)S(1)} %get-tuple-element.42), channel_id=1, source_target_pairs={{0,8},{4,12},{8,0},{12,4},{16,24},{20,28},{24,16},{28,20},{1,9},{5... | collective-permute-start | bytes 294920 | tf_op jit(solution)/shard_map/ppermute | solution.py:41
  14.8 2.6 %collective-permute-start.8 = (bf16[192,256]{1,0:T(8,128)(2,1)S(1)}, bf16[192,256]{1,0:T(8,128)(2,1)S(1)}, u32[]{:S(2)}, u32[]{:S(2)}) collective-permute-start(bf16[192,256]{1,0:T(8,128)(2,1)S(1)} %get-tuple-element.43), channel_id=1, source_target_pairs={{0,16},{4,20},{8,24},{12,28},{16,0},{20,4},{24,8},{28,12},{1,17},{... | collective-permute-start | bytes 294920 | tf_op jit(solution)/shard_map/ppermute | solution.py:41
  17.4 0.2 collective-permute-start.9
  17.7 0.0 collective-permute-start.2
  17.7 1.2 %collective-permute-done.2.degree_other = s32[8,128]{1,0:T(8,128)S(1)} collective-permute-done((s32[8,128]{1,0:T(8,128)S(1)}, s32[8,128]{1,0:T(8,128)S(1)}, u32[]{:S(2)}, u32[]{:S(2)}) %collective-permute-start.2) | collective-permute-done | bytes 4128 | tf_op jit(solution)/shard_map/ppermute | solution.py:31
  18.8 0.1 shard_map.84.scale
  18.9 0.0 collective-permute-done.7.refs_0_
  18.9 5.8 %collective-permute-done.8.refs_1_ = bf16[192,256]{1,0:T(8,128)(2,1)S(1)} collective-permute-done((bf16[192,256]{1,0:T(8,128)(2,1)S(1)}, bf16[192,256]{1,0:T(8,128)(2,1)S(1)}, u32[]{:S(2)}, u32[]{:S(2)}) %collective-permute-start.8) | collective-permute-done | bytes 98336 | tf_op jit(solution)/shard_map/ppermute | solution.py:41
  24.7 0.0 collective-permute-done.9.refs_2_
  24.7 0.1 shard_map.88.hedge
  24.8 0.1 collective-permute-start.10
  24.9 0.3 shard_map.90.folded
  25.2 0.3 shard_map.91
  25.5 0.7 %collective-permute-done.10.hedge_other = bf16[192,256]{1,0:T(8,128)(2,1)S(1)} collective-permute-done((bf16[192,256]{1,0:T(8,128)(2,1)S(1)}, bf16[192,256]{1,0:T(8,128)(2,1)S(1)}, u32[]{:S(2)}, u32[]{:S(2)}) %collective-permute-start.10) | collective-permute-done | bytes 98336 | tf_op jit(solution)/shard_map/ppermute | solution.py:31
  26.2 0.6 %shard_map.92 = (f32[136,256]{1,0:T(8,128)S(1)}, bf16[136,256]{1,0:T(8,128)(2,1)S(1)}, bf16[136,256]{1,0:T(8,128)(2,1)S(1)}, bf16[136,256]{1,0:T(8,128)(2,1)S(1)}) custom-call(bf16[192,256]{1,0:T(8,128)(2,1)S(1)} %collective-permute-done.10.hedge_other, f32[192,512]{1,0:T(8,128)S(1)} %get-tuple-element.49.key_part, ...), custom_call_target="tpu_custom_call" | custom-call | tf_op jit(solution)/shard_map/pallas_call | solution.py:51
  26.8 1.6 %collective-permute-start.11 = (bf16[136,256]{1,0:T(8,128)(2,1)S(1)}, bf16[136,256]{1,0:T(8,128)(2,1)S(1)}, u32[]{:S(2)}, u32[]{:S(2)}) collective-permute-start(bf16[136,256]{1,0:T(8,128)(2,1)S(1)} %get-tuple-element.52), channel_id=1, source_target_pairs={{0,1},{1,0},{2,3},{3,2},{4,5},{5,4},{6,7},{7,6},{8,9},{9,8},{10,11... | collective-permute-start | bytes 208904 | tf_op jit(solution)/shard_map/ppermute | solution.py:36
  28.3 1.7 %collective-permute-start.12 = (bf16[136,256]{1,0:T(8,128)(2,1)S(1)}, bf16[136,256]{1,0:T(8,128)(2,1)S(1)}, u32[]{:S(2)}, u32[]{:S(2)}) collective-permute-start(bf16[136,256]{1,0:T(8,128)(2,1)S(1)} %get-tuple-element.53), channel_id=1, source_target_pairs={{0,2},{1,3},{2,0},{3,1},{4,6},{5,7},{6,4},{7,5},{8,10},{9,11},{10,... | collective-permute-start | bytes 208904 | tf_op jit(solution)/shard_map/ppermute | solution.py:36
  30.1 0.3 collective-permute-start.13
  30.3 0.8 %collective-permute-done.11.refs_0_ = bf16[136,256]{1,0:T(8,128)(2,1)S(1)} collective-permute-done((bf16[136,256]{1,0:T(8,128)(2,1)S(1)}, bf16[136,256]{1,0:T(8,128)(2,1)S(1)}, u32[]{:S(2)}, u32[]{:S(2)}) %collective-permute-start.11) | collective-permute-done | bytes 69664 | tf_op jit(solution)/shard_map/ppermute | solution.py:36
  31.1 1.5 %collective-permute-done.12.refs_1_ = bf16[136,256]{1,0:T(8,128)(2,1)S(1)} collective-permute-done((bf16[136,256]{1,0:T(8,128)(2,1)S(1)}, bf16[136,256]{1,0:T(8,128)(2,1)S(1)}, u32[]{:S(2)}, u32[]{:S(2)}) %collective-permute-start.12) | collective-permute-done | bytes 69664 | tf_op jit(solution)/shard_map/ppermute | solution.py:36
  32.6 2.6 %collective-permute-done.13.refs_2_ = bf16[136,256]{1,0:T(8,128)(2,1)S(1)} collective-permute-done((bf16[136,256]{1,0:T(8,128)(2,1)S(1)}, bf16[136,256]{1,0:T(8,128)(2,1)S(1)}, u32[]{:S(2)}, u32[]{:S(2)}) %collective-permute-start.13) | collective-permute-done | bytes 69664 | tf_op jit(solution)/shard_map/ppermute | solution.py:36
  35.3 1.7 %collective-permute-start.14 = (bf16[136,256]{1,0:T(8,128)(2,1)S(1)}, bf16[136,256]{1,0:T(8,128)(2,1)S(1)}, u32[]{:S(2)}, u32[]{:S(2)}) collective-permute-start(bf16[136,256]{1,0:T(8,128)(2,1)S(1)} %get-tuple-element.56), channel_id=1, source_target_pairs={{0,8},{4,12},{8,0},{12,4},{16,24},{20,28},{24,16},{28,20},{1,9},{5... | collective-permute-start | bytes 208904 | tf_op jit(solution)/shard_map/ppermute | solution.py:41
  37.0 1.4 %collective-permute-start.15 = (bf16[136,256]{1,0:T(8,128)(2,1)S(1)}, bf16[136,256]{1,0:T(8,128)(2,1)S(1)}, u32[]{:S(2)}, u32[]{:S(2)}) collective-permute-start(bf16[136,256]{1,0:T(8,128)(2,1)S(1)} %get-tuple-element.56), channel_id=1, source_target_pairs={{0,16},{4,20},{8,24},{12,28},{16,0},{20,4},{24,8},{28,12},{1,17},{... | collective-permute-start | bytes 208904 | tf_op jit(solution)/shard_map/ppermute | solution.py:41
  38.4 1.3 %collective-permute-start.16 = (bf16[136,256]{1,0:T(8,128)(2,1)S(1)}, bf16[136,256]{1,0:T(8,128)(2,1)S(1)}, u32[]{:S(2)}, u32[]{:S(2)}) collective-permute-start(bf16[136,256]{1,0:T(8,128)(2,1)S(1)} %get-tuple-element.56), channel_id=1, source_target_pairs={{0,24},{4,28},{8,16},{12,20},{16,8},{20,12},{24,0},{28,4},{1,25},{... | collective-permute-start | bytes 208904 | tf_op jit(solution)/shard_map/ppermute | solution.py:41
  39.8 0.3 collective-permute-done.14.refs_0_
  40.1 3.1 %collective-permute-done.15.refs_1_ = bf16[136,256]{1,0:T(8,128)(2,1)S(1)} collective-permute-done((bf16[136,256]{1,0:T(8,128)(2,1)S(1)}, bf16[136,256]{1,0:T(8,128)(2,1)S(1)}, u32[]{:S(2)}, u32[]{:S(2)}) %collective-permute-start.15) | collective-permute-done | bytes 69664 | tf_op jit(solution)/shard_map/ppermute | solution.py:41
  43.2 1.5 %collective-permute-done.16.refs_2_ = bf16[136,256]{1,0:T(8,128)(2,1)S(1)} collective-permute-done((bf16[136,256]{1,0:T(8,128)(2,1)S(1)}, bf16[136,256]{1,0:T(8,128)(2,1)S(1)}, u32[]{:S(2)}, u32[]{:S(2)}) %collective-permute-start.16) | collective-permute-done | bytes 69664 | tf_op jit(solution)/shard_map/ppermute | solution.py:41
  44.7 0.5 %collective-permute-start.17 = (bf16[128,256]{1,0:T(8,128)(2,1)S(1)}, bf16[128,256]{1,0:T(8,128)(2,1)S(1)}, u32[]{:S(2)}, u32[]{:S(2)}) collective-permute-start(bf16[128,256]{1,0:T(8,128)(2,1)S(1)} %get-tuple-element.58), channel_id=1, source_target_pairs={{0,3},{1,2},{2,1},{3,0},{4,7},{5,6},{6,5},{7,4},{8,11},{9,10},{10,... | collective-permute-start | bytes 196616 | tf_op jit(solution)/shard_map/ppermute | solution.py:36
  45.2 1.3 %collective-permute-start.18 = (bf16[128,256]{1,0:T(8,128)(2,1)S(1)}, bf16[128,256]{1,0:T(8,128)(2,1)S(1)}, u32[]{:S(2)}, u32[]{:S(2)}) collective-permute-start(bf16[128,256]{1,0:T(8,128)(2,1)S(1)} %get-tuple-element.58), channel_id=1, source_target_pairs={{0,1},{1,0},{2,3},{3,2},{4,5},{5,4},{6,7},{7,6},{8,9},{9,8},{10,11... | collective-permute-start | bytes 196616 | tf_op jit(solution)/shard_map/ppermute | solution.py:36
  46.6 1.7 %collective-permute-start.19 = (bf16[128,256]{1,0:T(8,128)(2,1)S(1)}, bf16[128,256]{1,0:T(8,128)(2,1)S(1)}, u32[]{:S(2)}, u32[]{:S(2)}) collective-permute-start(bf16[128,256]{1,0:T(8,128)(2,1)S(1)} %get-tuple-element.58), channel_id=1, source_target_pairs={{0,2},{1,3},{2,0},{3,1},{4,6},{5,7},{6,4},{7,5},{8,10},{9,11},{10,... | collective-permute-start | bytes 196616 | tf_op jit(solution)/shard_map/ppermute | solution.py:36
  48.3 0.3 shard_map.89.query
  48.6 0.1 shard_map.95.denom
  48.7 1.2 %collective-permute-done.17.refs_1_ = bf16[128,256]{1,0:T(8,128)(2,1)S(1)} collective-permute-done((bf16[128,256]{1,0:T(8,128)(2,1)S(1)}, bf16[128,256]{1,0:T(8,128)(2,1)S(1)}, u32[]{:S(2)}, u32[]{:S(2)}) %collective-permute-start.17) | collective-permute-done | bytes 65568 | tf_op jit(solution)/shard_map/ppermute | solution.py:36
  49.9 0.0 collective-permute-done.18.refs_2_
  49.9 0.2 shard_map.96.numer
  50.2 0.7 %collective-permute-done.19.refs_0_ = bf16[128,256]{1,0:T(8,128)(2,1)S(1)} collective-permute-done((bf16[128,256]{1,0:T(8,128)(2,1)S(1)}, bf16[128,256]{1,0:T(8,128)(2,1)S(1)}, u32[]{:S(2)}, u32[]{:S(2)}) %collective-permute-start.19) | collective-permute-done | bytes 65568 | tf_op jit(solution)/shard_map/ppermute | solution.py:36
  50.9 0.2 shard_map.97
  51.1 0.1 collective-permute-start.20
  51.1 0.6 %shard_map.98.refs_0_ = bf16[96,512]{1,0:T(8,128)(2,1)} custom-call(bf16[96,256]{1,0:T(8,128)(2,1)S(1)} %get-tuple-element.60.value), custom_call_target="tpu_custom_call" | custom-call | tf_op jit(solution)/shard_map/pallas_call | solution.py:354
  51.8 0.6 %collective-permute-done.20.value = bf16[96,256]{1,0:T(8,128)(2,1)S(1)} collective-permute-done((bf16[96,256]{1,0:T(8,128)(2,1)S(1)}, bf16[96,256]{1,0:T(8,128)(2,1)S(1)}, u32[]{:S(2)}, u32[]{:S(2)}) %collective-permute-start.20) | collective-permute-done | bytes 49184 | tf_op jit(solution)/shard_map/ppermute | solution.py:31
  52.4 0.6 %shard_map.99 = bf16[96,512]{1,0:T(8,128)(2,1)} custom-call(bf16[96,256]{1,0:T(8,128)(2,1)S(1)} %collective-permute-done.20.value, bf16[96,512]{1,0:T(8,128)(2,1)} %shard_map.98.refs_0_), custom_call_target="tpu_custom_call", output_to_operand_aliasing={{}: (1, {})} | custom-call | tf_op jit(solution)/shard_map/pallas_call | solution.py:354
  (3 shorter events, 0.1 us)
Async XLA Ops:
  0.0 1.7 %collective-permute-start.3 = (bf16[128,512]{1,0:T(8,128)(2,1)}, bf16[128,512]{1,0:T(8,128)(2,1)S(1)}, u32[]{:S(2)}, u32[]{:S(2)}) collective-permute-start(bf16[128,512]{1,0:T(8,128)(2,1)} %source.1), channel_id=1, source_target_pairs={{0,4},{4,0},{8,12},{12,8},{16,20},{20,16},{24,28},{28,24},{1,5},{5... | collective-permute-start | bytes 393224 | tf_op jit(solution)/shard_map/ppermute | solution.py:31
  1.7 8.5 %collective-permute-start.4 = (bf16[256,256]{1,0:T(8,128)(2,1)S(1)}, bf16[256,256]{1,0:T(8,128)(2,1)S(1)}, u32[]{:S(2)}, u32[]{:S(2)}) collective-permute-start(bf16[256,256]{1,0:T(8,128)(2,1)S(1)} %shard_map.85.refs_0_), channel_id=1, source_target_pairs={{0,3},{1,2},{2,1},{3,0},{4,7},{5,6},{6,5},{7,4},{8,11},{9,10},{10,... | collective-permute-start | bytes 393224 | tf_op jit(solution)/shard_map/ppermute | solution.py:36
  5.6 6.9 %collective-permute-start.5 = (bf16[256,256]{1,0:T(8,128)(2,1)S(1)}, bf16[256,256]{1,0:T(8,128)(2,1)S(1)}, u32[]{:S(2)}, u32[]{:S(2)}) collective-permute-start(bf16[256,256]{1,0:T(8,128)(2,1)S(1)} %shard_map.85.refs_0_), channel_id=1, source_target_pairs={{0,1},{1,0},{2,3},{3,2},{4,5},{5,4},{6,7},{7,6},{8,9},{9,8},{10,11... | collective-permute-start | bytes 393224 | tf_op jit(solution)/shard_map/ppermute | solution.py:36
  6.1 6.8 %collective-permute-start.6 = (bf16[256,256]{1,0:T(8,128)(2,1)S(1)}, bf16[256,256]{1,0:T(8,128)(2,1)S(1)}, u32[]{:S(2)}, u32[]{:S(2)}) collective-permute-start(bf16[256,256]{1,0:T(8,128)(2,1)S(1)} %shard_map.85.refs_0_), channel_id=1, source_target_pairs={{0,2},{1,3},{2,0},{3,1},{4,6},{5,7},{6,4},{7,5},{8,10},{9,11},{10,... | collective-permute-start | bytes 393224 | tf_op jit(solution)/shard_map/ppermute | solution.py:36
  6.2 1.4 %collective-permute-start = (s32[4,768]{1,0:T(4,128)}, s32[4,768]{1,0:T(4,128)S(1)}, u32[]{:S(2)}, u32[]{:S(2)}) collective-permute-start(s32[4,768]{1,0:T(4,128)} %bitcast.3), channel_id=1, source_target_pairs={{0,4},{4,0},{8,12},{12,8},{16,20},{20,16},{24,28},{28,24},{1,5},{5... | collective-permute-start | bytes 36872 | tf_op jit(solution)/shard_map/ppermute | solution.py:31
  6.2 1.6 %collective-permute-start.1 = (s32[4,768]{1,0:T(4,128)}, s32[4,768]{1,0:T(4,128)S(1)}, u32[]{:S(2)}, u32[]{:S(2)}) collective-permute-start(s32[4,768]{1,0:T(4,128)} %bitcast.6), channel_id=1, source_target_pairs={{0,4},{4,0},{8,12},{12,8},{16,20},{20,16},{24,28},{28,24},{1,5},{5... | collective-permute-start | bytes 36872 | tf_op jit(solution)/shard_map/ppermute | solution.py:31
  13.2 5.7 %collective-permute-start.7 = (bf16[192,256]{1,0:T(8,128)(2,1)S(1)}, bf16[192,256]{1,0:T(8,128)(2,1)S(1)}, u32[]{:S(2)}, u32[]{:S(2)}) collective-permute-start(bf16[192,256]{1,0:T(8,128)(2,1)S(1)} %get-tuple-element.42), channel_id=1, source_target_pairs={{0,8},{4,12},{8,0},{12,4},{16,24},{20,28},{24,16},{28,20},{1,9},{5... | collective-permute-start | bytes 294920 | tf_op jit(solution)/shard_map/ppermute | solution.py:41
  14.8 9.9 %collective-permute-start.8 = (bf16[192,256]{1,0:T(8,128)(2,1)S(1)}, bf16[192,256]{1,0:T(8,128)(2,1)S(1)}, u32[]{:S(2)}, u32[]{:S(2)}) collective-permute-start(bf16[192,256]{1,0:T(8,128)(2,1)S(1)} %get-tuple-element.43), channel_id=1, source_target_pairs={{0,16},{4,20},{8,24},{12,28},{16,0},{20,4},{24,8},{28,12},{1,17},{... | collective-permute-start | bytes 294920 | tf_op jit(solution)/shard_map/ppermute | solution.py:41
  17.4 7.3 %collective-permute-start.9 = (bf16[192,256]{1,0:T(8,128)(2,1)S(1)}, bf16[192,256]{1,0:T(8,128)(2,1)S(1)}, u32[]{:S(2)}, u32[]{:S(2)}) collective-permute-start(bf16[192,256]{1,0:T(8,128)(2,1)S(1)} %get-tuple-element.44), channel_id=1, source_target_pairs={{0,24},{4,28},{8,16},{12,20},{16,8},{20,12},{24,0},{28,4},{1,25},{... | collective-permute-start | bytes 294920 | tf_op jit(solution)/shard_map/ppermute | solution.py:41
  17.7 1.2 %collective-permute-start.2 = (s32[8,128]{1,0:T(8,128)S(1)}, s32[8,128]{1,0:T(8,128)S(1)}, u32[]{:S(2)}, u32[]{:S(2)}) collective-permute-start(s32[8,128]{1,0:T(8,128)S(1)} %get-tuple-element.39.degree), channel_id=1, source_target_pairs={{0,4},{4,0},{8,12},{12,8},{16,20},{20,16},{24,28},{28,24},{1,5},{5... | collective-permute-start | bytes 12296 | tf_op jit(solution)/shard_map/ppermute | solution.py:31
  24.8 1.4 %collective-permute-start.10 = (bf16[192,256]{1,0:T(8,128)(2,1)S(1)}, bf16[192,256]{1,0:T(8,128)(2,1)S(1)}, u32[]{:S(2)}, u32[]{:S(2)}) collective-permute-start(bf16[192,256]{1,0:T(8,128)(2,1)S(1)} %shard_map.88.hedge), channel_id=1, source_target_pairs={{0,4},{4,0},{8,12},{12,8},{16,20},{20,16},{24,28},{28,24},{1,5},{5... | collective-permute-start | bytes 294920 | tf_op jit(solution)/shard_map/ppermute | solution.py:31
  26.8 4.4 %collective-permute-start.11 = (bf16[136,256]{1,0:T(8,128)(2,1)S(1)}, bf16[136,256]{1,0:T(8,128)(2,1)S(1)}, u32[]{:S(2)}, u32[]{:S(2)}) collective-permute-start(bf16[136,256]{1,0:T(8,128)(2,1)S(1)} %get-tuple-element.52), channel_id=1, source_target_pairs={{0,1},{1,0},{2,3},{3,2},{4,5},{5,4},{6,7},{7,6},{8,9},{9,8},{10,11... | collective-permute-start | bytes 208904 | tf_op jit(solution)/shard_map/ppermute | solution.py:36
  28.3 4.3 %collective-permute-start.12 = (bf16[136,256]{1,0:T(8,128)(2,1)S(1)}, bf16[136,256]{1,0:T(8,128)(2,1)S(1)}, u32[]{:S(2)}, u32[]{:S(2)}) collective-permute-start(bf16[136,256]{1,0:T(8,128)(2,1)S(1)} %get-tuple-element.53), channel_id=1, source_target_pairs={{0,2},{1,3},{2,0},{3,1},{4,6},{5,7},{6,4},{7,5},{8,10},{9,11},{10,... | collective-permute-start | bytes 208904 | tf_op jit(solution)/shard_map/ppermute | solution.py:36
  30.1 5.2 %collective-permute-start.13 = (bf16[136,256]{1,0:T(8,128)(2,1)S(1)}, bf16[136,256]{1,0:T(8,128)(2,1)S(1)}, u32[]{:S(2)}, u32[]{:S(2)}) collective-permute-start(bf16[136,256]{1,0:T(8,128)(2,1)S(1)} %get-tuple-element.54), channel_id=1, source_target_pairs={{0,3},{1,2},{2,1},{3,0},{4,7},{5,6},{6,5},{7,4},{8,11},{9,10},{10,... | collective-permute-start | bytes 208904 | tf_op jit(solution)/shard_map/ppermute | solution.py:36
  35.3 4.8 %collective-permute-start.14 = (bf16[136,256]{1,0:T(8,128)(2,1)S(1)}, bf16[136,256]{1,0:T(8,128)(2,1)S(1)}, u32[]{:S(2)}, u32[]{:S(2)}) collective-permute-start(bf16[136,256]{1,0:T(8,128)(2,1)S(1)} %get-tuple-element.56), channel_id=1, source_target_pairs={{0,8},{4,12},{8,0},{12,4},{16,24},{20,28},{24,16},{28,20},{1,9},{5... | collective-permute-start | bytes 208904 | tf_op jit(solution)/shard_map/ppermute | solution.py:41
  37.0 6.2 %collective-permute-start.15 = (bf16[136,256]{1,0:T(8,128)(2,1)S(1)}, bf16[136,256]{1,0:T(8,128)(2,1)S(1)}, u32[]{:S(2)}, u32[]{:S(2)}) collective-permute-start(bf16[136,256]{1,0:T(8,128)(2,1)S(1)} %get-tuple-element.56), channel_id=1, source_target_pairs={{0,16},{4,20},{8,24},{12,28},{16,0},{20,4},{24,8},{28,12},{1,17},{... | collective-permute-start | bytes 208904 | tf_op jit(solution)/shard_map/ppermute | solution.py:41
  38.4 6.2 %collective-permute-start.16 = (bf16[136,256]{1,0:T(8,128)(2,1)S(1)}, bf16[136,256]{1,0:T(8,128)(2,1)S(1)}, u32[]{:S(2)}, u32[]{:S(2)}) collective-permute-start(bf16[136,256]{1,0:T(8,128)(2,1)S(1)} %get-tuple-element.56), channel_id=1, source_target_pairs={{0,24},{4,28},{8,16},{12,20},{16,8},{20,12},{24,0},{28,4},{1,25},{... | collective-permute-start | bytes 208904 | tf_op jit(solution)/shard_map/ppermute | solution.py:41
  44.7 5.2 %collective-permute-start.17 = (bf16[128,256]{1,0:T(8,128)(2,1)S(1)}, bf16[128,256]{1,0:T(8,128)(2,1)S(1)}, u32[]{:S(2)}, u32[]{:S(2)}) collective-permute-start(bf16[128,256]{1,0:T(8,128)(2,1)S(1)} %get-tuple-element.58), channel_id=1, source_target_pairs={{0,3},{1,2},{2,1},{3,0},{4,7},{5,6},{6,5},{7,4},{8,11},{9,10},{10,... | collective-permute-start | bytes 196616 | tf_op jit(solution)/shard_map/ppermute | solution.py:36
  45.2 4.7 %collective-permute-start.18 = (bf16[128,256]{1,0:T(8,128)(2,1)S(1)}, bf16[128,256]{1,0:T(8,128)(2,1)S(1)}, u32[]{:S(2)}, u32[]{:S(2)}) collective-permute-start(bf16[128,256]{1,0:T(8,128)(2,1)S(1)} %get-tuple-element.58), channel_id=1, source_target_pairs={{0,1},{1,0},{2,3},{3,2},{4,5},{5,4},{6,7},{7,6},{8,9},{9,8},{10,11... | collective-permute-start | bytes 196616 | tf_op jit(solution)/shard_map/ppermute | solution.py:36
  46.6 4.3 %collective-permute-start.19 = (bf16[128,256]{1,0:T(8,128)(2,1)S(1)}, bf16[128,256]{1,0:T(8,128)(2,1)S(1)}, u32[]{:S(2)}, u32[]{:S(2)}) collective-permute-start(bf16[128,256]{1,0:T(8,128)(2,1)S(1)} %get-tuple-element.58), channel_id=1, source_target_pairs={{0,2},{1,3},{2,0},{3,1},{4,6},{5,7},{6,4},{7,5},{8,10},{9,11},{10,... | collective-permute-start | bytes 196616 | tf_op jit(solution)/shard_map/ppermute | solution.py:36
  51.1 1.3 %collective-permute-start.20 = (bf16[96,256]{1,0:T(8,128)(2,1)S(1)}, bf16[96,256]{1,0:T(8,128)(2,1)S(1)}, u32[]{:S(2)}, u32[]{:S(2)}) collective-permute-start(bf16[96,256]{1,0:T(8,128)(2,1)S(1)} %get-tuple-element.59), channel_id=1, source_target_pairs={{0,4},{4,0},{8,12},{12,8},{16,20},{20,16},{24,28},{28,24},{1,5},{5... | collective-permute-start | bytes 147464 | tf_op jit(solution)/shard_map/ppermute | solution.py:31

commit v4 on v3

--- a/solution.py
+++ b/solution.py
@@ -61,7 +61,8 @@
 
 
 def fetch_kernel(source, out, sem):
-    move = pltpu.make_async_copy(source, out, sem)
+    here, _ = half_place(out.shape[1])
+    move = pltpu.make_async_copy(source.at[:, here], out, sem)
     move.start()
     move.wait()
 
@@ -69,7 +70,7 @@
 def fetch(value):
     return pl.pallas_call(
         fetch_kernel,
-        out_shape=pltpu.VMEM(value.shape, value.dtype),
+        out_shape=pltpu.VMEM((value.shape[0], value.shape[1] // CORES), value.dtype),
         in_specs=[pl.BlockSpec(memory_space=pltpu.HBM)],
         out_specs=pl.BlockSpec(memory_space=pltpu.VMEM),
         scratch_shapes=[pltpu.SemaphoreType.DMA],
@@ -90,10 +91,10 @@
 
 
 def pack_kernel(own, other, out):
-    part, width = own.shape
-    columns, _ = half_place(width // CORES)
+    part, half = own.shape
+    columns, _ = half_place(half)
     mine, theirs = half_place(part)
-    out[mine, :] = own[:, columns]
+    out[mine, :] = own[...]
     out[theirs, :] = other[:, columns]
 
 

time: 53.2 us -> 53.2 us (level)
  no operation moved by 1% of the time
where the time goes in v4:
time: 53.2 us; the launch traced here: 53 us
  waiting for transfers between devices  23.5 us (44%)
  starting transfers between devices  21.7 us (41%)
  Pallas kernels  7.6 us (14%)
    ppermute x9, starting transfers between devices, send_edge(): lax.ppermute(value, 'edge', [(i, to_peer(i, step, count)) for i in range(...  11.6 us
    ppermute x6, waiting for transfers between devices, send_chip(): lax.ppermute(value, 'node', [(i, to_peer(i // CORES, step, chips) * CORES...  10.7 us
    ppermute x9, waiting for transfers between devices, send_edge(): lax.ppermute(value, 'edge', [(i, to_peer(i, step, count)) for i in range(...  9.06 us
    ppermute x6, starting transfers between devices, send_chip(): lax.ppermute(value, 'node', [(i, to_peer(i // CORES, step, chips) * CORES...  8.9 us
    ppermute x6, waiting for transfers between devices, swap_cores(): return lax.ppermute(value, 'node', [(i, i ^ 1) for i in range(count)])  3.83 us
    pallas_call x14, Pallas kernels, call(): pl.pallas_call(kernel, out_shape=[pltpu.VMEM(shape, dtype) for shape, dty...  3.01 us
    pallas_call x2, Pallas kernels, prepare(): pl.pallas_call(functools.partial(prepare_kernel, turn, chips, edges, owne...  2.47 us
    pallas_call x2, Pallas kernels, store(): pl.pallas_call(functools.partial(store_kernel, side), out_shape=pltpu.HBM...  1.27 us
  transfers between devices with their start and end apart: 21, of which 16 were waited for; matrix products, arithmetic and copies ran while one was open for 0% of the time, Pallas kernels for 11%

profile of v4, /device:TPU:0, one launch (start us, length us, event | category | flops | bytes accessed | tf_op | source)
XLA Modules:
  0.0 53.0 jit_solution(1570295804432627721)
XLA Ops:
  0.0 0.5 collective-permute-start.3
  0.5 0.8 %fetch.1.own = bf16[128,256]{1,0:T(8,128)(2,1)S(1)} custom-call(bf16[128,512]{1,0:T(8,128)(2,1)} %source.1), custom_call_target="tpu_custom_call" | custom-call | tf_op jit(solution)/shard_map/fetch/pallas_call | solution.py:71
  1.3 0.3 collective-permute-done.3.other
  1.7 3.9 %collective-permute-start.4 = (bf16[256,256]{1,0:T(8,128)(2,1)S(1)}, bf16[256,256]{1,0:T(8,128)(2,1)S(1)}, u32[]{:S(2)}, u32[]{:S(2)}) collective-permute-start(bf16[256,256]{1,0:T(8,128)(2,1)S(1)} %shard_map.85.refs_0_), channel_id=1, source_target_pairs={{0,3},{1,2},{2,1},{3,0},{4,7},{5,6},{6,5},{7,4},{8,11},{9,10},{10,... | collective-permute-start | bytes 393224 | tf_op jit(solution)/shard_map/ppermute | solution.py:36
  5.6 0.5 %collective-permute-start.5 = (bf16[256,256]{1,0:T(8,128)(2,1)S(1)}, bf16[256,256]{1,0:T(8,128)(2,1)S(1)}, u32[]{:S(2)}, u32[]{:S(2)}) collective-permute-start(bf16[256,256]{1,0:T(8,128)(2,1)S(1)} %shard_map.85.refs_0_), channel_id=1, source_target_pairs={{0,1},{1,0},{2,3},{3,2},{4,5},{5,4},{6,7},{7,6},{8,9},{9,8},{10,11... | collective-permute-start | bytes 393224 | tf_op jit(solution)/shard_map/ppermute | solution.py:36
  6.1 0.1 collective-permute-start.6
  6.2 0.0 collective-permute-start
  6.2 0.5 collective-permute-start.1
  6.7 0.9 %collective-permute-done.refs_3_ = s32[4,768]{1,0:T(4,128)S(1)} collective-permute-done((s32[4,768]{1,0:T(4,128)}, s32[4,768]{1,0:T(4,128)S(1)}, u32[]{:S(2)}, u32[]{:S(2)}) %collective-permute-start) | collective-permute-done | bytes 12320 | tf_op jit(solution)/shard_map/ppermute | solution.py:31
  7.6 0.2 collective-permute-done.1.refs_4_
  7.8 2.4 %shard_map.82 = (bf16[768,1024]{1,0:T(8,128)(2,1)S(1)}, s32[8,128]{1,0:T(8,128)S(1)}, bf16[512,512]{1,0:T(8,128)(2,1)S(1)}, bf16[512,512]{1,0:T(8,128)(2,1)S(1)}...) custom-call(s32[4,768]{1,0:T(4,128)} %bitcast.4, s32[4,768]{1,0:T(4,128)} %bitcast.7, s32[1,96]{1,0:T(1,128)} %bitcast.9, ...), custom_call_target="tpu_custom_call" | custom-call | tf_op jit(solution)/shard_map/pallas_call | solution.py:180
  10.1 0.1 shard_map.83
  10.2 0.0 collective-permute-done.4.refs_1_
  10.3 2.2 %collective-permute-done.5.refs_2_ = bf16[256,256]{1,0:T(8,128)(2,1)S(1)} collective-permute-done((bf16[256,256]{1,0:T(8,128)(2,1)S(1)}, bf16[256,256]{1,0:T(8,128)(2,1)S(1)}, u32[]{:S(2)}, u32[]{:S(2)}) %collective-permute-start.5) | collective-permute-done | bytes 131104 | tf_op jit(solution)/shard_map/ppermute | solution.py:36
  12.4 0.5 shard_map.86.first
  12.9 0.0 collective-permute-done.6.refs_0_
  12.9 0.3 shard_map.87
  13.2 1.6 %collective-permute-start.7 = (bf16[192,256]{1,0:T(8,128)(2,1)S(1)}, bf16[192,256]{1,0:T(8,128)(2,1)S(1)}, u32[]{:S(2)}, u32[]{:S(2)}) collective-permute-start(bf16[192,256]{1,0:T(8,128)(2,1)S(1)} %get-tuple-element.42), channel_id=1, source_target_pairs={{0,8},{4,12},{8,0},{12,4},{16,24},{20,28},{24,16},{28,20},{1,9},{5... | collective-permute-start | bytes 294920 | tf_op jit(solution)/shard_map/ppermute | solution.py:41
  14.8 2.6 %collective-permute-start.8 = (bf16[192,256]{1,0:T(8,128)(2,1)S(1)}, bf16[192,256]{1,0:T(8,128)(2,1)S(1)}, u32[]{:S(2)}, u32[]{:S(2)}) collective-permute-start(bf16[192,256]{1,0:T(8,128)(2,1)S(1)} %get-tuple-element.43), channel_id=1, source_target_pairs={{0,16},{4,20},{8,24},{12,28},{16,0},{20,4},{24,8},{28,12},{1,17},{... | collective-permute-start | bytes 294920 | tf_op jit(solution)/shard_map/ppermute | solution.py:41
  17.4 0.2 collective-permute-start.9
  17.7 0.0 collective-permute-start.2
  17.7 1.2 %collective-permute-done.2.degree_other = s32[8,128]{1,0:T(8,128)S(1)} collective-permute-done((s32[8,128]{1,0:T(8,128)S(1)}, s32[8,128]{1,0:T(8,128)S(1)}, u32[]{:S(2)}, u32[]{:S(2)}) %collective-permute-start.2) | collective-permute-done | bytes 4128 | tf_op jit(solution)/shard_map/ppermute | solution.py:31
  18.8 0.1 shard_map.84.scale
  18.9 0.0 collective-permute-done.7.refs_0_
  18.9 5.8 %collective-permute-done.8.refs_1_ = bf16[192,256]{1,0:T(8,128)(2,1)S(1)} collective-permute-done((bf16[192,256]{1,0:T(8,128)(2,1)S(1)}, bf16[192,256]{1,0:T(8,128)(2,1)S(1)}, u32[]{:S(2)}, u32[]{:S(2)}) %collective-permute-start.8) | collective-permute-done | bytes 98336 | tf_op jit(solution)/shard_map/ppermute | solution.py:41
  24.7 0.0 collective-permute-done.9.refs_2_
  24.7 0.1 shard_map.88.hedge
  24.8 0.1 collective-permute-start.10
  24.9 0.3 shard_map.90.folded
  25.2 0.3 shard_map.91
  25.5 0.7 %collective-permute-done.10.hedge_other = bf16[192,256]{1,0:T(8,128)(2,1)S(1)} collective-permute-done((bf16[192,256]{1,0:T(8,128)(2,1)S(1)}, bf16[192,256]{1,0:T(8,128)(2,1)S(1)}, u32[]{:S(2)}, u32[]{:S(2)}) %collective-permute-start.10) | collective-permute-done | bytes 98336 | tf_op jit(solution)/shard_map/ppermute | solution.py:31
  26.2 0.6 %shard_map.92 = (f32[136,256]{1,0:T(8,128)S(1)}, bf16[136,256]{1,0:T(8,128)(2,1)S(1)}, bf16[136,256]{1,0:T(8,128)(2,1)S(1)}, bf16[136,256]{1,0:T(8,128)(2,1)S(1)}) custom-call(bf16[192,256]{1,0:T(8,128)(2,1)S(1)} %collective-permute-done.10.hedge_other, f32[192,512]{1,0:T(8,128)S(1)} %get-tuple-element.49.key_part, ...), custom_call_target="tpu_custom_call" | custom-call | tf_op jit(solution)/shard_map/pallas_call | solution.py:51
  26.8 1.6 %collective-permute-start.11 = (bf16[136,256]{1,0:T(8,128)(2,1)S(1)}, bf16[136,256]{1,0:T(8,128)(2,1)S(1)}, u32[]{:S(2)}, u32[]{:S(2)}) collective-permute-start(bf16[136,256]{1,0:T(8,128)(2,1)S(1)} %get-tuple-element.52), channel_id=1, source_target_pairs={{0,1},{1,0},{2,3},{3,2},{4,5},{5,4},{6,7},{7,6},{8,9},{9,8},{10,11... | collective-permute-start | bytes 208904 | tf_op jit(solution)/shard_map/ppermute | solution.py:36
  28.3 1.7 %collective-permute-start.12 = (bf16[136,256]{1,0:T(8,128)(2,1)S(1)}, bf16[136,256]{1,0:T(8,128)(2,1)S(1)}, u32[]{:S(2)}, u32[]{:S(2)}) collective-permute-start(bf16[136,256]{1,0:T(8,128)(2,1)S(1)} %get-tuple-element.53), channel_id=1, source_target_pairs={{0,2},{1,3},{2,0},{3,1},{4,6},{5,7},{6,4},{7,5},{8,10},{9,11},{10,... | collective-permute-start | bytes 208904 | tf_op jit(solution)/shard_map/ppermute | solution.py:36
  30.1 0.3 collective-permute-start.13
  30.3 0.8 %collective-permute-done.11.refs_0_ = bf16[136,256]{1,0:T(8,128)(2,1)S(1)} collective-permute-done((bf16[136,256]{1,0:T(8,128)(2,1)S(1)}, bf16[136,256]{1,0:T(8,128)(2,1)S(1)}, u32[]{:S(2)}, u32[]{:S(2)}) %collective-permute-start.11) | collective-permute-done | bytes 69664 | tf_op jit(solution)/shard_map/ppermute | solution.py:36
  31.2 1.5 %collective-permute-done.12.refs_1_ = bf16[136,256]{1,0:T(8,128)(2,1)S(1)} collective-permute-done((bf16[136,256]{1,0:T(8,128)(2,1)S(1)}, bf16[136,256]{1,0:T(8,128)(2,1)S(1)}, u32[]{:S(2)}, u32[]{:S(2)}) %collective-permute-start.12) | collective-permute-done | bytes 69664 | tf_op jit(solution)/shard_map/ppermute | solution.py:36
  32.7 2.6 %collective-permute-done.13.refs_2_ = bf16[136,256]{1,0:T(8,128)(2,1)S(1)} collective-permute-done((bf16[136,256]{1,0:T(8,128)(2,1)S(1)}, bf16[136,256]{1,0:T(8,128)(2,1)S(1)}, u32[]{:S(2)}, u32[]{:S(2)}) %collective-permute-start.13) | collective-permute-done | bytes 69664 | tf_op jit(solution)/shard_map/ppermute | solution.py:36
  35.3 1.7 %collective-permute-start.14 = (bf16[136,256]{1,0:T(8,128)(2,1)S(1)}, bf16[136,256]{1,0:T(8,128)(2,1)S(1)}, u32[]{:S(2)}, u32[]{:S(2)}) collective-permute-start(bf16[136,256]{1,0:T(8,128)(2,1)S(1)} %get-tuple-element.56), channel_id=1, source_target_pairs={{0,8},{4,12},{8,0},{12,4},{16,24},{20,28},{24,16},{28,20},{1,9},{5... | collective-permute-start | bytes 208904 | tf_op jit(solution)/shard_map/ppermute | solution.py:41
  37.0 1.4 %collective-permute-start.15 = (bf16[136,256]{1,0:T(8,128)(2,1)S(1)}, bf16[136,256]{1,0:T(8,128)(2,1)S(1)}, u32[]{:S(2)}, u32[]{:S(2)}) collective-permute-start(bf16[136,256]{1,0:T(8,128)(2,1)S(1)} %get-tuple-element.56), channel_id=1, source_target_pairs={{0,16},{4,20},{8,24},{12,28},{16,0},{20,4},{24,8},{28,12},{1,17},{... | collective-permute-start | bytes 208904 | tf_op jit(solution)/shard_map/ppermute | solution.py:41
  38.4 1.3 %collective-permute-start.16 = (bf16[136,256]{1,0:T(8,128)(2,1)S(1)}, bf16[136,256]{1,0:T(8,128)(2,1)S(1)}, u32[]{:S(2)}, u32[]{:S(2)}) collective-permute-start(bf16[136,256]{1,0:T(8,128)(2,1)S(1)} %get-tuple-element.56), channel_id=1, source_target_pairs={{0,24},{4,28},{8,16},{12,20},{16,8},{20,12},{24,0},{28,4},{1,25},{... | collective-permute-start | bytes 208904 | tf_op jit(solution)/shard_map/ppermute | solution.py:41
  39.8 0.3 collective-permute-done.14.refs_0_
  40.1 3.1 %collective-permute-done.15.refs_1_ = bf16[136,256]{1,0:T(8,128)(2,1)S(1)} collective-permute-done((bf16[136,256]{1,0:T(8,128)(2,1)S(1)}, bf16[136,256]{1,0:T(8,128)(2,1)S(1)}, u32[]{:S(2)}, u32[]{:S(2)}) %collective-permute-start.15) | collective-permute-done | bytes 69664 | tf_op jit(solution)/shard_map/ppermute | solution.py:41
  43.2 1.5 %collective-permute-done.16.refs_2_ = bf16[136,256]{1,0:T(8,128)(2,1)S(1)} collective-permute-done((bf16[136,256]{1,0:T(8,128)(2,1)S(1)}, bf16[136,256]{1,0:T(8,128)(2,1)S(1)}, u32[]{:S(2)}, u32[]{:S(2)}) %collective-permute-start.16) | collective-permute-done | bytes 69664 | tf_op jit(solution)/shard_map/ppermute | solution.py:41
  44.7 0.5 %collective-permute-start.17 = (bf16[128,256]{1,0:T(8,128)(2,1)S(1)}, bf16[128,256]{1,0:T(8,128)(2,1)S(1)}, u32[]{:S(2)}, u32[]{:S(2)}) collective-permute-start(bf16[128,256]{1,0:T(8,128)(2,1)S(1)} %get-tuple-element.58), channel_id=1, source_target_pairs={{0,3},{1,2},{2,1},{3,0},{4,7},{5,6},{6,5},{7,4},{8,11},{9,10},{10,... | collective-permute-start | bytes 196616 | tf_op jit(solution)/shard_map/ppermute | solution.py:36
  45.2 1.3 %collective-permute-start.18 = (bf16[128,256]{1,0:T(8,128)(2,1)S(1)}, bf16[128,256]{1,0:T(8,128)(2,1)S(1)}, u32[]{:S(2)}, u32[]{:S(2)}) collective-permute-start(bf16[128,256]{1,0:T(8,128)(2,1)S(1)} %get-tuple-element.58), channel_id=1, source_target_pairs={{0,1},{1,0},{2,3},{3,2},{4,5},{5,4},{6,7},{7,6},{8,9},{9,8},{10,11... | collective-permute-start | bytes 196616 | tf_op jit(solution)/shard_map/ppermute | solution.py:36
  46.6 1.7 %collective-permute-start.19 = (bf16[128,256]{1,0:T(8,128)(2,1)S(1)}, bf16[128,256]{1,0:T(8,128)(2,1)S(1)}, u32[]{:S(2)}, u32[]{:S(2)}) collective-permute-start(bf16[128,256]{1,0:T(8,128)(2,1)S(1)} %get-tuple-element.58), channel_id=1, source_target_pairs={{0,2},{1,3},{2,0},{3,1},{4,6},{5,7},{6,4},{7,5},{8,10},{9,11},{10,... | collective-permute-start | bytes 196616 | tf_op jit(solution)/shard_map/ppermute | solution.py:36
  48.3 0.3 shard_map.89.query
  48.6 0.1 shard_map.95.denom
  48.7 1.2 %collective-permute-done.17.refs_1_ = bf16[128,256]{1,0:T(8,128)(2,1)S(1)} collective-permute-done((bf16[128,256]{1,0:T(8,128)(2,1)S(1)}, bf16[128,256]{1,0:T(8,128)(2,1)S(1)}, u32[]{:S(2)}, u32[]{:S(2)}) %collective-permute-start.17) | collective-permute-done | bytes 65568 | tf_op jit(solution)/shard_map/ppermute | solution.py:36
  49.9 0.0 collective-permute-done.18.refs_2_
  49.9 0.2 shard_map.96.numer
  50.2 0.7 %collective-permute-done.19.refs_0_ = bf16[128,256]{1,0:T(8,128)(2,1)S(1)} collective-permute-done((bf16[128,256]{1,0:T(8,128)(2,1)S(1)}, bf16[128,256]{1,0:T(8,128)(2,1)S(1)}, u32[]{:S(2)}, u32[]{:S(2)}) %collective-permute-start.19) | collective-permute-done | bytes 65568 | tf_op jit(solution)/shard_map/ppermute | solution.py:36
  50.9 0.2 shard_map.97
  51.0 0.1 collective-permute-start.20
  51.1 0.6 %shard_map.98.refs_0_ = bf16[96,512]{1,0:T(8,128)(2,1)} custom-call(bf16[96,256]{1,0:T(8,128)(2,1)S(1)} %get-tuple-element.60.value), custom_call_target="tpu_custom_call" | custom-call | tf_op jit(solution)/shard_map/pallas_call | solution.py:355
  51.8 0.6 %collective-permute-done.20.value = bf16[96,256]{1,0:T(8,128)(2,1)S(1)} collective-permute-done((bf16[96,256]{1,0:T(8,128)(2,1)S(1)}, bf16[96,256]{1,0:T(8,128)(2,1)S(1)}, u32[]{:S(2)}, u32[]{:S(2)}) %collective-permute-start.20) | collective-permute-done | bytes 49184 | tf_op jit(solution)/shard_map/ppermute | solution.py:31
  52.3 0.6 %shard_map.99 = bf16[96,512]{1,0:T(8,128)(2,1)} custom-call(bf16[96,256]{1,0:T(8,128)(2,1)S(1)} %collective-permute-done.20.value, bf16[96,512]{1,0:T(8,128)(2,1)} %shard_map.98.refs_0_), custom_call_target="tpu_custom_call", output_to_operand_aliasing={{}: (1, {})} | custom-call | tf_op jit(solution)/shard_map/pallas_call | solution.py:355
  (3 shorter events, 0.1 us)
Async XLA Ops:
  0.0 1.7 %collective-permute-start.3 = (bf16[128,512]{1,0:T(8,128)(2,1)}, bf16[128,512]{1,0:T(8,128)(2,1)S(1)}, u32[]{:S(2)}, u32[]{:S(2)}) collective-permute-start(bf16[128,512]{1,0:T(8,128)(2,1)} %source.1), channel_id=1, source_target_pairs={{0,4},{4,0},{8,12},{12,8},{16,20},{20,16},{24,28},{28,24},{1,5},{5... | collective-permute-start | bytes 393224 | tf_op jit(solution)/shard_map/ppermute | solution.py:31
  1.7 8.5 %collective-permute-start.4 = (bf16[256,256]{1,0:T(8,128)(2,1)S(1)}, bf16[256,256]{1,0:T(8,128)(2,1)S(1)}, u32[]{:S(2)}, u32[]{:S(2)}) collective-permute-start(bf16[256,256]{1,0:T(8,128)(2,1)S(1)} %shard_map.85.refs_0_), channel_id=1, source_target_pairs={{0,3},{1,2},{2,1},{3,0},{4,7},{5,6},{6,5},{7,4},{8,11},{9,10},{10,... | collective-permute-start | bytes 393224 | tf_op jit(solution)/shard_map/ppermute | solution.py:36
  5.6 6.9 %collective-permute-start.5 = (bf16[256,256]{1,0:T(8,128)(2,1)S(1)}, bf16[256,256]{1,0:T(8,128)(2,1)S(1)}, u32[]{:S(2)}, u32[]{:S(2)}) collective-permute-start(bf16[256,256]{1,0:T(8,128)(2,1)S(1)} %shard_map.85.refs_0_), channel_id=1, source_target_pairs={{0,1},{1,0},{2,3},{3,2},{4,5},{5,4},{6,7},{7,6},{8,9},{9,8},{10,11... | collective-permute-start | bytes 393224 | tf_op jit(solution)/shard_map/ppermute | solution.py:36
  6.1 6.8 %collective-permute-start.6 = (bf16[256,256]{1,0:T(8,128)(2,1)S(1)}, bf16[256,256]{1,0:T(8,128)(2,1)S(1)}, u32[]{:S(2)}, u32[]{:S(2)}) collective-permute-start(bf16[256,256]{1,0:T(8,128)(2,1)S(1)} %shard_map.85.refs_0_), channel_id=1, source_target_pairs={{0,2},{1,3},{2,0},{3,1},{4,6},{5,7},{6,4},{7,5},{8,10},{9,11},{10,... | collective-permute-start | bytes 393224 | tf_op jit(solution)/shard_map/ppermute | solution.py:36
  6.2 1.4 %collective-permute-start = (s32[4,768]{1,0:T(4,128)}, s32[4,768]{1,0:T(4,128)S(1)}, u32[]{:S(2)}, u32[]{:S(2)}) collective-permute-start(s32[4,768]{1,0:T(4,128)} %bitcast.3), channel_id=1, source_target_pairs={{0,4},{4,0},{8,12},{12,8},{16,20},{20,16},{24,28},{28,24},{1,5},{5... | collective-permute-start | bytes 36872 | tf_op jit(solution)/shard_map/ppermute | solution.py:31
  6.2 1.6 %collective-permute-start.1 = (s32[4,768]{1,0:T(4,128)}, s32[4,768]{1,0:T(4,128)S(1)}, u32[]{:S(2)}, u32[]{:S(2)}) collective-permute-start(s32[4,768]{1,0:T(4,128)} %bitcast.6), channel_id=1, source_target_pairs={{0,4},{4,0},{8,12},{12,8},{16,20},{20,16},{24,28},{28,24},{1,5},{5... | collective-permute-start | bytes 36872 | tf_op jit(solution)/shard_map/ppermute | solution.py:31
  13.2 5.7 %collective-permute-start.7 = (bf16[192,256]{1,0:T(8,128)(2,1)S(1)}, bf16[192,256]{1,0:T(8,128)(2,1)S(1)}, u32[]{:S(2)}, u32[]{:S(2)}) collective-permute-start(bf16[192,256]{1,0:T(8,128)(2,1)S(1)} %get-tuple-element.42), channel_id=1, source_target_pairs={{0,8},{4,12},{8,0},{12,4},{16,24},{20,28},{24,16},{28,20},{1,9},{5... | collective-permute-start | bytes 294920 | tf_op jit(solution)/shard_map/ppermute | solution.py:41
  14.8 9.9 %collective-permute-start.8 = (bf16[192,256]{1,0:T(8,128)(2,1)S(1)}, bf16[192,256]{1,0:T(8,128)(2,1)S(1)}, u32[]{:S(2)}, u32[]{:S(2)}) collective-permute-start(bf16[192,256]{1,0:T(8,128)(2,1)S(1)} %get-tuple-element.43), channel_id=1, source_target_pairs={{0,16},{4,20},{8,24},{12,28},{16,0},{20,4},{24,8},{28,12},{1,17},{... | collective-permute-start | bytes 294920 | tf_op jit(solution)/shard_map/ppermute | solution.py:41
  17.4 7.3 %collective-permute-start.9 = (bf16[192,256]{1,0:T(8,128)(2,1)S(1)}, bf16[192,256]{1,0:T(8,128)(2,1)S(1)}, u32[]{:S(2)}, u32[]{:S(2)}) collective-permute-start(bf16[192,256]{1,0:T(8,128)(2,1)S(1)} %get-tuple-element.44), channel_id=1, source_target_pairs={{0,24},{4,28},{8,16},{12,20},{16,8},{20,12},{24,0},{28,4},{1,25},{... | collective-permute-start | bytes 294920 | tf_op jit(solution)/shard_map/ppermute | solution.py:41
  17.7 1.2 %collective-permute-start.2 = (s32[8,128]{1,0:T(8,128)S(1)}, s32[8,128]{1,0:T(8,128)S(1)}, u32[]{:S(2)}, u32[]{:S(2)}) collective-permute-start(s32[8,128]{1,0:T(8,128)S(1)} %get-tuple-element.39.degree), channel_id=1, source_target_pairs={{0,4},{4,0},{8,12},{12,8},{16,20},{20,16},{24,28},{28,24},{1,5},{5... | collective-permute-start | bytes 12296 | tf_op jit(solution)/shard_map/ppermute | solution.py:31
  24.8 1.4 %collective-permute-start.10 = (bf16[192,256]{1,0:T(8,128)(2,1)S(1)}, bf16[192,256]{1,0:T(8,128)(2,1)S(1)}, u32[]{:S(2)}, u32[]{:S(2)}) collective-permute-start(bf16[192,256]{1,0:T(8,128)(2,1)S(1)} %shard_map.88.hedge), channel_id=1, source_target_pairs={{0,4},{4,0},{8,12},{12,8},{16,20},{20,16},{24,28},{28,24},{1,5},{5... | collective-permute-start | bytes 294920 | tf_op jit(solution)/shard_map/ppermute | solution.py:31
  26.8 4.4 %collective-permute-start.11 = (bf16[136,256]{1,0:T(8,128)(2,1)S(1)}, bf16[136,256]{1,0:T(8,128)(2,1)S(1)}, u32[]{:S(2)}, u32[]{:S(2)}) collective-permute-start(bf16[136,256]{1,0:T(8,128)(2,1)S(1)} %get-tuple-element.52), channel_id=1, source_target_pairs={{0,1},{1,0},{2,3},{3,2},{4,5},{5,4},{6,7},{7,6},{8,9},{9,8},{10,11... | collective-permute-start | bytes 208904 | tf_op jit(solution)/shard_map/ppermute | solution.py:36
  28.3 4.3 %collective-permute-start.12 = (bf16[136,256]{1,0:T(8,128)(2,1)S(1)}, bf16[136,256]{1,0:T(8,128)(2,1)S(1)}, u32[]{:S(2)}, u32[]{:S(2)}) collective-permute-start(bf16[136,256]{1,0:T(8,128)(2,1)S(1)} %get-tuple-element.53), channel_id=1, source_target_pairs={{0,2},{1,3},{2,0},{3,1},{4,6},{5,7},{6,4},{7,5},{8,10},{9,11},{10,... | collective-permute-start | bytes 208904 | tf_op jit(solution)/shard_map/ppermute | solution.py:36
  30.1 5.2 %collective-permute-start.13 = (bf16[136,256]{1,0:T(8,128)(2,1)S(1)}, bf16[136,256]{1,0:T(8,128)(2,1)S(1)}, u32[]{:S(2)}, u32[]{:S(2)}) collective-permute-start(bf16[136,256]{1,0:T(8,128)(2,1)S(1)} %get-tuple-element.54), channel_id=1, source_target_pairs={{0,3},{1,2},{2,1},{3,0},{4,7},{5,6},{6,5},{7,4},{8,11},{9,10},{10,... | collective-permute-start | bytes 208904 | tf_op jit(solution)/shard_map/ppermute | solution.py:36
  35.3 4.8 %collective-permute-start.14 = (bf16[136,256]{1,0:T(8,128)(2,1)S(1)}, bf16[136,256]{1,0:T(8,128)(2,1)S(1)}, u32[]{:S(2)}, u32[]{:S(2)}) collective-permute-start(bf16[136,256]{1,0:T(8,128)(2,1)S(1)} %get-tuple-element.56), channel_id=1, source_target_pairs={{0,8},{4,12},{8,0},{12,4},{16,24},{20,28},{24,16},{28,20},{1,9},{5... | collective-permute-start | bytes 208904 | tf_op jit(solution)/shard_map/ppermute | solution.py:41
  37.0 6.2 %collective-permute-start.15 = (bf16[136,256]{1,0:T(8,128)(2,1)S(1)}, bf16[136,256]{1,0:T(8,128)(2,1)S(1)}, u32[]{:S(2)}, u32[]{:S(2)}) collective-permute-start(bf16[136,256]{1,0:T(8,128)(2,1)S(1)} %get-tuple-element.56), channel_id=1, source_target_pairs={{0,16},{4,20},{8,24},{12,28},{16,0},{20,4},{24,8},{28,12},{1,17},{... | collective-permute-start | bytes 208904 | tf_op jit(solution)/shard_map/ppermute | solution.py:41
  38.4 6.2 %collective-permute-start.16 = (bf16[136,256]{1,0:T(8,128)(2,1)S(1)}, bf16[136,256]{1,0:T(8,128)(2,1)S(1)}, u32[]{:S(2)}, u32[]{:S(2)}) collective-permute-start(bf16[136,256]{1,0:T(8,128)(2,1)S(1)} %get-tuple-element.56), channel_id=1, source_target_pairs={{0,24},{4,28},{8,16},{12,20},{16,8},{20,12},{24,0},{28,4},{1,25},{... | collective-permute-start | bytes 208904 | tf_op jit(solution)/shard_map/ppermute | solution.py:41
  44.7 5.2 %collective-permute-start.17 = (bf16[128,256]{1,0:T(8,128)(2,1)S(1)}, bf16[128,256]{1,0:T(8,128)(2,1)S(1)}, u32[]{:S(2)}, u32[]{:S(2)}) collective-permute-start(bf16[128,256]{1,0:T(8,128)(2,1)S(1)} %get-tuple-element.58), channel_id=1, source_target_pairs={{0,3},{1,2},{2,1},{3,0},{4,7},{5,6},{6,5},{7,4},{8,11},{9,10},{10,... | collective-permute-start | bytes 196616 | tf_op jit(solution)/shard_map/ppermute | solution.py:36
  45.2 4.7 %collective-permute-start.18 = (bf16[128,256]{1,0:T(8,128)(2,1)S(1)}, bf16[128,256]{1,0:T(8,128)(2,1)S(1)}, u32[]{:S(2)}, u32[]{:S(2)}) collective-permute-start(bf16[128,256]{1,0:T(8,128)(2,1)S(1)} %get-tuple-element.58), channel_id=1, source_target_pairs={{0,1},{1,0},{2,3},{3,2},{4,5},{5,4},{6,7},{7,6},{8,9},{9,8},{10,11... | collective-permute-start | bytes 196616 | tf_op jit(solution)/shard_map/ppermute | solution.py:36
  46.6 4.3 %collective-permute-start.19 = (bf16[128,256]{1,0:T(8,128)(2,1)S(1)}, bf16[128,256]{1,0:T(8,128)(2,1)S(1)}, u32[]{:S(2)}, u32[]{:S(2)}) collective-permute-start(bf16[128,256]{1,0:T(8,128)(2,1)S(1)} %get-tuple-element.58), channel_id=1, source_target_pairs={{0,2},{1,3},{2,0},{3,1},{4,6},{5,7},{6,4},{7,5},{8,10},{9,11},{10,... | collective-permute-start | bytes 196616 | tf_op jit(solution)/shard_map/ppermute | solution.py:36
  51.0 1.3 %collective-permute-start.20 = (bf16[96,256]{1,0:T(8,128)(2,1)S(1)}, bf16[96,256]{1,0:T(8,128)(2,1)S(1)}, u32[]{:S(2)}, u32[]{:S(2)}) collective-permute-start(bf16[96,256]{1,0:T(8,128)(2,1)S(1)} %get-tuple-element.59), channel_id=1, source_target_pairs={{0,4},{4,0},{8,12},{12,8},{16,20},{20,16},{24,28},{28,24},{1,5},{5... | collective-permute-start | bytes 147464 | tf_op jit(solution)/shard_map/ppermute | solution.py:31

commit v5 on v2

--- a/solution.py
+++ b/solution.py
@@ -61,7 +61,8 @@
 
 
 def fetch_kernel(source, out, sem):
-    move = pltpu.make_async_copy(source, out, sem)
+    here, _ = half_place(out.shape[1])
+    move = pltpu.make_async_copy(source.at[:, here], out, sem)
     move.start()
     move.wait()
 
@@ -69,7 +70,7 @@
 def fetch(value):
     return pl.pallas_call(
         fetch_kernel,
-        out_shape=pltpu.VMEM(value.shape, value.dtype),
+        out_shape=pltpu.VMEM((value.shape[0], value.shape[1] // CORES), value.dtype),
         in_specs=[pl.BlockSpec(memory_space=pltpu.HBM)],
         out_specs=pl.BlockSpec(memory_space=pltpu.VMEM),
         scratch_shapes=[pltpu.SemaphoreType.DMA],
@@ -90,10 +91,10 @@
 
 
 def pack_kernel(own, other, out):
-    part, width = own.shape
-    columns, _ = half_place(width // CORES)
+    part, half = own.shape
+    columns, _ = half_place(half)
     mine, theirs = half_place(part)
-    out[mine, :] = own[:, columns]
+    out[mine, :] = own[...]
     out[theirs, :] = other[:, columns]
 
 
@@ -402,7 +403,7 @@
     given += (swap_cores(given[0]), swap_cores(given[1])) + weights
     held = prepare(1 - SENDS_FIRST, sizes, (), *given)
     counts, degree, w_query, w_key, w_value, w_out = prepare(SENDS_FIRST, sizes, held, *given)
-    early, late = [0, edges - 1], list(range(1, edges - 1))
+    early, late = [0, edges - 1] + list(range(1, edges - 2)), [edges - 2]
     (first,) = vmem_call(
         functools.partial(first_kernel, min(chips, 4) * pair, early), [((shard, half), f32)]
     )(counts, *[blocks[i] for i in early])

time: 53.5 us -> 53.4 us (level)
  no operation moved by 1% of the time
where the time goes in v5:
time: 53.4 us; the launch traced here: 53.2 us
  waiting for transfers between devices  24.3 us (46%)
  starting transfers between devices  21.7 us (41%)
  Pallas kernels  7.03 us (13%)
    ppermute x9, starting transfers between devices, send_edge(): lax.ppermute(value, 'edge', [(i, to_peer(i, step, count)) for i in range(...  11.6 us
    ppermute x6, waiting for transfers between devices, send_chip(): lax.ppermute(value, 'node', [(i, to_peer(i // CORES, step, chips) * CORES...  10.7 us
    ppermute x9, waiting for transfers between devices, send_edge(): lax.ppermute(value, 'edge', [(i, to_peer(i, step, count)) for i in range(...  9.04 us
    ppermute x6, starting transfers between devices, send_chip(): lax.ppermute(value, 'node', [(i, to_peer(i // CORES, step, chips) * CORES...  8.9 us
    ppermute x6, waiting for transfers between devices, swap_cores(): return lax.ppermute(value, 'node', [(i, i ^ 1) for i in range(count)])  4.6 us
    pallas_call x14, Pallas kernels, call(): pl.pallas_call(kernel, out_shape=[pltpu.VMEM(shape, dtype) for shape, dty...  2.89 us
    pallas_call x2, Pallas kernels, prepare(): pl.pallas_call(functools.partial(prepare_kernel, turn, chips, edges, owne...  2.47 us
    ppermute x6, starting transfers between devices, swap_cores(): return lax.ppermute(value, 'node', [(i, i ^ 1) for i in range(count)])  1.15 us
  transfers between devices with their start and end apart: 21, of which 16 were waited for; matrix products, arithmetic and copies ran while one was open for 0% of the time, Pallas kernels for 9%

profile of v5, /device:TPU:0, one launch (start us, length us, event | category | flops | bytes accessed | tf_op | source)
XLA Modules:
  0.0 53.2 jit_solution(2314905959538505554)
XLA Ops:
  0.0 0.5 collective-permute-start.3
  0.5 0.8 %fetch.1.own = bf16[128,256]{1,0:T(8,128)(2,1)S(1)} custom-call(bf16[128,512]{1,0:T(8,128)(2,1)} %source.1), custom_call_target="tpu_custom_call" | custom-call | tf_op jit(solution)/shard_map/fetch/pallas_call | solution.py:71
  1.3 0.3 collective-permute-done.3.other
  1.7 3.9 %collective-permute-start.4 = (bf16[256,256]{1,0:T(8,128)(2,1)S(1)}, bf16[256,256]{1,0:T(8,128)(2,1)S(1)}, u32[]{:S(2)}, u32[]{:S(2)}) collective-permute-start(bf16[256,256]{1,0:T(8,128)(2,1)S(1)} %shard_map.85.refs_0_), channel_id=1, source_target_pairs={{0,3},{1,2},{2,1},{3,0},{4,7},{5,6},{6,5},{7,4},{8,11},{9,10},{10,... | collective-permute-start | bytes 393224 | tf_op jit(solution)/shard_map/ppermute | solution.py:36
  5.6 0.5 %collective-permute-start.5 = (bf16[256,256]{1,0:T(8,128)(2,1)S(1)}, bf16[256,256]{1,0:T(8,128)(2,1)S(1)}, u32[]{:S(2)}, u32[]{:S(2)}) collective-permute-start(bf16[256,256]{1,0:T(8,128)(2,1)S(1)} %shard_map.85.refs_0_), channel_id=1, source_target_pairs={{0,1},{1,0},{2,3},{3,2},{4,5},{5,4},{6,7},{7,6},{8,9},{9,8},{10,11... | collective-permute-start | bytes 393224 | tf_op jit(solution)/shard_map/ppermute | solution.py:36
  6.1 0.1 collective-permute-start.6
  6.2 0.0 collective-permute-start
  6.2 0.5 collective-permute-start.1
  6.7 0.9 %collective-permute-done.refs_3_ = s32[4,768]{1,0:T(4,128)S(1)} collective-permute-done((s32[4,768]{1,0:T(4,128)}, s32[4,768]{1,0:T(4,128)S(1)}, u32[]{:S(2)}, u32[]{:S(2)}) %collective-permute-start) | collective-permute-done | bytes 12320 | tf_op jit(solution)/shard_map/ppermute | solution.py:31
  7.6 0.2 collective-permute-done.1.refs_4_
  7.8 2.4 %shard_map.82 = (bf16[768,1024]{1,0:T(8,128)(2,1)S(1)}, s32[8,128]{1,0:T(8,128)S(1)}, bf16[512,512]{1,0:T(8,128)(2,1)S(1)}, bf16[512,512]{1,0:T(8,128)(2,1)S(1)}...) custom-call(s32[4,768]{1,0:T(4,128)} %bitcast.4, s32[4,768]{1,0:T(4,128)} %bitcast.7, s32[1,96]{1,0:T(1,128)} %bitcast.9, ...), custom_call_target="tpu_custom_call" | custom-call | tf_op jit(solution)/shard_map/pallas_call | solution.py:180
  10.1 0.1 shard_map.83
  10.2 0.0 collective-permute-done.4.refs_1_
  10.3 2.2 %collective-permute-done.5.refs_2_ = bf16[256,256]{1,0:T(8,128)(2,1)S(1)} collective-permute-done((bf16[256,256]{1,0:T(8,128)(2,1)S(1)}, bf16[256,256]{1,0:T(8,128)(2,1)S(1)}, u32[]{:S(2)}, u32[]{:S(2)}) %collective-permute-start.5) | collective-permute-done | bytes 131104 | tf_op jit(solution)/shard_map/ppermute | solution.py:36
  12.4 0.5 shard_map.86.first
  12.9 0.0 collective-permute-done.6.refs_0_
  12.9 0.3 shard_map.87
  13.2 1.6 %collective-permute-start.7 = (bf16[192,256]{1,0:T(8,128)(2,1)S(1)}, bf16[192,256]{1,0:T(8,128)(2,1)S(1)}, u32[]{:S(2)}, u32[]{:S(2)}) collective-permute-start(bf16[192,256]{1,0:T(8,128)(2,1)S(1)} %get-tuple-element.44), channel_id=1, source_target_pairs={{0,8},{4,12},{8,0},{12,4},{16,24},{20,28},{24,16},{28,20},{1,9},{5... | collective-permute-start | bytes 294920 | tf_op jit(solution)/shard_map/ppermute | solution.py:41
  14.8 2.6 %collective-permute-start.8 = (bf16[192,256]{1,0:T(8,128)(2,1)S(1)}, bf16[192,256]{1,0:T(8,128)(2,1)S(1)}, u32[]{:S(2)}, u32[]{:S(2)}) collective-permute-start(bf16[192,256]{1,0:T(8,128)(2,1)S(1)} %get-tuple-element.45), channel_id=1, source_target_pairs={{0,16},{4,20},{8,24},{12,28},{16,0},{20,4},{24,8},{28,12},{1,17},{... | collective-permute-start | bytes 294920 | tf_op jit(solution)/shard_map/ppermute | solution.py:41
  17.4 0.2 collective-permute-start.9
  17.7 0.0 collective-permute-start.2
  17.7 1.2 %collective-permute-done.2.degree_other = s32[8,128]{1,0:T(8,128)S(1)} collective-permute-done((s32[8,128]{1,0:T(8,128)S(1)}, s32[8,128]{1,0:T(8,128)S(1)}, u32[]{:S(2)}, u32[]{:S(2)}) %collective-permute-start.2) | collective-permute-done | bytes 4128 | tf_op jit(solution)/shard_map/ppermute | solution.py:31
  18.8 0.1 shard_map.84.scale
  18.9 0.0 collective-permute-done.7.refs_0_
  18.9 5.8 %collective-permute-done.8.refs_1_ = bf16[192,256]{1,0:T(8,128)(2,1)S(1)} collective-permute-done((bf16[192,256]{1,0:T(8,128)(2,1)S(1)}, bf16[192,256]{1,0:T(8,128)(2,1)S(1)}, u32[]{:S(2)}, u32[]{:S(2)}) %collective-permute-start.8) | collective-permute-done | bytes 98336 | tf_op jit(solution)/shard_map/ppermute | solution.py:41
  24.7 0.0 collective-permute-done.9.refs_2_
  24.7 0.1 shard_map.88.hedge
  24.8 0.1 collective-permute-start.10
  24.9 0.3 shard_map.90
  25.2 1.0 %collective-permute-done.10.hedge_other = bf16[192,256]{1,0:T(8,128)(2,1)S(1)} collective-permute-done((bf16[192,256]{1,0:T(8,128)(2,1)S(1)}, bf16[192,256]{1,0:T(8,128)(2,1)S(1)}, u32[]{:S(2)}, u32[]{:S(2)}) %collective-permute-start.10) | collective-permute-done | bytes 98336 | tf_op jit(solution)/shard_map/ppermute | solution.py:31
  26.2 0.6 %shard_map.91 = (f32[136,256]{1,0:T(8,128)S(1)}, bf16[136,256]{1,0:T(8,128)(2,1)S(1)}, bf16[136,256]{1,0:T(8,128)(2,1)S(1)}, bf16[136,256]{1,0:T(8,128)(2,1)S(1)}) custom-call(bf16[192,256]{1,0:T(8,128)(2,1)S(1)} %collective-permute-done.10.hedge_other, f32[192,512]{1,0:T(8,128)S(1)} %get-tuple-element.52.key_part, ...), custom_call_target="tpu_custom_call" | custom-call | tf_op jit(solution)/shard_map/pallas_call | solution.py:51
  26.8 1.6 %collective-permute-start.11 = (bf16[136,256]{1,0:T(8,128)(2,1)S(1)}, bf16[136,256]{1,0:T(8,128)(2,1)S(1)}, u32[]{:S(2)}, u32[]{:S(2)}) collective-permute-start(bf16[136,256]{1,0:T(8,128)(2,1)S(1)} %get-tuple-element.55), channel_id=1, source_target_pairs={{0,1},{1,0},{2,3},{3,2},{4,5},{5,4},{6,7},{7,6},{8,9},{9,8},{10,11... | collective-permute-start | bytes 208904 | tf_op jit(solution)/shard_map/ppermute | solution.py:36
  28.3 1.7 %collective-permute-start.12 = (bf16[136,256]{1,0:T(8,128)(2,1)S(1)}, bf16[136,256]{1,0:T(8,128)(2,1)S(1)}, u32[]{:S(2)}, u32[]{:S(2)}) collective-permute-start(bf16[136,256]{1,0:T(8,128)(2,1)S(1)} %get-tuple-element.56), channel_id=1, source_target_pairs={{0,2},{1,3},{2,0},{3,1},{4,6},{5,7},{6,4},{7,5},{8,10},{9,11},{10,... | collective-permute-start | bytes 208904 | tf_op jit(solution)/shard_map/ppermute | solution.py:36
  30.1 0.3 collective-permute-start.13
  30.3 0.8 %collective-permute-done.11.refs_0_ = bf16[136,256]{1,0:T(8,128)(2,1)S(1)} collective-permute-done((bf16[136,256]{1,0:T(8,128)(2,1)S(1)}, bf16[136,256]{1,0:T(8,128)(2,1)S(1)}, u32[]{:S(2)}, u32[]{:S(2)}) %collective-permute-start.11) | collective-permute-done | bytes 69664 | tf_op jit(solution)/shard_map/ppermute | solution.py:36
  31.2 1.5 %collective-permute-done.12.refs_1_ = bf16[136,256]{1,0:T(8,128)(2,1)S(1)} collective-permute-done((bf16[136,256]{1,0:T(8,128)(2,1)S(1)}, bf16[136,256]{1,0:T(8,128)(2,1)S(1)}, u32[]{:S(2)}, u32[]{:S(2)}) %collective-permute-start.12) | collective-permute-done | bytes 69664 | tf_op jit(solution)/shard_map/ppermute | solution.py:36
  32.7 2.6 %collective-permute-done.13.refs_2_ = bf16[136,256]{1,0:T(8,128)(2,1)S(1)} collective-permute-done((bf16[136,256]{1,0:T(8,128)(2,1)S(1)}, bf16[136,256]{1,0:T(8,128)(2,1)S(1)}, u32[]{:S(2)}, u32[]{:S(2)}) %collective-permute-start.13) | collective-permute-done | bytes 69664 | tf_op jit(solution)/shard_map/ppermute | solution.py:36
  35.3 1.7 %collective-permute-start.14 = (bf16[136,256]{1,0:T(8,128)(2,1)S(1)}, bf16[136,256]{1,0:T(8,128)(2,1)S(1)}, u32[]{:S(2)}, u32[]{:S(2)}) collective-permute-start(bf16[136,256]{1,0:T(8,128)(2,1)S(1)} %get-tuple-element.59), channel_id=1, source_target_pairs={{0,8},{4,12},{8,0},{12,4},{16,24},{20,28},{24,16},{28,20},{1,9},{5... | collective-permute-start | bytes 208904 | tf_op jit(solution)/shard_map/ppermute | solution.py:41
  37.0 1.4 %collective-permute-start.15 = (bf16[136,256]{1,0:T(8,128)(2,1)S(1)}, bf16[136,256]{1,0:T(8,128)(2,1)S(1)}, u32[]{:S(2)}, u32[]{:S(2)}) collective-permute-start(bf16[136,256]{1,0:T(8,128)(2,1)S(1)} %get-tuple-element.59), channel_id=1, source_target_pairs={{0,16},{4,20},{8,24},{12,28},{16,0},{20,4},{24,8},{28,12},{1,17},{... | collective-permute-start | bytes 208904 | tf_op jit(solution)/shard_map/ppermute | solution.py:41
  38.4 1.3 %collective-permute-start.16 = (bf16[136,256]{1,0:T(8,128)(2,1)S(1)}, bf16[136,256]{1,0:T(8,128)(2,1)S(1)}, u32[]{:S(2)}, u32[]{:S(2)}) collective-permute-start(bf16[136,256]{1,0:T(8,128)(2,1)S(1)} %get-tuple-element.59), channel_id=1, source_target_pairs={{0,24},{4,28},{8,16},{12,20},{16,8},{20,12},{24,0},{28,4},{1,25},{... | collective-permute-start | bytes 208904 | tf_op jit(solution)/shard_map/ppermute | solution.py:41
  39.8 0.3 collective-permute-done.14.refs_0_
  40.1 3.1 %collective-permute-done.15.refs_1_ = bf16[136,256]{1,0:T(8,128)(2,1)S(1)} collective-permute-done((bf16[136,256]{1,0:T(8,128)(2,1)S(1)}, bf16[136,256]{1,0:T(8,128)(2,1)S(1)}, u32[]{:S(2)}, u32[]{:S(2)}) %collective-permute-start.15) | collective-permute-done | bytes 69664 | tf_op jit(solution)/shard_map/ppermute | solution.py:41
  43.2 1.5 %collective-permute-done.16.refs_2_ = bf16[136,256]{1,0:T(8,128)(2,1)S(1)} collective-permute-done((bf16[136,256]{1,0:T(8,128)(2,1)S(1)}, bf16[136,256]{1,0:T(8,128)(2,1)S(1)}, u32[]{:S(2)}, u32[]{:S(2)}) %collective-permute-start.16) | collective-permute-done | bytes 69664 | tf_op jit(solution)/shard_map/ppermute | solution.py:41
  44.7 0.5 %collective-permute-start.17 = (bf16[128,256]{1,0:T(8,128)(2,1)S(1)}, bf16[128,256]{1,0:T(8,128)(2,1)S(1)}, u32[]{:S(2)}, u32[]{:S(2)}) collective-permute-start(bf16[128,256]{1,0:T(8,128)(2,1)S(1)} %get-tuple-element.61), channel_id=1, source_target_pairs={{0,3},{1,2},{2,1},{3,0},{4,7},{5,6},{6,5},{7,4},{8,11},{9,10},{10,... | collective-permute-start | bytes 196616 | tf_op jit(solution)/shard_map/ppermute | solution.py:36
  45.2 1.3 %collective-permute-start.18 = (bf16[128,256]{1,0:T(8,128)(2,1)S(1)}, bf16[128,256]{1,0:T(8,128)(2,1)S(1)}, u32[]{:S(2)}, u32[]{:S(2)}) collective-permute-start(bf16[128,256]{1,0:T(8,128)(2,1)S(1)} %get-tuple-element.61), channel_id=1, source_target_pairs={{0,1},{1,0},{2,3},{3,2},{4,5},{5,4},{6,7},{7,6},{8,9},{9,8},{10,11... | collective-permute-start | bytes 196616 | tf_op jit(solution)/shard_map/ppermute | solution.py:36
  46.6 1.7 %collective-permute-start.19 = (bf16[128,256]{1,0:T(8,128)(2,1)S(1)}, bf16[128,256]{1,0:T(8,128)(2,1)S(1)}, u32[]{:S(2)}, u32[]{:S(2)}) collective-permute-start(bf16[128,256]{1,0:T(8,128)(2,1)S(1)} %get-tuple-element.61), channel_id=1, source_target_pairs={{0,2},{1,3},{2,0},{3,1},{4,6},{5,7},{6,4},{7,5},{8,10},{9,11},{10,... | collective-permute-start | bytes 196616 | tf_op jit(solution)/shard_map/ppermute | solution.py:36
  48.2 0.3 shard_map.89
  48.6 0.1 shard_map.94.denom
  48.7 1.2 %collective-permute-done.17.refs_1_ = bf16[128,256]{1,0:T(8,128)(2,1)S(1)} collective-permute-done((bf16[128,256]{1,0:T(8,128)(2,1)S(1)}, bf16[128,256]{1,0:T(8,128)(2,1)S(1)}, u32[]{:S(2)}, u32[]{:S(2)}) %collective-permute-start.17) | collective-permute-done | bytes 65568 | tf_op jit(solution)/shard_map/ppermute | solution.py:36
  49.9 0.0 collective-permute-done.18.refs_2_
  49.9 0.2 shard_map.95.numer
  50.2 0.7 %collective-permute-done.19.refs_0_ = bf16[128,256]{1,0:T(8,128)(2,1)S(1)} collective-permute-done((bf16[128,256]{1,0:T(8,128)(2,1)S(1)}, bf16[128,256]{1,0:T(8,128)(2,1)S(1)}, u32[]{:S(2)}, u32[]{:S(2)}) %collective-permute-start.19) | collective-permute-done | bytes 65568 | tf_op jit(solution)/shard_map/ppermute | solution.py:36
  50.8 0.2 shard_map.96
  51.0 0.1 collective-permute-start.20
  51.1 0.2 shard_map.97.base
  51.3 1.0 %collective-permute-done.20.other = bf16[96,256]{1,0:T(8,128)(2,1)S(1)} collective-permute-done((bf16[96,256]{1,0:T(8,128)(2,1)S(1)}, bf16[96,256]{1,0:T(8,128)(2,1)S(1)}, u32[]{:S(2)}, u32[]{:S(2)}) %collective-permute-start.20) | collective-permute-done | bytes 49184 | tf_op jit(solution)/shard_map/ppermute | solution.py:31
  52.3 0.8 %output.1 = bf16[96,512]{1,0:T(8,128)(2,1)} custom-call(f32[96,512]{1,0:T(8,128)S(1)} %shard_map.97.base, bf16[96,256]{1,0:T(8,128)(2,1)S(1)} %collective-permute-done.20.other, bf16[512,512]{1,0:T(8,128)(2,1)S(1)} %get-tuple-element.63.w_out), custom_call_target="tpu_custom_call" | custom-call | tf_op jit(solution)/shard_map/output/pallas_call | solution.py:369
  (3 shorter events, 0.1 us)
Async XLA Ops:
  0.0 1.7 %collective-permute-start.3 = (bf16[128,512]{1,0:T(8,128)(2,1)}, bf16[128,512]{1,0:T(8,128)(2,1)S(1)}, u32[]{:S(2)}, u32[]{:S(2)}) collective-permute-start(bf16[128,512]{1,0:T(8,128)(2,1)} %source.1), channel_id=1, source_target_pairs={{0,4},{4,0},{8,12},{12,8},{16,20},{20,16},{24,28},{28,24},{1,5},{5... | collective-permute-start | bytes 393224 | tf_op jit(solution)/shard_map/ppermute | solution.py:31
  1.7 8.5 %collective-permute-start.4 = (bf16[256,256]{1,0:T(8,128)(2,1)S(1)}, bf16[256,256]{1,0:T(8,128)(2,1)S(1)}, u32[]{:S(2)}, u32[]{:S(2)}) collective-permute-start(bf16[256,256]{1,0:T(8,128)(2,1)S(1)} %shard_map.85.refs_0_), channel_id=1, source_target_pairs={{0,3},{1,2},{2,1},{3,0},{4,7},{5,6},{6,5},{7,4},{8,11},{9,10},{10,... | collective-permute-start | bytes 393224 | tf_op jit(solution)/shard_map/ppermute | solution.py:36
  5.6 6.9 %collective-permute-start.5 = (bf16[256,256]{1,0:T(8,128)(2,1)S(1)}, bf16[256,256]{1,0:T(8,128)(2,1)S(1)}, u32[]{:S(2)}, u32[]{:S(2)}) collective-permute-start(bf16[256,256]{1,0:T(8,128)(2,1)S(1)} %shard_map.85.refs_0_), channel_id=1, source_target_pairs={{0,1},{1,0},{2,3},{3,2},{4,5},{5,4},{6,7},{7,6},{8,9},{9,8},{10,11... | collective-permute-start | bytes 393224 | tf_op jit(solution)/shard_map/ppermute | solution.py:36
  6.1 6.8 %collective-permute-start.6 = (bf16[256,256]{1,0:T(8,128)(2,1)S(1)}, bf16[256,256]{1,0:T(8,128)(2,1)S(1)}, u32[]{:S(2)}, u32[]{:S(2)}) collective-permute-start(bf16[256,256]{1,0:T(8,128)(2,1)S(1)} %shard_map.85.refs_0_), channel_id=1, source_target_pairs={{0,2},{1,3},{2,0},{3,1},{4,6},{5,7},{6,4},{7,5},{8,10},{9,11},{10,... | collective-permute-start | bytes 393224 | tf_op jit(solution)/shard_map/ppermute | solution.py:36
  6.2 1.4 %collective-permute-start = (s32[4,768]{1,0:T(4,128)}, s32[4,768]{1,0:T(4,128)S(1)}, u32[]{:S(2)}, u32[]{:S(2)}) collective-permute-start(s32[4,768]{1,0:T(4,128)} %bitcast.3), channel_id=1, source_target_pairs={{0,4},{4,0},{8,12},{12,8},{16,20},{20,16},{24,28},{28,24},{1,5},{5... | collective-permute-start | bytes 36872 | tf_op jit(solution)/shard_map/ppermute | solution.py:31
  6.2 1.6 %collective-permute-start.1 = (s32[4,768]{1,0:T(4,128)}, s32[4,768]{1,0:T(4,128)S(1)}, u32[]{:S(2)}, u32[]{:S(2)}) collective-permute-start(s32[4,768]{1,0:T(4,128)} %bitcast.6), channel_id=1, source_target_pairs={{0,4},{4,0},{8,12},{12,8},{16,20},{20,16},{24,28},{28,24},{1,5},{5... | collective-permute-start | bytes 36872 | tf_op jit(solution)/shard_map/ppermute | solution.py:31
  13.2 5.7 %collective-permute-start.7 = (bf16[192,256]{1,0:T(8,128)(2,1)S(1)}, bf16[192,256]{1,0:T(8,128)(2,1)S(1)}, u32[]{:S(2)}, u32[]{:S(2)}) collective-permute-start(bf16[192,256]{1,0:T(8,128)(2,1)S(1)} %get-tuple-element.44), channel_id=1, source_target_pairs={{0,8},{4,12},{8,0},{12,4},{16,24},{20,28},{24,16},{28,20},{1,9},{5... | collective-permute-start | bytes 294920 | tf_op jit(solution)/shard_map/ppermute | solution.py:41
  14.8 9.9 %collective-permute-start.8 = (bf16[192,256]{1,0:T(8,128)(2,1)S(1)}, bf16[192,256]{1,0:T(8,128)(2,1)S(1)}, u32[]{:S(2)}, u32[]{:S(2)}) collective-permute-start(bf16[192,256]{1,0:T(8,128)(2,1)S(1)} %get-tuple-element.45), channel_id=1, source_target_pairs={{0,16},{4,20},{8,24},{12,28},{16,0},{20,4},{24,8},{28,12},{1,17},{... | collective-permute-start | bytes 294920 | tf_op jit(solution)/shard_map/ppermute | solution.py:41
  17.4 7.3 %collective-permute-start.9 = (bf16[192,256]{1,0:T(8,128)(2,1)S(1)}, bf16[192,256]{1,0:T(8,128)(2,1)S(1)}, u32[]{:S(2)}, u32[]{:S(2)}) collective-permute-start(bf16[192,256]{1,0:T(8,128)(2,1)S(1)} %get-tuple-element.46), channel_id=1, source_target_pairs={{0,24},{4,28},{8,16},{12,20},{16,8},{20,12},{24,0},{28,4},{1,25},{... | collective-permute-start | bytes 294920 | tf_op jit(solution)/shard_map/ppermute | solution.py:41
  17.7 1.2 %collective-permute-start.2 = (s32[8,128]{1,0:T(8,128)S(1)}, s32[8,128]{1,0:T(8,128)S(1)}, u32[]{:S(2)}, u32[]{:S(2)}) collective-permute-start(s32[8,128]{1,0:T(8,128)S(1)} %get-tuple-element.41.degree), channel_id=1, source_target_pairs={{0,4},{4,0},{8,12},{12,8},{16,20},{20,16},{24,28},{28,24},{1,5},{5... | collective-permute-start | bytes 12296 | tf_op jit(solution)/shard_map/ppermute | solution.py:31
  24.8 1.4 %collective-permute-start.10 = (bf16[192,256]{1,0:T(8,128)(2,1)S(1)}, bf16[192,256]{1,0:T(8,128)(2,1)S(1)}, u32[]{:S(2)}, u32[]{:S(2)}) collective-permute-start(bf16[192,256]{1,0:T(8,128)(2,1)S(1)} %shard_map.88.hedge), channel_id=1, source_target_pairs={{0,4},{4,0},{8,12},{12,8},{16,20},{20,16},{24,28},{28,24},{1,5},{5... | collective-permute-start | bytes 294920 | tf_op jit(solution)/shard_map/ppermute | solution.py:31
  26.8 4.4 %collective-permute-start.11 = (bf16[136,256]{1,0:T(8,128)(2,1)S(1)}, bf16[136,256]{1,0:T(8,128)(2,1)S(1)}, u32[]{:S(2)}, u32[]{:S(2)}) collective-permute-start(bf16[136,256]{1,0:T(8,128)(2,1)S(1)} %get-tuple-element.55), channel_id=1, source_target_pairs={{0,1},{1,0},{2,3},{3,2},{4,5},{5,4},{6,7},{7,6},{8,9},{9,8},{10,11... | collective-permute-start | bytes 208904 | tf_op jit(solution)/shard_map/ppermute | solution.py:36
  28.3 4.3 %collective-permute-start.12 = (bf16[136,256]{1,0:T(8,128)(2,1)S(1)}, bf16[136,256]{1,0:T(8,128)(2,1)S(1)}, u32[]{:S(2)}, u32[]{:S(2)}) collective-permute-start(bf16[136,256]{1,0:T(8,128)(2,1)S(1)} %get-tuple-element.56), channel_id=1, source_target_pairs={{0,2},{1,3},{2,0},{3,1},{4,6},{5,7},{6,4},{7,5},{8,10},{9,11},{10,... | collective-permute-start | bytes 208904 | tf_op jit(solution)/shard_map/ppermute | solution.py:36
  30.1 5.2 %collective-permute-start.13 = (bf16[136,256]{1,0:T(8,128)(2,1)S(1)}, bf16[136,256]{1,0:T(8,128)(2,1)S(1)}, u32[]{:S(2)}, u32[]{:S(2)}) collective-permute-start(bf16[136,256]{1,0:T(8,128)(2,1)S(1)} %get-tuple-element.57), channel_id=1, source_target_pairs={{0,3},{1,2},{2,1},{3,0},{4,7},{5,6},{6,5},{7,4},{8,11},{9,10},{10,... | collective-permute-start | bytes 208904 | tf_op jit(solution)/shard_map/ppermute | solution.py:36
  35.3 4.8 %collective-permute-start.14 = (bf16[136,256]{1,0:T(8,128)(2,1)S(1)}, bf16[136,256]{1,0:T(8,128)(2,1)S(1)}, u32[]{:S(2)}, u32[]{:S(2)}) collective-permute-start(bf16[136,256]{1,0:T(8,128)(2,1)S(1)} %get-tuple-element.59), channel_id=1, source_target_pairs={{0,8},{4,12},{8,0},{12,4},{16,24},{20,28},{24,16},{28,20},{1,9},{5... | collective-permute-start | bytes 208904 | tf_op jit(solution)/shard_map/ppermute | solution.py:41
  37.0 6.2 %collective-permute-start.15 = (bf16[136,256]{1,0:T(8,128)(2,1)S(1)}, bf16[136,256]{1,0:T(8,128)(2,1)S(1)}, u32[]{:S(2)}, u32[]{:S(2)}) collective-permute-start(bf16[136,256]{1,0:T(8,128)(2,1)S(1)} %get-tuple-element.59), channel_id=1, source_target_pairs={{0,16},{4,20},{8,24},{12,28},{16,0},{20,4},{24,8},{28,12},{1,17},{... | collective-permute-start | bytes 208904 | tf_op jit(solution)/shard_map/ppermute | solution.py:41
  38.4 6.2 %collective-permute-start.16 = (bf16[136,256]{1,0:T(8,128)(2,1)S(1)}, bf16[136,256]{1,0:T(8,128)(2,1)S(1)}, u32[]{:S(2)}, u32[]{:S(2)}) collective-permute-start(bf16[136,256]{1,0:T(8,128)(2,1)S(1)} %get-tuple-element.59), channel_id=1, source_target_pairs={{0,24},{4,28},{8,16},{12,20},{16,8},{20,12},{24,0},{28,4},{1,25},{... | collective-permute-start | bytes 208904 | tf_op jit(solution)/shard_map/ppermute | solution.py:41
  44.7 5.2 %collective-permute-start.17 = (bf16[128,256]{1,0:T(8,128)(2,1)S(1)}, bf16[128,256]{1,0:T(8,128)(2,1)S(1)}, u32[]{:S(2)}, u32[]{:S(2)}) collective-permute-start(bf16[128,256]{1,0:T(8,128)(2,1)S(1)} %get-tuple-element.61), channel_id=1, source_target_pairs={{0,3},{1,2},{2,1},{3,0},{4,7},{5,6},{6,5},{7,4},{8,11},{9,10},{10,... | collective-permute-start | bytes 196616 | tf_op jit(solution)/shard_map/ppermute | solution.py:36
  45.2 4.7 %collective-permute-start.18 = (bf16[128,256]{1,0:T(8,128)(2,1)S(1)}, bf16[128,256]{1,0:T(8,128)(2,1)S(1)}, u32[]{:S(2)}, u32[]{:S(2)}) collective-permute-start(bf16[128,256]{1,0:T(8,128)(2,1)S(1)} %get-tuple-element.61), channel_id=1, source_target_pairs={{0,1},{1,0},{2,3},{3,2},{4,5},{5,4},{6,7},{7,6},{8,9},{9,8},{10,11... | collective-permute-start | bytes 196616 | tf_op jit(solution)/shard_map/ppermute | solution.py:36
  46.6 4.3 %collective-permute-start.19 = (bf16[128,256]{1,0:T(8,128)(2,1)S(1)}, bf16[128,256]{1,0:T(8,128)(2,1)S(1)}, u32[]{:S(2)}, u32[]{:S(2)}) collective-permute-start(bf16[128,256]{1,0:T(8,128)(2,1)S(1)} %get-tuple-element.61), channel_id=1, source_target_pairs={{0,2},{1,3},{2,0},{3,1},{4,6},{5,7},{6,4},{7,5},{8,10},{9,11},{10,... | collective-permute-start | bytes 196616 | tf_op jit(solution)/shard_map/ppermute | solution.py:36
  51.0 1.3 %collective-permute-start.20 = (bf16[96,256]{1,0:T(8,128)(2,1)S(1)}, bf16[96,256]{1,0:T(8,128)(2,1)S(1)}, u32[]{:S(2)}, u32[]{:S(2)}) collective-permute-start(bf16[96,256]{1,0:T(8,128)(2,1)S(1)} %get-tuple-element.64), channel_id=1, source_target_pairs={{0,4},{4,0},{8,12},{12,8},{16,20},{20,16},{24,28},{28,24},{1,5},{5... | collective-permute-start | bytes 147464 | tf_op jit(solution)/shard_map/ppermute | solution.py:31
